TPU v7x, 32 devices: a whole 2x2x4 slice. The times are simulated.
32 devices in a mesh: dp: 8 (over z, y), section: 4 (over x, core).
Axes of the slice: x: 2, y: 2, z: 4, core: 2. Of those that a mesh axis runs over, the one named last changes fastest.
Arguments:
- tokens: bfloat16 [8192, 768], P(('dp', 'section')), may hold values from -6 to 6
- cotangent: bfloat16 [8192, 768], P(('dp', 'section')), may hold values from -6 to 6
- section_weight: bfloat16 [4, 768, 2304], P('section')
- norm_gain: float32 [4, 768], P('section'), may hold values from 0.1 to 1.9
- norm_bias: float32 [4, 768], P('section'), may hold values from -1.75 to 1.75
- mol_ids: int32 [32, 256], P(('dp', 'section')), may hold values from 0 to 2, never falling along the last dimension, each value on 1 to 128 neighbouring positions
- key_mask: int32 [32, 256], P(('dp', 'section')), may hold values 0 or 1
Outputs:
- final_out: bfloat16 [8192, 768], P(('dp', 'section'))
- input_grad: float32 [8192, 768], P(('dp', 'section'))
- weight_grad: float32 [4, 768, 2304], P('section', None, 'dp')
- gain_grad: float32 [4, 768], P('section', 'dp')
- bias_grad: float32 [4, 768], P('section', 'dp')
Inputs may be any that keep to these rules, and one draw needn't show every extreme that they name: `mol_ids`: in every row (one micro-batch) the molecule numbers never fall, each molecule covers 1 to 128 consecutive slots, and in every row some molecule covers exactly 128.
All inputs are finite; a program needn't handle non-finite values. No bound on the sum of `key_mask` on one device may be relied on, other than what follows from the above.
Results may differ from a plain program's by a relative error of at most 0.02.
Values may be sent and summed in bfloat16 or wider, within the bound.
A program may use at most 256 MiB of HBM per device.

v0:
```python
import jax
import jax.numpy as jnp
from jax import lax
from jax.sharding import PartitionSpec as P

HEADS = 32
HS = 24


NORM_EPS = 1e-05
NEG_FILL = -1e30


def shifted(block, axis, distance):
    devices = range(lax.axis_size(axis))
    route = [(i - distance, i) for i in devices if i - distance in devices]
    return lax.ppermute(block, axis, route)


def normalize(values, gain_row, bias_row):
    center = values - jnp.mean(values, axis=-1, keepdims=True)
    spread = jnp.mean(center * center, axis=-1, keepdims=True)
    return center * lax.rsqrt(spread + NORM_EPS) * gain_row + bias_row


def head_groups(matrix):
    row_count = matrix.shape[0]
    group_size = min(8, HEADS)
    return jnp.transpose(
        matrix.reshape(row_count, HEADS // group_size, group_size, HS), (1, 2, 0, 3)
    )


def join_heads(grouped):
    row_count = grouped.shape[2]
    return jnp.transpose(grouped, (2, 0, 1, 3)).reshape(row_count, HEADS * HS)


def allowed_pairs(mol_row, key_row):
    row_count = mol_row.shape[0]
    same_mol = mol_row[:, None] == mol_row[None, :]
    row_pos = lax.broadcasted_iota(jnp.int32, (row_count, row_count), 0)
    col_pos = lax.broadcasted_iota(jnp.int32, (row_count, row_count), 1)
    return same_mol & ((key_row[None, :] == 1) | (row_pos == col_pos))


def softmax_probs(q_group, k_group, allowed):
    scores = jnp.einsum(
        "gqd,gkd->gqk", q_group, k_group, preferred_element_type=jnp.float32
    ) * HS ** (-0.5)
    scores = jnp.where(allowed[None], scores, NEG_FILL)
    top_score = jnp.max(scores, axis=-1, keepdims=True)
    weights_exp = jnp.exp(scores - top_score)
    return weights_exp / jnp.sum(weights_exp, axis=-1, keepdims=True)


def attention_values(normed, weight_local):
    model_width = weight_local.shape[0]
    qkv_all = jnp.dot(normed, weight_local, preferred_element_type=jnp.float32).astype(jnp.bfloat16)
    return (
        head_groups(qkv_all[:, :model_width]),
        head_groups(qkv_all[:, model_width : 2 * model_width]),
        head_groups(qkv_all[:, 2 * model_width :]),
    )


def attention_forward(in_pair, weight_local, gain_row, bias_row, allowed):
    xin = in_pair[0].astype(jnp.float32) + in_pair[1].astype(jnp.float32)
    normed = normalize(xin, gain_row, bias_row).astype(jnp.bfloat16)
    queries, keys_part, values_part = attention_values(normed, weight_local)

    def one_group(group_items):
        q_group, k_group, v_group = group_items
        soft_probs = softmax_probs(q_group, k_group, allowed)
        return jnp.einsum(
            "gqk,gkd->gqd",
            soft_probs.astype(jnp.bfloat16),
            v_group,
            preferred_element_type=jnp.float32,
        )

    context = join_heads(lax.map(one_group, (queries, keys_part, values_part)))
    return jnp.stack([xin.astype(jnp.bfloat16), context.astype(jnp.bfloat16)])


def ffn_forward(in_pair, weight_local, gain_row, bias_row, allowed):
    model_width = weight_local.shape[0]
    hidden = in_pair[0].astype(jnp.float32) + jnp.dot(
        in_pair[1], weight_local[:, :model_width], preferred_element_type=jnp.float32
    )
    normed = normalize(hidden, gain_row, bias_row).astype(jnp.bfloat16)
    pre_act = jnp.dot(
        normed, weight_local[:, model_width : 2 * model_width], preferred_element_type=jnp.float32
    )
    activated = jax.nn.gelu(pre_act).astype(jnp.bfloat16)
    branch = jnp.dot(
        activated, weight_local[:, 2 * model_width :], preferred_element_type=jnp.float32
    )
    return jnp.stack([hidden.astype(jnp.bfloat16), branch.astype(jnp.bfloat16)])


def attention_backward(in_pair, grad_pair, weight_local, gain_row, bias_row, allowed):
    xin = in_pair[0].astype(jnp.float32) + in_pair[1].astype(jnp.float32)
    normed_full, norm_back = jax.vjp(normalize, xin, gain_row, bias_row)
    normed = normed_full.astype(jnp.bfloat16)
    queries, keys_part, values_part = attention_values(normed, weight_local)
    grad_context = head_groups(grad_pair[1])
    scale_factor = HS ** (-0.5)

    def one_group(group_items):
        q_group, k_group, v_group, g_group = group_items
        soft_probs = softmax_probs(q_group, k_group, allowed)
        grad_values = jnp.einsum(
            "gqk,gqd->gkd",
            soft_probs.astype(jnp.bfloat16),
            g_group,
            preferred_element_type=jnp.float32,
        )
        grad_probs = jnp.einsum(
            "gqd,gkd->gqk", g_group, v_group, preferred_element_type=jnp.float32
        )
        grad_scores = soft_probs * (
            grad_probs - jnp.sum(soft_probs * grad_probs, axis=-1, keepdims=True)
        )
        grad_scores = grad_scores.astype(jnp.bfloat16)
        grad_queries = (
            jnp.einsum("gqk,gkd->gqd", grad_scores, k_group, preferred_element_type=jnp.float32)
            * scale_factor
        )
        grad_keys = (
            jnp.einsum("gqk,gqd->gkd", grad_scores, q_group, preferred_element_type=jnp.float32)
            * scale_factor
        )
        return (grad_queries, grad_keys, grad_values)

    grad_q, grad_k, grad_v = lax.map(one_group, (queries, keys_part, values_part, grad_context))
    grad_qkv = jnp.concatenate(
        [join_heads(grad_q), join_heads(grad_k), join_heads(grad_v)], axis=1
    ).astype(jnp.bfloat16)
    grad_weight = jnp.einsum("rk,rj->kj", normed, grad_qkv, preferred_element_type=jnp.float32)
    grad_normed = jnp.einsum(
        "rj,kj->rk", grad_qkv, weight_local, preferred_element_type=jnp.float32
    )
    grad_x, grad_gain, grad_bias = norm_back(grad_normed)
    grad_x = grad_x + grad_pair[0].astype(jnp.float32)
    return (jnp.stack([grad_x, grad_x]), grad_weight, grad_gain, grad_bias)


def ffn_backward(in_pair, grad_pair, weight_local, gain_row, bias_row, allowed):
    model_width = weight_local.shape[0]
    w_mix = weight_local[:, :model_width]
    w_in = weight_local[:, model_width : 2 * model_width]
    w_out = weight_local[:, 2 * model_width :]
    hidden = in_pair[0].astype(jnp.float32) + jnp.dot(
        in_pair[1], w_mix, preferred_element_type=jnp.float32
    )
    normed_full, norm_back = jax.vjp(normalize, hidden, gain_row, bias_row)
    normed = normed_full.astype(jnp.bfloat16)
    act_full, gelu_back = jax.vjp(
        jax.nn.gelu, jnp.dot(normed, w_in, preferred_element_type=jnp.float32)
    )
    activated = act_full.astype(jnp.bfloat16)
    grad_branch = grad_pair[1]
    grad_w_out = jnp.einsum("rk,rj->kj", activated, grad_branch, preferred_element_type=jnp.float32)
    grad_act = jnp.einsum("rj,kj->rk", grad_branch, w_out, preferred_element_type=jnp.float32)
    grad_pre = gelu_back(grad_act)[0].astype(jnp.bfloat16)
    grad_w_in = jnp.einsum("rk,rj->kj", normed, grad_pre, preferred_element_type=jnp.float32)
    grad_normed = jnp.einsum("rj,kj->rk", grad_pre, w_in, preferred_element_type=jnp.float32)
    grad_hidden, grad_gain, grad_bias = norm_back(grad_normed)
    grad_hidden = grad_hidden + grad_pair[0].astype(jnp.float32)
    grad_mixed = grad_hidden.astype(jnp.bfloat16)
    grad_w_mix = jnp.einsum("rk,rj->kj", in_pair[1], grad_mixed, preferred_element_type=jnp.float32)
    grad_context = jnp.einsum("rj,kj->rk", grad_mixed, w_mix, preferred_element_type=jnp.float32)
    grad_weight = jnp.concatenate([grad_w_mix, grad_w_in, grad_w_out], axis=1)
    return (jnp.stack([grad_hidden, grad_context]), grad_weight, grad_gain, grad_bias)


def shards(tokens, cotangent, section_weight, norm_gain, norm_bias, mol_ids, key_mask):
    row_count, model_width = tokens.shape
    sections = lax.axis_size("section")
    section_index = lax.axis_index("section")
    steps_total = sections + sections - 1
    all_tokens, all_cot, all_mols, all_keys = (
        lax.all_gather(tokens, "section", axis=0, tiled=True),
        lax.all_gather(cotangent, "section", axis=0, tiled=True),
        lax.all_gather(mol_ids, "section", axis=0, tiled=True),
        lax.all_gather(key_mask, "section", axis=0, tiled=True),
    )
    weight_local = section_weight[0]
    gain_row = norm_gain[0]
    bias_row = norm_bias[0]
    is_attention = section_index % 2 == 0
    is_first = section_index == 0
    is_last = section_index == sections - 1

    def block_of(source, micro_index):
        return lax.dynamic_slice_in_dim(source, micro_index * row_count, row_count, 0)

    zero_pair = jnp.zeros((2, row_count, model_width), jnp.bfloat16)
    incoming = zero_pair
    saved_pairs = jnp.zeros((sections, 2, row_count, model_width), jnp.bfloat16)
    final_buf = jnp.zeros((sections, row_count, model_width), jnp.float32)
    for step_index in range(steps_total):
        micro_index = step_index - section_index
        is_valid = (micro_index >= 0) & (micro_index < sections)
        slot_index = jnp.clip(micro_index, 0, sections - 1)
        first_pair = jnp.stack([block_of(all_tokens, slot_index), jnp.zeros_like(tokens)])
        in_pair = jnp.where(is_first, first_pair, incoming)
        allowed = allowed_pairs(all_mols[slot_index], all_keys[slot_index])
        saved_pairs = saved_pairs.at[slot_index].set(
            jnp.where(is_valid, in_pair, saved_pairs[slot_index])
        )
        out_pair = lax.cond(
            is_attention,
            attention_forward,
            ffn_forward,
            in_pair,
            weight_local,
            gain_row,
            bias_row,
            allowed,
        )
        summed = out_pair[0].astype(jnp.float32) + out_pair[1].astype(jnp.float32)
        final_buf = final_buf.at[slot_index].set(
            jnp.where(is_valid & is_last, summed, final_buf[slot_index])
        )
        if step_index + 1 < steps_total:
            incoming = shifted(out_pair, "section", 1)
    grad_in = zero_pair
    grad_buf = jnp.zeros((sections, row_count, model_width), jnp.float32)
    reduced = None
    for step_index in range(steps_total):
        micro_index = step_index - (sections - 1 - section_index)
        is_valid = (micro_index >= 0) & (micro_index < sections)
        slot_index = jnp.clip(micro_index, 0, sections - 1)
        in_pair = saved_pairs[slot_index]
        allowed = allowed_pairs(all_mols[slot_index], all_keys[slot_index])
        cot_block = block_of(all_cot, slot_index)
        grad_pair = jnp.where(is_last, jnp.stack([cot_block, cot_block]), grad_in)
        out_grads, grad_weight, grad_gain, grad_bias = lax.cond(
            is_attention,
            attention_backward,
            ffn_backward,
            in_pair,
            grad_pair,
            weight_local,
            gain_row,
            bias_row,
            allowed,
        )
        grad_weight = jnp.where(is_valid, grad_weight, 0.0)
        grad_gain = jnp.where(is_valid, grad_gain, 0.0)
        grad_bias = jnp.where(is_valid, grad_bias, 0.0)
        reduced_now = (
            lax.psum_scatter(grad_weight[None], "dp", scatter_dimension=2, tiled=True),
            lax.psum_scatter(grad_gain[None], "dp", scatter_dimension=1, tiled=True),
            lax.psum_scatter(grad_bias[None], "dp", scatter_dimension=1, tiled=True),
        )
        reduced = reduced_now if reduced is None else jax.tree.map(jnp.add, reduced, reduced_now)
        grad_buf = grad_buf.at[slot_index].set(
            jnp.where(is_valid & is_first, out_grads[0], grad_buf[slot_index])
        )
        if step_index + 1 < steps_total:
            grad_in = shifted(out_grads.astype(jnp.bfloat16), "section", -1)
    final_rows, input_rows = (
        lax.psum_scatter(
            final_buf.reshape(sections * row_count, model_width).astype(jnp.bfloat16),
            "section",
            scatter_dimension=0,
            tiled=True,
        ).astype(jnp.float32),
        lax.psum_scatter(
            grad_buf.reshape(sections * row_count, model_width).astype(jnp.bfloat16),
            "section",
            scatter_dimension=0,
            tiled=True,
        ).astype(jnp.float32),
    )
    final_low = final_rows.astype(jnp.bfloat16)
    return (final_low, input_rows, reduced[0], reduced[1], reduced[2])


def solution(mesh):
    return jax.shard_map(
        shards,
        mesh=mesh,
        in_specs=(
            P(("dp", "section"), None),
            P(("dp", "section"), None),
            P("section", None, None),
            P("section", None),
            P("section", None),
            P(("dp", "section"), None),
            P(("dp", "section"), None),
        ),
        out_specs=(
            P(("dp", "section"), None),
            P(("dp", "section"), None),
            P("section", None, "dp"),
            P("section", "dp"),
            P("section", "dp"),
        ),
        check_vma=False,
    )
```

profile of v0, /device:TPU:0, one launch (start us, length us, event | category | flops | bytes accessed | tf_op | source)
XLA Modules:
  0.0 1401.8 jit_solution(15066317496017826387)
XLA Ops:
  36.3 41.0 %conditional.14 = (bf16[2,256,768]{1,2,0:T(8,128)(2,1)}) conditional(s32[]{:T(128)} %convert_element_type.1241, (bf16[2,256,768]{2,1,0:T(8,128)(2,1)}, bf16[768,2304]{1,0:T(8,128)(2,1)S(1)}, f32[1,768]{1,0:T(1,128)S(1)}, f32[1,768]{1,0:T(1,128)S(1)}) %tuple.892, (bf16[2,256,768]{2,1,0:T(8,128)(2,1)}, f32[1,768]{1,0:T(1,128)S(1)}, ...), branch_computations={%region_1.4_spmd, %region_4.11_spmd} | conditional | flops 991104000 | bytes 16338605 | solution.py:213
  89.5 41.3 %conditional.15 = (bf16[2,256,768]{1,2,0:T(8,128)(2,1)}) conditional(s32[]{:T(128)} %convert_element_type.1241, (bf16[2,256,768]{2,1,0:T(8,128)(2,1)}, bf16[768,2304]{1,0:T(8,128)(2,1)S(1)}, f32[1,768]{1,0:T(1,128)S(1)}, f32[1,768]{1,0:T(1,128)S(1)}) %tuple.894, (bf16[2,256,768]{2,1,0:T(8,128)(2,1)}, f32[1,768]{1,0:T(1,128)S(1)}, ...), branch_computations={%region_12.15_spmd, %region_15.22_spmd} | conditional | flops 991104000 | bytes 16338605 | solution.py:213
  139.7 41.1 %conditional.16 = (bf16[2,256,768]{1,2,0:T(8,128)(2,1)}) conditional(s32[]{:T(128)} %convert_element_type.1241, (bf16[2,256,768]{2,1,0:T(8,128)(2,1)}, bf16[768,2304]{1,0:T(8,128)(2,1)S(1)}, f32[1,768]{1,0:T(1,128)S(1)}, f32[1,768]{1,0:T(1,128)S(1)}) %tuple.896, (bf16[2,256,768]{2,1,0:T(8,128)(2,1)}, f32[1,768]{1,0:T(1,128)S(1)}, ...), branch_computations={%region_23.26_spmd, %region_26.33_spmd} | conditional | flops 991104000 | bytes 16338605 | solution.py:213
  191.5 41.1 %conditional.17 = (bf16[2,256,768]{1,2,0:T(8,128)(2,1)}) conditional(s32[]{:T(128)} %convert_element_type.1241, (bf16[2,256,768]{2,1,0:T(8,128)(2,1)}, bf16[768,2304]{1,0:T(8,128)(2,1)S(1)}, f32[1,768]{1,0:T(1,128)S(1)}, f32[1,768]{1,0:T(1,128)S(1)}) %tuple.898, (bf16[2,256,768]{2,1,0:T(8,128)(2,1)}, f32[1,768]{1,0:T(1,128)S(1)}, ...), branch_computations={%region_34.37_spmd, %region_37.44_spmd} | conditional | flops 991104000 | bytes 16338605 | solution.py:213
  241.6 41.3 %conditional.18 = (bf16[2,256,768]{1,2,0:T(8,128)(2,1)}) conditional(s32[]{:T(128)} %convert_element_type.1241, (bf16[2,256,768]{2,1,0:T(8,128)(2,1)}, bf16[768,2304]{1,0:T(8,128)(2,1)S(1)}, f32[1,768]{1,0:T(1,128)S(1)}, f32[1,768]{1,0:T(1,128)S(1)}) %tuple.900, (bf16[2,256,768]{2,1,0:T(8,128)(2,1)}, f32[1,768]{1,0:T(1,128)S(1)}, ...), branch_computations={%region_45.48_spmd, %region_48.55_spmd} | conditional | flops 991104000 | bytes 16338605 | solution.py:213
  305.6 41.1 %conditional.19 = (bf16[2,256,768]{1,2,0:T(8,128)(2,1)}) conditional(s32[]{:T(128)} %convert_element_type.1241, (bf16[2,256,768]{2,1,0:T(8,128)(2,1)}, bf16[768,2304]{1,0:T(8,128)(2,1)S(1)}, f32[1,768]{1,0:T(1,128)S(1)}, f32[1,768]{1,0:T(1,128)S(1)}) %tuple.902, (bf16[2,256,768]{2,1,0:T(8,128)(2,1)}, f32[1,768]{1,0:T(1,128)S(1)}, ...), branch_computations={%region_56.59_spmd, %region_59.66_spmd} | conditional | flops 991104000 | bytes 16338605 | solution.py:213
  369.1 77.6 %conditional.21 = (bf16[2,256,768]{2,1,0:T(8,128)(2,1)S(1)}, f32[768,2304]{0,1:T(8,128)S(1)}, f32[]{:T(128)}, f32[256,768]{1,0:T(8,128)}, f32[256,768]{1,0:T(8,128)}) conditional(s32[]{:T(128)} %convert_element_type.1241, (bf16[2,256,768]{2,1,0:T(8,128)(2,1)}, bf16[768,2304]{1,0:T(8,128)(2,1)S(1)}, bf16[2,256,768]{2,1,0:T(8,128)(2,1)}, ...), branch_computations={%region_86.91_spmd, %region_91.101_spmd} | conditional | flops 2893908480 | bytes 82910520 | solution.py:240
  389.7 50.3 %while.385 = (s32[]{:T(128)}, bf16[4,8,256,24]{2,3,1,0:T(8,128)(2,1)}, bf16[4,8,256,24]{2,3,1,0:T(8,128)(2,1)}, bf16[4,8,256,24]{2,3,1,0:T(8,128)(2,1)}, pred[25...) while((s32[]{:T(128)}, ...), condition=%wide.region_98.98_spmd, body=%wide.region_94.97_spmd.sunk | while | flops 159482368 | bytes 29972728 | solution.py:136
  453.1 85.0 %conditional.22 = (bf16[2,256,768]{2,1,0:T(8,128)(2,1)S(1)}, f32[768,2304]{0,1:T(8,128)S(1)}, f32[]{:T(128)}, f32[256,768]{1,0:T(8,128)}, f32[256,768]{1,0:T(8,128)}) conditional(s32[]{:T(128)} %convert_element_type.1241, (bf16[2,256,768]{2,1,0:T(8,128)(2,1)}, bf16[768,2304]{1,0:T(8,128)(2,1)S(1)}, bf16[2,256,768]{2,1,0:T(8,128)(2,1)}, ...), branch_computations={%region_102.107_spmd, %region_107.117_spmd} | conditional | flops 2893908480 | bytes 82910520 | solution.py:240
  480.8 50.5 %while.386 = (s32[]{:T(128)}, bf16[4,8,256,24]{2,3,1,0:T(8,128)(2,1)}, bf16[4,8,256,24]{2,3,1,0:T(8,128)(2,1)}, bf16[4,8,256,24]{2,3,1,0:T(8,128)(2,1)}, pred[25...) while((s32[]{:T(128)}, ...), condition=%wide.region_114.114_spmd, body=%wide.region_110.113_spmd.sunk | while | flops 159482368 | bytes 29972728 | solution.py:136
  544.4 90.9 %conditional.23 = (bf16[2,256,768]{2,1,0:T(8,128)(2,1)}, f32[768,2304]{0,1:T(8,128)}, f32[]{:T(128)}, f32[256,768]{1,0:T(8,128)}, f32[256,768]{1,0:T(8,128)}) conditional(s32[]{:T(128)} %convert_element_type.1241, (bf16[2,256,768]{2,1,0:T(8,128)(2,1)}, bf16[768,2304]{1,0:T(8,128)(2,1)S(1)}, bf16[2,256,768]{2,1,0:T(8,128)(2,1)}, ...), branch_computations={%region_118.123_spmd, %region_123.0_spmd} | conditional | flops 2893908480 | bytes 76619000 | solution.py:240
  573.5 50.2 %while.387 = (s32[]{:T(128)}, bf16[4,8,256,24]{2,3,1,0:T(8,128)(2,1)}, bf16[4,8,256,24]{2,3,1,0:T(8,128)(2,1)}, bf16[4,8,256,24]{2,3,1,0:T(8,128)(2,1)}, pred[25...) while((s32[]{:T(128)}, ...), condition=%wide.region_130.130_spmd, body=%wide.region_126.129_spmd.sunk | while | flops 159482368 | bytes 29972728 | solution.py:136
  643.4 86.0 %conditional.24 = (bf16[2,256,768]{2,1,0:T(8,128)(2,1)S(1)}, f32[768,2304]{0,1:T(8,128)S(1)}, f32[]{:T(128)}, f32[256,768]{1,0:T(8,128)}, f32[256,768]{1,0:T(8,128)}) conditional(s32[]{:T(128)} %convert_element_type.1241, (bf16[2,256,768]{2,1,0:T(8,128)(2,1)}, bf16[768,2304]{1,0:T(8,128)(2,1)S(1)}, bf16[2,256,768]{2,1,0:T(8,128)(2,1)}, ...), branch_computations={%region_134.139_spmd, %region_139.0_spmd} | conditional | flops 2893908480 | bytes 82910520 | solution.py:240
  672.4 50.2 %while.388 = (s32[]{:T(128)}, bf16[4,8,256,24]{2,3,1,0:T(8,128)(2,1)}, bf16[4,8,256,24]{2,3,1,0:T(8,128)(2,1)}, bf16[4,8,256,24]{2,3,1,0:T(8,128)(2,1)}, pred[25...) while((s32[]{:T(128)}, ...), condition=%wide.region_146.146_spmd, body=%wide.region_142.145_spmd.sunk | while | flops 159482368 | bytes 29972728 | solution.py:136
  739.2 79.0 %conditional.25 = (bf16[2,256,768]{2,1,0:T(8,128)(2,1)S(1)}, f32[768,2304]{0,1:T(8,128)S(1)}, f32[]{:T(128)}, f32[256,768]{1,0:T(8,128)}, f32[256,768]{1,0:T(8,128)}) conditional(s32[]{:T(128)} %convert_element_type.1241, (bf16[2,256,768]{2,1,0:T(8,128)(2,1)}, bf16[768,2304]{1,0:T(8,128)(2,1)S(1)}, bf16[2,256,768]{2,1,0:T(8,128)(2,1)}, ...), branch_computations={%region_150.155_spmd, %region_155.0_spmd} | conditional | flops 2893908480 | bytes 82910520 | solution.py:240
  761.2 50.2 %while.389 = (s32[]{:T(128)}, bf16[4,8,256,24]{2,3,1,0:T(8,128)(2,1)}, bf16[4,8,256,24]{2,3,1,0:T(8,128)(2,1)}, bf16[4,8,256,24]{2,3,1,0:T(8,128)(2,1)}, pred[25...) while((s32[]{:T(128)}, ...), condition=%wide.region_162.162_spmd, body=%wide.region_158.161_spmd.sunk | while | flops 159482368 | bytes 29972728 | solution.py:136
  831.1 85.5 %conditional.26 = (bf16[2,256,768]{2,1,0:T(8,128)(2,1)S(1)}, f32[768,2304]{0,1:T(8,128)S(1)}, f32[]{:T(128)}, f32[256,768]{1,0:T(8,128)}, f32[256,768]{1,0:T(8,128)S(1)}) conditional(s32[]{:T(128)} %convert_element_type.1241, (bf16[2,256,768]{2,1,0:T(8,128)(2,1)}, bf16[768,2304]{1,0:T(8,128)(2,1)S(1)}, bf16[2,256,768]{2,1,0:T(8,128)(2,1)}, ...), branch_computations={%region_166.171_spmd, %region_171.0_spmd} | conditional | flops 2893908480 | bytes 86056272 | solution.py:240
  859.3 50.5 %while.390 = (s32[]{:T(128)}, bf16[4,8,256,24]{2,3,1,0:T(8,128)(2,1)}, bf16[4,8,256,24]{2,3,1,0:T(8,128)(2,1)}, bf16[4,8,256,24]{2,3,1,0:T(8,128)(2,1)}, pred[25...) while((s32[]{:T(128)}, ...), condition=%wide.region_178.178_spmd, body=%wide.region_174.177_spmd.sunk | while | flops 159482368 | bytes 29972728 | solution.py:136
  931.0 81.1 %conditional.27 = (f32[768,2304]{0,1:T(8,128)}, bf16[256,768]{1,0:T(8,128)(2,1)S(1)}, f32[]{:T(128)}, f32[256,768]{1,0:T(8,128)}, f32[256,768]{1,0:T(8,128)S(1)}) conditional(s32[]{:T(128)} %convert_element_type.1241, (bf16[2,256,768]{2,1,0:T(8,128)(2,1)}, bf16[768,2304]{1,0:T(8,128)(2,1)S(1)}, bf16[2,256,768]{2,1,0:T(8,128)(2,1)}, ...), branch_computations={%region_182.187_spmd, %region_187.0_spmd} | conditional | flops 2893515264 | bytes 84876640 | solution.py:240
  952.2 50.3 %while.391 = (s32[]{:T(128)}, bf16[4,8,256,24]{2,3,1,0:T(8,128)(2,1)}, bf16[4,8,256,24]{2,3,1,0:T(8,128)(2,1)}, bf16[4,8,256,24]{2,3,1,0:T(8,128)(2,1)}, pred[25...) while((s32[]{:T(128)}, ...), condition=%wide.region_194.194_spmd, body=%wide.region_190.193_spmd.sunk | while | flops 159482368 | bytes 29972728 | solution.py:136
  1065.4 71.3 %reduce-scatter.18.cloned.1.call-done = f32[96,1]{1,0:T(8,128)} async-done(((f32[768,1]{1,0:T(8,128)}), f32[96,1]{1,0:T(8,128)}) %reduce-scatter.18.cloned.1.call-update) | async-done | bytes 400
  1138.1 62.2 %reduce-scatter.16.cloned.1.call-done = f32[96,1]{1,0:T(8,128)} async-done(((f32[768,1]{1,0:T(8,128)}), f32[96,1]{1,0:T(8,128)}) %reduce-scatter.16.cloned.1.call-update) | async-done | bytes 400
  1231.8 29.4 %reduce-scatter.10.cloned.1.call-done = bf16[256,768]{1,0:T(8,128)(2,1)} async-done(((bf16[1024,768]{1,0:T(8,128)(2,1)}), bf16[256,768]{1,0:T(8,128)(2,1)}) %reduce-scatter.10.cloned.1.call-update) | async-done | bytes 393232 | tf_op jit(solution)/shard_map/reduce_scatter | solution.py:266
  1261.2 133.3 %reduce-scatter.14.cloned.1.call-done = f32[1,768,288]{1,2,0:T(8,128)} async-done(((f32[1,768,2304]{1,2,0:T(8,128)}), f32[1,768,288]{1,2,0:T(8,128)}) %reduce-scatter.14.cloned.1.call-update) | async-done | bytes 884752 | tf_op jit(solution)/shard_map/reduce_scatter | solution.py:255
  (1242 shorter events, 1210.0 us)
Async XLA Ops:
  7.2 24.8 %all-gather.5.cloned.1.call-start = ((), (), s32[]{:S(2)}) async-start(), calls=%async_computation.5 | async-start | bytes 1966080 | tf_op jit(solution)/shard_map/all_gather | solution.py:184
  7.9 352.6 %all-gather.7.cloned.1.call-start = ((), (), s32[]{:S(2)}) async-start(), calls=%async_computation.7 | async-start | bytes 1966080 | tf_op jit(solution)/shard_map/all_gather | solution.py:185
  14.2 354.9 %copy-start.144 = (s32[4,1,256]{2,0,1:T(4,128)}, s32[4,1,256]{2,0,1:T(4,128)S(1)}, u32[]{:S(2)}) copy-start(s32[4,1,256]{2,0,1:T(4,128)S(1)} %copy.412) | copy-start | bytes 12292
  21.0 15.2 %copy-start = (bf16[1,768,2304]{2,1,0:T(8,128)(2,1)S(1)}, bf16[1,768,2304]{2,1,0:T(8,128)(2,1)}, u32[]{:S(2)}) copy-start(bf16[1,768,2304]{2,1,0:T(8,128)(2,1)} %param.107) | copy-start | bytes 10616836
  21.0 15.2 %copy-start.74 = (f32[1,768]{1,0:T(1,128)S(1)}, f32[1,768]{1,0:T(1,128)}, u32[]{:S(2)}) copy-start(f32[1,768]{1,0:T(1,128)} %param.108) | copy-start | bytes 9220
  21.0 15.2 %copy-start.75 = (f32[1,768]{1,0:T(1,128)S(1)}, f32[1,768]{1,0:T(1,128)}, u32[]{:S(2)}) copy-start(f32[1,768]{1,0:T(1,128)} %param.109) | copy-start | bytes 9220
  36.2 332.9 %copy-start.139 = (s32[1,256]{1,0:T(1,128)}, s32[1,256]{1,0:T(1,128)S(1)}, u32[]{:S(2)}) copy-start(s32[1,256]{1,0:T(1,128)S(1)} %broadcast.1924) | copy-start | bytes 3076
  79.6 6.2 collective-permute-start
  133.1 3.5 collective-permute-start.1
  183.1 5.2 collective-permute-start.2
  234.9 3.5 collective-permute-start.3
  237.1 899.5 %reduce-scatter.18.cloned.1.call-start = ((), (), s32[]{:S(2)}) async-start(), calls=%async_computation.11 | async-start | bytes 442368
  285.2 17.2 %collective-permute-start.4 = (bf16[2,256,768]{2,1,0:T(8,128)(2,1)}, bf16[2,256,768]{2,1,0:T(8,128)(2,1)}, u32[]{:S(2)}, u32[]{:S(2)}) collective-permute-start(bf16[2,256,768]{2,1,0:T(8,128)(2,1)} %copy.356), channel_id=1, source_target_pairs={{0,1},{1,2},{2,3},{4,5},{5,6},{6,7},{8,9},{9,10},{10,11},{12,13},{... | collective-permute-start | bytes 2359304 | tf_op jit(solution)/shard_map/ppermute | solution.py:17
  349.1 15.8 %collective-permute-start.5 = (bf16[2,256,768]{2,1,0:T(8,128)(2,1)}, bf16[2,256,768]{2,1,0:T(8,128)(2,1)}, u32[]{:S(2)}, u32[]{:S(2)}) collective-permute-start(bf16[2,256,768]{2,1,0:T(8,128)(2,1)} %copy.360), channel_id=1, source_target_pairs={{0,1},{1,2},{2,3},{4,5},{5,6},{6,7},{8,9},{9,10},{10,11},{12,13},{... | collective-permute-start | bytes 2359304 | tf_op jit(solution)/shard_map/ppermute | solution.py:17
  446.8 4.2 collective-permute-start.6
  538.1 4.2 collective-permute-start.7
  635.3 5.7 collective-permute-start.8
  729.4 8.4 collective-permute-start.9
  818.2 11.9 collective-permute-start.10
  916.6 13.3 collective-permute-start.11
  1015.7 184.5 %reduce-scatter.16.cloned.1.call-start = ((), (), s32[]{:S(2)}) async-start(), calls=%async_computation.10 | async-start | bytes 442368
  1017.5 212.3 %reduce-scatter.12.cloned.1.call-start = ((), (), s32[]{:S(2)}) async-start(), calls=%async_computation.8 | async-start | bytes 1966080 | tf_op jit(solution)/shard_map/reduce_scatter | solution.py:272
  1020.1 241.1 %reduce-scatter.10.cloned.1.call-start = ((), (), s32[]{:S(2)}) async-start(), calls=%async_computation.6 | async-start | bytes 1966080 | tf_op jit(solution)/shard_map/reduce_scatter | solution.py:266
  1051.5 343.0 %reduce-scatter.14.cloned.1.call-start = ((), (), s32[]{:S(2)}) async-start(), calls=%async_computation.9 | async-start | bytes 7962624 | tf_op jit(solution)/shard_map/reduce_scatter | solution.py:255
  (286 other events, 766.7 us)
Sparse Core Ops, SparseCore 0:
  9.6 22.3 all-gather.4
  237.3 46.8 all-gather.6
  1015.9 120.7 reduce-scatter.17
  1139.8 60.3 reduce-scatter.15
  1202.6 27.1 reduce-scatter.11
  1233.0 28.1 reduce-scatter.9
  1265.4 129.0 reduce-scatter.13
where the time goes:
time: 1420 us; the launch traced here: 1400 us
  matrix products  502 us (35%)
  waiting for transfers between devices  342 us (24%)
  other arithmetic  234 us (16%)
  local copies, waits for them, and re-layouts  220 us (15%)
  starting transfers between devices  43.5 us (3%)
  loops' own time  32.5 us (2%)
  between operations  15.4 us (1%)
    sub x56, matrix products, softmax_probs(): weights_exp = jnp.exp(scores - top_score)  150 us
    unnamed x9, waiting for transfers between devices  134 us
    reduce_scatter x1, waiting for transfers between devices, shards(): lax.psum_scatter(grad_weight[None], 'dp', scatter_dimension=2, tiled=True)  133 us
    dot_general x28, matrix products, one_group(): jnp.einsum('gqk,gqd->gkd', soft_probs.astype(jnp.bfloat16), g_group, pref...  76.3 us
    dot_general x28, matrix products, one_group(): jnp.einsum('gqk,gkd->gqd', soft_probs.astype(jnp.bfloat16), v_group, pref...  70.6 us
    dot_general x28, matrix products, one_group(): jnp.einsum('gqd,gkd->gqk', g_group, v_group, preferred_element_type=jnp.f...  65.2 us
    ppermute x12, starting transfers between devices, shifted(): return lax.ppermute(block, axis, route)  43.2 us
    slice x28, local copies, waits for them, and re-layouts, attention_values(): qkv_all[:, 2 * model_width:]  39 us
  transfers between devices with their start and end apart: 19, of which 9 were waited for; matrix products, arithmetic and copies ran while one was open for 14% of the time, Pallas kernels for 0%

commit v1 on v0

v1 whole, which is shorter than its diff:
```python
import math
import jax
import jax.numpy as jnp
import numpy as np
from jax import lax
from jax.experimental import pallas as pl
from jax.experimental.pallas import tpu as pltpu
from jax.sharding import PartitionSpec as P

HEADS=32; HS=24; EPS=1e-5; NEG=-1e30
BF = jnp.bfloat16
F32 = jnp.float32
I32 = jnp.int32
MESH = pl.DeviceIdType.MESH

GELU_A=0.7978845608028654; GELU_B=0.044715

def dotf(a,b): return jnp.dot(a,b,preferred_element_type=F32)
def dot_t(a,b): return lax.dot_general(a,b,(((1,),(1,)),((),())),preferred_element_type=F32)

def head_masks():
    m=np.zeros((16,256),np.float32)
    for h in range(16):
        lo=24*h-(0 if h<10 else 128)
        m[h,lo:lo+24]=1
    return m

def ln_fwd(x, g, b):
    c=x-jnp.mean(x,axis=-1,keepdims=True)
    v=jnp.mean(c*c,axis=-1,keepdims=True)
    r=lax.rsqrt(v+EPS)
    xh=c*r
    return xh, r, (xh*g+b).astype(BF)

def ln_bwd(gn, xh, r, g):
    gg=gn*g
    m1=jnp.mean(gg,axis=-1,keepdims=True)
    m2=jnp.mean(gg*xh,axis=-1,keepdims=True)
    return r*(gg-m1-xh*m2)


RC=256
HW=[0]*10+[1]*6
def rows_of(i, n):
    return pl.ds(pl.multiple_of(i * n, n), n)

def layer_fwd(xb, wa, wf, lnp, mb, hm, S, ctxT, vec):
    R,D=xb.shape
    NB=R//128
    xh,r,n=ln_fwd(xb[...].astype(F32), lnp[0:1,:], lnp[1:2,:])
    S["xha"][...]=xh; S["ra"][...]=r; S["an"][...]=n
    S["qkv"][...]=dotf(S["an"][...], wa[...]).astype(BF)
    @pl.loop(0,3)
    def _(i):
        cs=rows_of(i,D)
        S["qkvT"][cs,:]=S["qkv"][:,cs].T
    c=(HS**-0.5)*1.4426950408889634
    @pl.loop(0,NB*2)
    def _(it):
        b=it//2; g=it-2*b
        rows=rows_of(b,128)
        base=g*384
        mbias=mb[rows,:]
        qw=[S["qkv"][rows,pl.ds(pl.multiple_of(base+128*w,128),256)] for w in (0,1)]
        kw=[S["qkv"][rows,pl.ds(pl.multiple_of(D+base+128*w,128),256)] for w in (0,1)]
        for h in range(16):
            s=dot_t(kw[HW[h]]*hm[h:h+1,:], qw[HW[h]])*c+mbias
            m=jnp.max(s,axis=0,keepdims=True)
            ex=jnp.exp2(s-m)
            l=jnp.sum(ex,axis=0,keepdims=True)
            S["pT"][it*16+h]=(ex*(1.0/l)).astype(BF)
    @pl.loop(0,NB*2)
    def _(it):
        b=it//2; g=it-2*b
        rows=rows_of(b,128)
        base=g*384
        for j in range(8):
            vt=S["qkvT"][pl.ds(pl.multiple_of(2*D+base+48*j,16),48),rows]
            o=dotf(vt, jnp.concatenate([S["pT"][it*16+2*j],S["pT"][it*16+2*j+1]],axis=1))
            ctxT[pl.ds(pl.multiple_of(base+48*j,8),24),rows]=o[0:24,0:128]
            ctxT[pl.ds(pl.multiple_of(base+48*j+24,8),24),rows]=o[24:48,128:256]
    S["ctx"][...]=ctxT[...].astype(BF).T
    vec[...]=xb[...].astype(F32)+dotf(S["ctx"][...], wf[:,0:D])
    xh,r,n=ln_fwd(vec[...], lnp[2:3,:], lnp[3:4,:])
    S["xhf"][...]=xh; S["rf"][...]=r; S["fn"][...]=n
    u=dotf(S["fn"][...], wf[:,D:2*D])
    u2=u*u
    t=jnp.tanh(GELU_A*(u+GELU_B*u*u2))
    S["act"][...]=(0.5*u*(1.0+t)).astype(BF)
    S["gp"][...]=0.5*(1.0+t)+0.5*u*(1.0-t*t)*(GELU_A+3*GELU_A*GELU_B*u2)
    br=dotf(S["act"][...], wf[:,2*D:3*D]).astype(BF).astype(F32)
    return (vec[...].astype(BF).astype(F32)+br).astype(BF)

def layer_bwd(G, wa, wf, lnp, hm, S, gwa, gwf, glnp, gxT, gb, gbT, gctx, gctxT, gqT, gqb, gsT, vec, u):
    R,D=G.shape
    NB=R//128
    def put(ref,rows,val):
        ref[rows,:]=jnp.where(u>0,ref[rows,:],0.0)+val
    gbT[...]=G[...].T
    put(gwf,pl.ds(2*D,D),dotf(gbT[...],S["act"][...]))
    gb[...]=(dot_t(G[...], wf[:,2*D:3*D])*S["gp"][...]).astype(BF)
    gbT[...]=gb[...].T
    put(gwf,pl.ds(D,D),dotf(gbT[...],S["fn"][...]))
    vec[...]=dot_t(gb[...], wf[:,D:2*D])
    def lnb(gref, xh, r, grow, gi, resid, outref):
        gn=gref[...]; x=xh[...]
        gv=ln_bwd(gn,x,r[...],grow)
        outref[...]=(gv+resid[...].astype(F32)).astype(BF)
        put(glnp,slice(gi,gi+1),jnp.sum(gn*x,axis=0,keepdims=True)); put(glnp,slice(gi+1,gi+2),jnp.sum(gn,axis=0,keepdims=True))
    lnb(vec,S["xhf"],S["rf"],lnp[2:3,:],2,G,gb)
    gbT[...]=gb[...].T
    put(gwf,pl.ds(0,D),dotf(gbT[...],S["ctx"][...]))
    gctx[...]=dot_t(gb[...], wf[:,0:D]).astype(BF)
    gctxT[...]=gctx[...].T
    sc=HS**-0.5
    @pl.loop(0,NB*2)
    def _(it):
        b=it//2; g=it-2*b
        rows=rows_of(b,128)
        base=g*384
        vw=[S["qkv"][rows,pl.ds(pl.multiple_of(2*D+base+128*w,128),256)] for w in (0,1)]
        gw=[gctx[rows,pl.ds(pl.multiple_of(base+128*w,128),256)] for w in (0,1)]
        for h in range(16):
            gp=dot_t(vw[HW[h]]*hm[h:h+1,:], gw[HW[h]])
            pf=S["pT"][it*16+h].astype(F32)
            d=jnp.sum(pf*gp,axis=0,keepdims=True)
            gsT[it*16+h]=(pf*(gp-d)).astype(BF)
    def prod(k,fn):
        @pl.loop(0,NB*2)
        def _(it):
            b=it//2; g=it-2*b
            rows=rows_of(b,128)
            base=g*384
            for j in range(8):
                v=fn(it,rows,base,j)
                gqT[pl.ds(pl.multiple_of(k*D+base+48*j,8),24),rows]=v[0:24,0:128]
                gqT[pl.ds(pl.multiple_of(k*D+base+48*j+24,8),24),rows]=v[24:48,128:256]
    def pr(ref,it,j,ax): return jnp.concatenate([ref[it*16+2*j],ref[it*16+2*j+1]],axis=ax)
    prod(2,lambda it,rows,base,j: dot_t(gctxT[pl.ds(pl.multiple_of(base+48*j,16),48),rows], pr(S["pT"],it,j,0)))
    prod(1,lambda it,rows,base,j: dot_t(S["qkvT"][pl.ds(pl.multiple_of(base+48*j,16),48),rows], pr(gsT,it,j,0))*sc)
    prod(0,lambda it,rows,base,j: dotf(S["qkvT"][pl.ds(pl.multiple_of(D+base+48*j,16),48),rows], pr(gsT,it,j,1))*sc)
    gqb[...]=gqT[...].astype(BF)
    put(gwa,pl.ds(0,3*D),dotf(gqb[...],S["an"][...]))
    vec[...]=dotf(wa[...],gqb[...]).T
    lnb(vec,S["xha"],S["ra"],lnp[0:1,:],0,gb,gxT)


def remote(src, dst, ss, rs, dev):
    return pltpu.make_async_remote_copy(
        src_ref=src, dst_ref=dst, send_sem=ss, recv_sem=rs, device_id=dev, device_id_type=MESH
    )


UNIT = ("xha", "ra", "an", "qkv", "qkvT", "pT", "ctx", "xhf", "rf", "fn", "act", "gp")


def unit_shapes(R, D):
    return (
        ((R, D), F32), ((R, 1), F32), ((R, D), BF), ((R, 3 * D), BF), ((3 * D, R), BF),
        ((R // 128 * HEADS, 128, 128), BF), ((R, D), BF), ((R, D), F32), ((R, 1), F32),
        ((R, D), BF), ((R, D), BF), ((R, D), F32),
    )


def rotation(meta, R):
    mol = meta[0:1, :]
    c0 = jnp.sum((mol == 0).astype(I32), axis=1, keepdims=True)
    c1 = jnp.sum((mol == 1).astype(I32), axis=1, keepdims=True)
    start = jnp.where(c0 == 128, 0, jnp.where(c1 == 128, c0, c0 + c1))
    i0 = lax.broadcasted_iota(I32, (R, R), 0)
    i1 = lax.broadcasted_iota(I32, (R, R), 1)

    def onehot(a, b):
        t = a + start
        t = jnp.where(t >= R, t - R, t)
        return jnp.where(t == b, 1.0, 0.0).astype(BF)

    return onehot(i0, i1), onehot(i1, i0)


def pair_bias(meta, rot, out, R):
    mk = meta[...].astype(F32).astype(BF)
    row = dot_t(mk, rot)
    col = dot_t(rot, mk)
    k0 = lax.broadcasted_iota(I32, (128, 128), 0)
    q0 = lax.broadcasted_iota(I32, (128, 128), 1)
    for b in range(R // 128):
        rs = slice(b * 128, b * 128 + 128)
        same = col[rs, 0:1] == row[0:1, rs]
        ok = same & ((col[rs, 1:2] > 0.5) | (k0 == q0))
        out[rs, :] = jnp.where(ok, 0.0, NEG)


def relay_kernel(
    tok, cot, w, ln, meta, hm,
    fo, ig, gsum, glsum,
    *scr,
):
    R, D = tok.shape
    n = len(UNIT)
    U = {k: r for k, r in zip(UNIT, scr[:n])}
    (
        wa, wf, lna, lnf, metas, rots, rinv, mb, X, G, ys, fob, igb,
        gwa, gwf, glp, ctxT, vec, gb, gbT, gctx, gctxT, gqT, gqb, gsT, gx, sb, rb, glr,
        wl_s, w_s, w_r, l_s, l_r, m_s, m_r, ex_s, ex_r, y_s, y_r, fo_s, fo_r, g_s, g_r, ig_s, ig_r, p_s, p_r,
    ) = scr[n:]
    s = lax.axis_index("section")
    e = lax.rem(s, 2)
    L = s // 2
    mate = {"section": s + 1 - 2 * e}
    other = {"section": s + 2 - 4 * L}
    bar = pltpu.get_barrier_semaphore()
    pl.semaphore_signal(bar, inc=1, device_id=mate, device_id_type=MESH)
    pl.semaphore_signal(bar, inc=1, device_id=other, device_id_type=MESH)
    pl.semaphore_wait(bar, 2)

    def both(fn):
        @pl.when(e == 0)
        def _():
            fn(wa, lna, glp, gwa, gwf)

        @pl.when(e == 1)
        def _():
            fn(wf, lnf, glp, gwf, gwa)

    def send_w(wd, ld, *_):
        pltpu.make_async_copy(w, wd, wl_s.at[0]).start()
        pltpu.make_async_copy(ln, ld, wl_s.at[1]).start()
        remote(w, wd, w_s, w_r, mate).start()
        remote(ln, ld, l_s, l_r, mate).start()

    both(send_w)
    m_copy = remote(meta, metas, m_s, m_r, other)
    m_copy.start()
    rot, inv = rotation(meta, R)
    rots[...] = rot
    rinv[...] = inv
    xr = dotf(rot, tok[...]).astype(BF)
    cr = dotf(rot, cot[...]).astype(BF)

    @pl.when(L == 0)
    def _():
        X[0] = xr
        ys[0] = cr
        remote(ys.at[0], G.at[0], ex_s, ex_r, other).start()

    @pl.when(L == 1)
    def _():
        ys[0] = xr
        G[1] = cr
        remote(ys.at[0], X.at[1], ex_s, ex_r, other).start()

    m_copy.wait()
    rot2, _ = rotation(metas, R)

    @pl.when(L == 0)
    def _():
        pair_bias(meta, rots[...], mb.at[0], R)
        pair_bias(metas, rot2, mb.at[1], R)

    @pl.when(L == 1)
    def _():
        pair_bias(metas, rot2, mb.at[0], R)
        pair_bias(meta, rots[...], mb.at[1], R)

    def wait_w(wd, ld, *_):
        pltpu.make_async_copy(w, wd, wl_s.at[0]).wait()
        pltpu.make_async_copy(ln, ld, wl_s.at[1]).wait()
        remote(w, wd, w_s, w_r, mate).wait()
        remote(ln, ld, l_s, l_r, mate).wait()

    both(wait_w)
    lnp = LnRows(lna, lnf)

    def unit(u):
        return {k: r.at[u] for k, r in U.items()}

    @pl.loop(0, 2)
    def _(u):
        @pl.when(L == 1)
        def _():
            remote(ys.at[1], X.at[u], y_s.at[u], y_r.at[u], other).wait_recv()

        @pl.when((L == 0) & (u == 1))
        def _():
            remote(ys.at[0], X.at[1], ex_s, ex_r, other).wait_recv()

        y = layer_fwd(X.at[u], wa, wf, lnp, mb.at[u], hm, unit(u), ctxT, vec)

        @pl.when(L == 0)
        def _():
            ys[1 + u] = y
            remote(ys.at[1 + u], X.at[u], y_s.at[u], y_r.at[u], other).start()

        @pl.when((L == 1) & (u == 0))
        def _():
            ys[1] = y
            remote(ys.at[1], fob, fo_s, fo_r, other).start()

        @pl.when((L == 1) & (u == 1))
        def _():
            fob[...] = y

    @pl.loop(0, 2)
    def _(u):
        @pl.when((L == 1) & (u == 0))
        def _():
            remote(ys.at[0], G.at[0], ex_s, ex_r, other).wait_recv()

        @pl.when(L == 0)
        def _():
            remote(gx.at[u], G.at[u], g_s.at[u], g_r.at[u], other).wait_recv()

        layer_bwd(
            G.at[u], wa, wf, lnp, hm, unit(u), gwa, gwf, glp, gx.at[u],
            gb, gbT, gctx, gctxT, gqT, gqb, gsT, vec, u,
        )

        @pl.when(L == 1)
        def _():
            remote(gx.at[u], G.at[u], g_s.at[u], g_r.at[u], other).start()

        @pl.when((L == 0) & (u == 0))
        def _():
            igb[...] = gx[0]

        @pl.when((L == 0) & (u == 1))
        def _():
            remote(gx.at[1], igb, ig_s, ig_r, other).start()

    def swap(wd, ld, gl, mine, theirs):
        sb[0:3 * D, :] = theirs[...].astype(BF)

    both(swap)
    p_copy = remote(sb, rb, p_s.at[0], p_r.at[0], mate)
    p_copy.start()
    l_copy = remote(glp, glr, p_s.at[1], p_r.at[1], mate)
    l_copy.start()

    @pl.when(L == 0)
    def _():
        remote(ys.at[1], fob, fo_s, fo_r, other).wait_recv()

    @pl.when(L == 1)
    def _():
        remote(gx.at[1], igb, ig_s, ig_r, other).wait_recv()

    fo[...] = dotf(rinv[...], fob[...]).astype(BF)
    ig[...] = dotf(rinv[...], igb[...])
    p_copy.wait()
    l_copy.wait()
    glsum[...] = glp[...] + glr[...]

    def add(wd, ld, gl, mine, theirs):
        gsum[...] = (mine[...] + rb[...].astype(F32)).astype(BF)

    both(add)

    remote(ys.at[0], X.at[1], ex_s, ex_r, other).wait_send()

    @pl.when(L == 0)
    def _():
        remote(ys.at[1], X.at[0], y_s.at[0], y_r.at[0], other).wait_send()
        remote(ys.at[2], X.at[1], y_s.at[1], y_r.at[1], other).wait_send()
        remote(gx.at[1], igb, ig_s, ig_r, other).wait_send()

    @pl.when(L == 1)
    def _():
        remote(ys.at[1], fob, fo_s, fo_r, other).wait_send()
        remote(gx.at[0], G.at[0], g_s.at[0], g_r.at[0], other).wait_send()
        remote(gx.at[1], G.at[1], g_s.at[1], g_r.at[1], other).wait_send()


class LnRows:
    def __init__(self, a, f):
        self.a, self.f = a, f

    def __getitem__(self, ix):
        r = ix[0].start
        src = self.a if r < 2 else self.f
        return src[r % 2:r % 2 + 1, :]


def relay(tok, cot, w, ln, meta, hm):
    R, D = tok.shape
    V = pl.BlockSpec(memory_space=pltpu.VMEM)
    dma, vm = pltpu.SemaphoreType.DMA, pltpu.VMEM
    scratch = [vm((2,) + sh, dt) for sh, dt in unit_shapes(R, D)] + [
        vm((D, 3 * D), BF), vm((D, 3 * D), BF), vm((8, D), F32), vm((8, D), F32),
        vm((8, R), I32), vm((R, R), BF), vm((R, R), BF), vm((2, R, 128), F32),
        vm((2, R, D), BF), vm((2, R, D), BF), vm((3, R, D), BF), vm((R, D), BF), vm((R, D), BF),
        vm((3 * D, D), F32), vm((3 * D, D), F32), vm((8, D), F32),
        vm((D, R), F32), vm((R, D), F32), vm((R, D), BF), vm((D, R), BF), vm((R, D), BF), vm((D, R), BF),
        vm((3 * D, R), F32), vm((3 * D, R), BF), vm((R // 128 * HEADS, 128, 128), BF), vm((2, R, D), BF),
        vm((3 * D, D), BF), vm((3 * D, D), BF), vm((8, D), F32),
        dma((2,)), dma, dma, dma, dma, dma, dma, dma, dma, dma((2,)), dma((2,)), dma, dma,
        dma((2,)), dma((2,)), dma, dma, dma((2,)), dma((2,)),
    ]
    return pl.pallas_call(
        relay_kernel,
        out_shape=[
            jax.ShapeDtypeStruct((R, D), BF),
            jax.ShapeDtypeStruct((R, D), F32),
            jax.ShapeDtypeStruct((3 * D, D), BF),
            jax.ShapeDtypeStruct((8, D), F32),
        ],
        in_specs=[V, V, pl.BlockSpec(memory_space=pl.ANY), V, V, V],
        out_specs=[V] * 4,
        scratch_shapes=scratch,
        compiler_params=pltpu.CompilerParams(
            collective_id=0, has_side_effects=True, vmem_limit_bytes=64 << 20
        ),
        name="relay",
    )(tok, cot, w, ln, meta, hm)


def shards(tokens, cotangent, section_weight, norm_gain, norm_bias, mol_ids, key_mask):
    R, D = tokens.shape
    ln = jnp.concatenate([norm_gain, norm_bias, jnp.zeros((6, D), F32)], axis=0)
    meta = jnp.concatenate([mol_ids, key_mask, jnp.zeros((6, R), I32)], axis=0)
    hm = jnp.asarray(head_masks(), BF)
    fo, ig, gsum, glsum = relay(tokens, cotangent, section_weight[0], ln, meta, hm)
    e = lax.rem(lax.axis_index("section"), 2)
    gl = lax.dynamic_slice_in_dim(glsum, 2 * e, 2, 0)
    gw = lax.psum_scatter(gsum, "dp", scatter_dimension=0, tiled=True)
    gl = lax.psum_scatter(gl, "dp", scatter_dimension=1, tiled=True)
    return fo, ig, gw.astype(F32).T[None], gl[0:1], gl[1:2]


def solution(mesh):
    return jax.shard_map(
        shards,
        mesh=mesh,
        in_specs=(
            P(("dp", "section"), None),
            P(("dp", "section"), None),
            P("section", None, None),
            P("section", None),
            P("section", None),
            P(("dp", "section"), None),
            P(("dp", "section"), None),
        ),
        out_specs=(
            P(("dp", "section"), None),
            P(("dp", "section"), None),
            P("section", None, "dp"),
            P("section", "dp"),
            P("section", "dp"),
        ),
        check_vma=False,
    )
```

time: 1420 us -> 264 us (0.19); the launches traced: 1400 us -> 263 us
  matrix products: 502 us -> 0 us
  other arithmetic: 234 us -> 4.72 us
  local copies, waits for them, and re-layouts: 220 us -> 5.69 us
  waiting for transfers between devices: 342 us -> 144 us
  Pallas kernels: 0 us -> 94.4 us
  starting transfers between devices: 43.5 us -> 0.08 us
  loops' own time: 32.5 us -> 0 us
    dot_general x168 -> x0, matrix products: 352 us -> none  [the longest x28 76.3 us: one_group(): jnp.einsum('gqk,gqd->gkd', soft_probs.astype(jnp.bfloat16), g_group, pref...]
    sub x56 -> x0, matrix products: 150 us -> none  [softmax_probs(): weights_exp = jnp.exp(scores - top_score)]
    slice x71 -> x1, local copies, waits for them, and re-layouts: 115 us -> 0.95 us  [shards(): return (fo, ig, gw.astype(F32).T[None], gl[0:1], gl[1:2])]
    reduce_scatter x3 -> x1, waiting for transfers between devices: 191 us -> 79.7 us  [shards(): gw = lax.psum_scatter(gsum, 'dp', scatter_dimension=0, tiled=True)]
    pallas_call x0 -> x1, Pallas kernels: none -> 94.4 us  [relay(): pl.pallas_call(relay_kernel, out_shape=[jax.ShapeDtypeStruct((R, D), BF),...]
    unnamed x9 -> x3, waiting for transfers between devices: 134 us -> 64.7 us
    reduce_sum x35 -> x0, other arithmetic: 56.6 us -> none  [the longest x14 20.6 us: normalize(): center = values - jnp.mean(values, axis=-1, keepdims=True)]
    ppermute x12 -> x0, starting transfers between devices: 43.2 us -> none  [shifted(): return lax.ppermute(block, axis, route)]
  transfers between devices with their start and end apart: 19 -> 2, of which waited for: 9 -> 2; matrix products, arithmetic and copies ran while one was open for 14% -> 1% of each run, Pallas kernels for 0% -> 0%
where the time goes in v1:
time: 264 us; the launch traced here: 263 us
  waiting for transfers between devices  144 us (55%)
  Pallas kernels  94.4 us (36%)
  between operations  14.1 us (5%)
  local copies, waits for them, and re-layouts  5.69 us (2%)
  other arithmetic  4.72 us (2%)
    pallas_call x1, Pallas kernels, relay(): pl.pallas_call(relay_kernel, out_shape=[jax.ShapeDtypeStruct((R, D), BF),...  94.4 us
    reduce_scatter x1, waiting for transfers between devices, shards(): gw = lax.psum_scatter(gsum, 'dp', scatter_dimension=0, tiled=True)  79.7 us
    unnamed x3, waiting for transfers between devices  64.7 us
  transfers between devices with their start and end apart: 2, of which 2 were waited for; matrix products, arithmetic and copies ran while one was open for 1% of the time, Pallas kernels for 0%

profile of v1, /device:TPU:0, one launch (start us, length us, event | category | flops | bytes accessed | tf_op | source)
XLA Modules:
  0.0 263.4 jit_solution(7466664487532940711)
XLA Ops:
  7.2 0.0 reduce-scatter.7.cloned.1.call-start
  7.2 0.1 pad.2.clone
  7.3 0.1 pad.5.clone
  7.4 1.4 maximum_maximum_fusion.ln
  8.8 1.4 add_add_fusion.meta
  10.1 94.4 %relay.1 = (bf16[256,768]{1,0:T(8,128)(2,1)}, f32[256,768]{1,0:T(8,128)}, bf16[2304,768]{1,0:T(8,128)(2,1)}, f32[8,768]{1,0:T(8,128)}) custom-call(bf16[256,768]{1,0:T(8,128)(2,1)} %tok.1, bf16[256,768]{1,0:T(8,128)(2,1)} %cot.1, bf16[768,2304]{1,0:T(8,128)(2,1)} %bitcast.7, f32[8,768]{1,0:T(8,128)} %maximum_maximum_fusion.ln, s32[8,256]{1,0:T(8,128)} %add_add_fusion.meta, ...), custom_call_target="tpu_custom_call" | custom-call | tf_op jit(solution)/shard_map/relay/pallas_call | solution.py:399
  104.5 0.0 copy-start.1
  104.5 0.0 copy-start
  104.6 0.8 constant_dynamic-slice_fusion
  105.4 0.9 copy.13
  106.3 0.0 reduce-scatter.7.cloned.1.call-update
  106.4 0.0 reduce-scatter.5.cloned.1.call-start
  106.4 0.7 reduce-scatter.5.cloned.1.call-update
  107.1 64.0 %reduce-scatter.7.cloned.1.call-done = f32[96,2]{1,0:T(8,128)} async-done(((f32[768,2]{1,0:T(8,128)}), f32[96,2]{1,0:T(8,128)}) %reduce-scatter.7.cloned.1.call-update) | async-done | bytes 784
  171.1 0.9 fusion
  172.0 0.6 copy.15
  172.6 0.6 copy.16
  173.2 79.7 %reduce-scatter.5.cloned.1.call-done = bf16[288,768]{1,0:T(8,128)(2,1)} async-done(((bf16[2304,768]{1,0:T(8,128)(2,1)}), bf16[288,768]{1,0:T(8,128)(2,1)}) %reduce-scatter.5.cloned.1.call-update) | async-done | bytes 442384 | tf_op jit(solution)/shard_map/reduce_scatter | solution.py:425
  252.9 2.0 convert_bitcast_fusion
  254.9 0.0 copy-done.1
  254.9 0.7 copy.19
  255.7 0.0 copy-done
  255.7 0.9 copy.20
  (2 shorter events, 0.0 us)
Async XLA Ops:
  7.2 163.9 %reduce-scatter.7.cloned.1.call-start = ((), (), s32[]{:S(2)}) async-start(), calls=%async_computation.3 | async-start | bytes 442368
  104.5 150.4 %copy-start.1 = (bf16[256,768]{1,0:T(8,128)(2,1)S(1)}, bf16[256,768]{1,0:T(8,128)(2,1)}, u32[]{:S(2)}) copy-start(bf16[256,768]{1,0:T(8,128)(2,1)} %get-tuple-element.20) | copy-start | bytes 1179652
  104.5 151.1 %copy-start = (f32[256,768]{1,0:T(8,128)S(1)}, f32[256,768]{1,0:T(8,128)}, u32[]{:S(2)}) copy-start(f32[256,768]{1,0:T(8,128)} %get-tuple-element.21) | copy-start | bytes 2359300
  106.4 146.6 %reduce-scatter.5.cloned.1.call-start = ((), (), s32[]{:S(2)}) async-start(), calls=%async_computation.2 | async-start | bytes 3981312 | tf_op jit(solution)/shard_map/reduce_scatter | solution.py:425
Sparse Core Ops, SparseCore 0:
  106.5 64.5 reduce-scatter.6
  174.7 78.1 reduce-scatter.4

commit v2 on v0

v2 whole, which is shorter than its diff:
```python
import jax
import jax.numpy as jnp
from jax import lax
from jax.experimental import pallas as pl
from jax.experimental.pallas import tpu as pltpu
from jax.sharding import PartitionSpec as P

HEADS = 32
HS = 24
EPS = 1e-5
NEG = -1e30
BF = jnp.bfloat16
F32 = jnp.float32
I32 = jnp.int32
MESH = pl.DeviceIdType.MESH
GELU_A = 0.7978845608028654
GELU_B = 0.044715
LOG2E = 1.4426950408889634
T = 128


def dotf(a, b):
    return jnp.dot(a, b, preferred_element_type=F32)


def dot_t(a, b):
    return lax.dot_general(a, b, (((1,), (1,)), ((), ())), preferred_element_type=F32)


def at(i, n):
    return pl.ds(pl.multiple_of(i * n, n), n)


HEAD_WIN = (0,) * 10 + (1,) * 6


def ln_rows(x, g, b):
    c = x - jnp.mean(x, axis=-1, keepdims=True)
    r = lax.rsqrt(jnp.mean(c * c, axis=-1, keepdims=True) + EPS)
    xh = c * r
    return xh, r, (xh * g + b).astype(BF)


def windows(ref, rows, base):
    return [ref[rows, pl.ds(pl.multiple_of(base + 128 * w, 128), 256)] for w in (0, 1)]


def put_heads(ref, base, j, v):
    ref[pl.ds(pl.multiple_of(base + 48 * j, 8), 24), :] = v[0:24, 0:T]
    ref[pl.ds(pl.multiple_of(base + 48 * j + 24, 8), 24), :] = v[24:48, T:2 * T]


def two(ref, i, axis):
    return jnp.concatenate([ref[i], ref[i + 1]], axis=axis)


def forward_stages(x, y, wa, wf, lna, lnf, mb, hm, S, ctxT, vec):
    D = x.shape[1]

    def norm_a():
        S["xha"][...], S["ra"][...], S["an"][...] = ln_rows(x[...].astype(F32), lna[0][...], lna[1][...])

    def project():
        S["qkv"][...] = dotf(S["an"][...], wa[...]).astype(BF)

    def flip():
        S["qkvT"][...] = S["qkv"][...].T

    def scores():
        @pl.loop(0, 2)
        def _(g):
            base = g * 384
            bias = mb[...]
            qw = windows(S["qkv"], slice(None), base)
            kw = windows(S["qkv"], slice(None), D + base)
            for h in range(16):
                w = HEAD_WIN[h]
                s = dot_t(kw[w] * hm[h:h + 1, :], qw[w]) * (HS ** -0.5 * LOG2E) + bias
                ex = jnp.exp2(s - jnp.max(s, axis=0, keepdims=True))
                S["pT"][g * 16 + h] = (ex * (1.0 / jnp.sum(ex, axis=0, keepdims=True))).astype(BF)

    def mix_values():
        @pl.loop(0, 2)
        def _(g):
            base = g * 384
            for j in range(8):
                vt = S["qkvT"][pl.ds(pl.multiple_of(2 * D + base + 48 * j, 16), 48), :]
                put_heads(ctxT, base, j, dotf(vt, two(S["pT"], g * 16 + 2 * j, 1)))

    def mixed():
        S["ctx"][...] = ctxT[...].astype(BF).T
        vec[...] = x[...].astype(F32) + dotf(S["ctx"][...], wf[:, 0:D])

    def norm_f():
        S["xhf"][...], S["rf"][...], S["fn"][...] = ln_rows(vec[...], lnf[0][...], lnf[1][...])

    def act():
        u = dotf(S["fn"][...], wf[:, D:2 * D])
        u2 = u * u
        t = jnp.tanh(GELU_A * (u + GELU_B * u * u2))
        S["act"][...] = (0.5 * u * (1.0 + t)).astype(BF)
        S["gp"][...] = 0.5 * (1.0 + t) + 0.5 * u * (1.0 - t * t) * (GELU_A + 3 * GELU_A * GELU_B * u2)

    def branch():
        br = dotf(S["act"][...], wf[:, 2 * D:3 * D]).astype(BF).astype(F32)
        y[...] = (vec[...].astype(BF).astype(F32) + br).astype(BF)

    return [norm_a, project, flip, scores, mix_values, mixed, norm_f, act, branch]


def backward_stages(G, gx, waT, wfT, lna, lnf, hm, S, W, glp, gb, gctx, gctxT, gqT, gsT, vec):
    D = G.shape[1]

    def ln_back(gref, xh, r, g, gi, resid, out):
        gn = gref[...]
        x = xh[...]
        gg = gn * g
        m1 = jnp.mean(gg, axis=-1, keepdims=True)
        m2 = jnp.mean(gg * x, axis=-1, keepdims=True)
        out[...] = (r[...] * (gg - m1 - x * m2) + resid[...].astype(F32)).astype(BF)
        glp[gi:gi + 1, :] += jnp.sum(gn * x, axis=0, keepdims=True)
        glp[gi + 1:gi + 2, :] += jnp.sum(gn, axis=0, keepdims=True)

    def g_act():
        W["f"][2 * D:3 * D, :] = G[...].T
        gb[...] = (dotf(G[...], wfT[2 * D:3 * D, :]) * S["gp"][...]).astype(BF)

    def g_norm():
        W["f"][D:2 * D, :] = gb[...].T
        vec[...] = dotf(gb[...], wfT[D:2 * D, :])

    def g_hidden():
        ln_back(vec, S["xhf"], S["rf"], lnf[0][...], 2, G, gb)

    def g_context():
        W["f"][0:D, :] = gb[...].T
        t = dotf(gb[...], wfT[0:D, :]).astype(BF)
        gctx[...] = t
        gctxT[...] = t.T

    def g_scores():
        @pl.loop(0, 2)
        def _(g):
            base = g * 384
            vw = windows(S["qkv"], slice(None), 2 * D + base)
            gw = windows(gctx, slice(None), base)
            for h in range(16):
                w = HEAD_WIN[h]
                gp = dot_t(vw[w] * hm[h:h + 1, :], gw[w])
                p = S["pT"][g * 16 + h].astype(F32)
                d = jnp.sum(p * gp, axis=0, keepdims=True)
                gsT[g * 16 + h] = (p * (gp - d)).astype(BF)

    def g_values():
        @pl.loop(0, 2)
        def _(g):
            base = g * 384
            for j in range(8):
                a = gctxT[pl.ds(pl.multiple_of(base + 48 * j, 16), 48), :]
                put_heads(gqT, 2 * D + base, j, dot_t(a, two(S["pT"], g * 16 + 2 * j, 0)))

    def g_keys():
        @pl.loop(0, 2)
        def _(g):
            base = g * 384
            for j in range(8):
                a = S["qkvT"][pl.ds(pl.multiple_of(base + 48 * j, 16), 48), :]
                put_heads(gqT, D + base, j, dot_t(a, two(gsT, g * 16 + 2 * j, 0)) * HS ** -0.5)

    def g_queries():
        @pl.loop(0, 2)
        def _(g):
            base = g * 384
            for j in range(8):
                a = S["qkvT"][pl.ds(pl.multiple_of(D + base + 48 * j, 16), 48), :]
                put_heads(gqT, base, j, dotf(a, two(gsT, g * 16 + 2 * j, 1)) * HS ** -0.5)

    def g_merge():
        t = gqT[...].astype(BF)
        W["a"][...] = t
        S["qkv"][...] = t.T

    def g_input():
        vec[...] = dotf(S["qkv"][...], waT[...])

    def g_x():
        ln_back(vec, S["xha"], S["ra"], lna[0][...], 0, gb, gx)

    return [g_act, g_norm, g_hidden, g_context, g_scores, g_values, g_keys, g_queries, g_merge, g_input, g_x]


def remote(src, dst, ss, rs, dev):
    return pltpu.make_async_remote_copy(
        src_ref=src, dst_ref=dst, send_sem=ss, recv_sem=rs, device_id=dev, device_id_type=MESH
    )


def when(cond, fn):
    pl.when(cond)(fn)


NZ = 4
SUB = 2
HALF = 1
ORDER = ((3, 2, 1, 0), (3, 0, 2, 1), (0, 3, 1, 2), (0, 1, 2, 3))


def by_place(vals, z):
    r = vals[-1]
    for i in range(len(vals) - 2, -1, -1):
        r = jnp.where(z == i, vals[i], r)
    return r


def rotation(mol, R):
    c0 = jnp.sum((mol == 0).astype(I32), axis=1, keepdims=True)
    c1 = jnp.sum((mol == 1).astype(I32), axis=1, keepdims=True)
    start = jnp.where(c0 == T, 0, jnp.where(c1 == T, c0, c0 + c1))
    i0 = lax.broadcasted_iota(I32, (R, R), 0)
    i1 = lax.broadcasted_iota(I32, (R, R), 1)

    def onehot(a, b):
        t = a + start
        t = jnp.where(t >= R, t - R, t)
        return jnp.where(t == b, 1.0, 0.0).astype(BF)

    return onehot(i0, i1), onehot(i1, i0)


def pair_bias(mol, key, rot, out, base, R):
    mk = jnp.concatenate([mol, key, jnp.zeros((6, R), I32)], axis=0).astype(F32).astype(BF)
    row = dot_t(mk, rot)
    col = dot_t(rot, mk)
    k0 = lax.broadcasted_iota(I32, (T, T), 0)
    q0 = lax.broadcasted_iota(I32, (T, T), 1)
    for b in range(R // T):
        rs = slice(b * T, b * T + T)
        ok = (col[rs, 0:1] == row[0:1, rs]) & ((col[rs, 1:2] > 0.5) | (k0 == q0))
        out[base + b] = jnp.where(ok, 0.0, NEG)


UNIT = ("xha", "ra", "an", "qkv", "qkvT", "pT", "ctx", "xhf", "rf", "fn", "act", "gp")


def unit_shapes(D):
    return (
        ((T, D), F32), ((T, 1), F32), ((T, D), BF), ((T, 3 * D), BF), ((3 * D, T), BF),
        ((HEADS, T, T), BF), ((T, D), BF), ((T, D), F32), ((T, 1), F32),
        ((T, D), BF), ((T, D), BF), ((T, D), F32),
    )


def relay_kernel(fused, tok, cot, w, gain, bias, mol, key, fo, ig, out_w, out_n, *scr):
    R, D = tok.shape
    n = len(UNIT)
    U = {k: r for k, r in zip(UNIT, scr[:n])}
    (
        wa, wf, waT, wfT, lga, lba, lgf, lbf, molo, keyo, rinv, hm, mb, X, G, ex, ys, gx, fob, igb,
        acca, accf, wga, wgf, rb, glp, glr, vec, gb, gctx, gctxT, gqT, gsT,
        wl_s, w_s, w_r, l_s, l_r, m_s, m_r, ex_s, ex_r, y_s, y_r, fo_s, fo_r, g_s, g_r, ig_s, ig_r,
        p_s, p_r, gl_s, gl_r,
    ) = scr[n:n + 54]
    s = lax.axis_index("section")
    e = lax.rem(s, 2)
    L = s // 2
    mate = {"section": s + 1 - 2 * e}
    other = {"section": s + 2 - 4 * L}
    d = lax.axis_index("dp")
    z = d // 2
    y = d - 2 * z
    across = {"dp": d + 1 - 2 * y}

    def on_line(zz):
        return {"dp": zz * 2 + y}

    bar = pltpu.get_barrier_semaphore()
    peers = [mate, other]
    if fused:
        peers += [across] + [on_line(lax.rem(z + t, NZ)) for t in range(1, NZ)]
    for p in peers:
        pl.semaphore_signal(bar, inc=1, device_id=p, device_id_type=MESH)
    pl.semaphore_wait(bar, len(peers))

    def third(c):
        return (slice(None), pl.ds(c * D, D))

    def w_local(k, j):
        src = (w, gain, bias)[j]
        return pltpu.make_async_copy(src, own[k][j], wl_s.at[j])

    def w_rem(k, j):
        if j < 3:
            return remote(w.at[third(j)], own[k][0].at[third(j)], w_s.at[j], w_r.at[j], mate)
        src = (gain, bias)[j - 3]
        return remote(src, own[k][j - 2], l_s.at[j - 3], l_r.at[j - 3], mate)

    own = ((wa, lga, lba), (wf, lgf, lbf))

    def per_core(fn):
        when(e == 0, lambda: fn(0))
        when(e == 1, lambda: fn(1))

    def send_weights(k):
        for j in (3, 4):
            w_rem(k, j).start()
        for j in range(3):
            w_local(k, j).start()
        for j in range(3):
            w_rem(k, j).start()

    per_core(send_weights)
    mol_copy = remote(mol, molo, m_s.at[0], m_r.at[0], other)
    key_copy = remote(key, keyo, m_s.at[1], m_r.at[1], other)
    mol_copy.start()
    key_copy.start()

    rot, inv = rotation(mol[...], R)
    rinv[...] = inv
    xr = dotf(rot, tok[...]).astype(BF)
    cr = dotf(rot, cot[...]).astype(BF)
    xu = xr.reshape(2, T, D)
    cu = cr.reshape(2, T, D)

    def ex_copy(dst):
        return remote(ex, dst, ex_s, ex_r, other)

    def stage0():
        ex[...] = cu
        ex_copy(G.at[pl.ds(0, 2)]).start()
        X[0:2] = xu

    def stage1():
        ex[...] = xu
        ex_copy(X.at[pl.ds(2, 2)]).start()
        G[2:4] = cu

    when(L == 0, stage0)
    when(L == 1, stage1)
    i0 = lax.broadcasted_iota(I32, (16, 256), 0)
    i1 = lax.broadcasted_iota(I32, (16, 256), 1)
    lo = HS * i0 - jnp.where(i0 < 10, 0, 128)
    hm[...] = jnp.where((i1 >= lo) & (i1 < lo + HS), 1.0, 0.0).astype(BF)
    glp[...] = jnp.zeros_like(glp)
    mol_copy.wait()
    key_copy.wait()
    pair_bias(mol[...], key[...], rot, mb, 2 * L, R)
    rot_o, _ = rotation(molo[...], R)
    pair_bias(molo[...], keyo[...], rot_o, mb, 2 - 2 * L, R)

    def wait_local(k):
        for j in range(3):
            w_local(k, j).wait()
        for j in (3, 4):
            w_rem(1 - k, j).wait_recv()

    per_core(wait_local)

    def wait_third(k, c):
        w_rem(k, c).wait_recv()

    def turn_weights():
        @pl.loop(0, 3)
        def _(i):
            cs = at(i, D)
            waT[cs, :] = wa[:, cs].T
            wfT[cs, :] = wf[:, cs].T

    def wait_all(k):
        for c in range(3):
            wait_third(1 - k, c)

    def ready1():
        per_core(wait_all)
        turn_weights()

    when(L == 1, ready1)

    def grads(acc, wg, rhs, p, first):
        for c in range(3):
            rs = slice(c * D, c * D + D)
            v = dotf(wg[p, rs, :], rhs[c][2 * p:2 * p + 2].reshape(2 * T, D))
            if not first:
                v = v + acc[rs, :].astype(F32)
            acc[rs, :] = v.astype(BF)

    def grads_f(p, first):
        grads(accf, wgf, (U["ctx"], U["fn"], U["act"]), p, first)

    def grads_a(p, first):
        grads(acca, wga, (U["an"],) * 3, p, first)

    if fused:
        yb, inb, raw, acc, gy, gz, ry_s, ry_r, rz_s, rz_r, rw_s, rw_r, rg_s, rg_r = scr[n + 54:]
        CH = 3 * D // (2 * NZ)
        SR = CH // SUB
        dest = [by_place([ORDER[k][i] for k in range(NZ)], z) for i in range(NZ)]
        buddy = z + 1 - 2 * lax.rem(z, 2)

        def rows(zz, yy, q):
            return pl.ds(pl.multiple_of((zz * 2 + yy) * CH + q * SR, 16), SR)

        def y_copy(i, q):
            return remote(rb.at[rows(dest[i], 1 - y, q), :], yb.at[i, q], ry_s.at[i, q], ry_r.at[i, q], across)

        def raw_copy(q):
            return remote(
                rb.at[rows(buddy, 1 - y, q), :], raw.at[q], rw_s.at[q], rw_r.at[q], on_line(buddy)
            )

        def piece(i):
            return pl.ds(pl.multiple_of(dest[i] * (2 * CH), 16), 2 * CH)
    else:
        def piece(i):
            return pl.ds(i * (3 * D // NZ), 3 * D // NZ)

    def p_copy(i, src):
        return remote(src.at[piece(i), :], rb.at[piece(i), :], p_s.at[i], p_r.at[i], mate)

    def give(src):
        for i in range(NZ):
            p_copy(i, src).start()

    def take(mine):
        for i in range(NZ):
            p_copy(i, mine).wait_recv()
            r = piece(i)
            rb[r, :] = (rb[r, :].astype(F32) + mine[r, :].astype(F32)).astype(BF)
            if fused and i < NZ - 1:
                def to_buddy():
                    for q in range(HALF):
                        raw_copy(q).start()

                def halves(i=i):
                    for q in range(HALF):
                        y_copy(i, q).start()

                when(dest[i] == buddy, to_buddy)
                when(dest[i] != buddy, halves)
                for q in range(HALF, SUB):
                    y_copy(i, q).start()

    def f_last():
        grads_f(1, False)
        when(e == 0, lambda: give(accf))

    def f_take():
        when(e == 1, lambda: take(accf))

    def a_last():
        grads_a(1, False)
        when(e == 1, lambda: give(acca))

    def y_copy_x(u):
        return remote(ys.at[u], X.at[u], y_s.at[u], y_r.at[u], other)

    def fo_copy(u):
        return remote(ys.at[u], fob.at[u], fo_s.at[u], fo_r.at[u], other)

    def g_copy(u):
        return remote(gx.at[u], G.at[u], g_s.at[u], g_r.at[u], other)

    def ig_copy(u):
        return remote(gx.at[u], igb.at[u - 2], ig_s.at[u - 2], ig_r.at[u - 2], other)

    def forward(u):
        S = {k: r.at[u] for k, r in U.items()}
        when(L == 1, lambda: y_copy_x(u).wait_recv())
        when((L == 0) & (u == 2), lambda: ex_copy(X.at[pl.ds(2, 2)]).wait_recv())
        opening = (L == 0) & (u == 0)
        st = forward_stages(
            X.at[u], ys.at[u], wa, wf, (lga, lba), (lgf, lbf), mb.at[u], hm, S, gqT.at[pl.ds(0, D)], vec
        )
        for f in st:
            if f.__name__ == "project":
                when(opening & (e == 1), lambda: wait_all(1))
            if f.__name__ in ("mixed", "act", "branch"):
                c = ("mixed", "act", "branch").index(f.__name__)
                when(opening & (e == 0), lambda c=c: wait_third(1, c))
            f()
        when(L == 0, lambda: y_copy_x(u).start())
        when((L == 1) & (u < 2), lambda: fo_copy(u).start())

        def keep():
            fob[u - 2] = ys[u]

        when((L == 1) & (u >= 2), keep)

    def backward(u):
        S = {k: r.at[u] for k, r in U.items()}
        when((L == 0) & (u == 0), turn_weights)
        when((L == 1) & (u == 0), lambda: ex_copy(G.at[pl.ds(0, 2)]).wait_recv())
        when(L == 0, lambda: g_copy(u).wait_recv())
        last = (L == 0) & (u == 3)
        p = u // 2
        lanes = at(u - 2 * p, T)
        st = backward_stages(
            G.at[u], gx.at[u], waT, wfT, (lga, lba), (lgf, lbf), hm, S,
            {"a": wga.at[p, :, lanes], "f": wgf.at[p, :, lanes]},
            glp, gb, gctx, gctxT, gqT, gsT, vec,
        )
        for f in st:
            f()
            if f.__name__ == "g_context":
                when(last, f_last)
            if f.__name__ == "g_scores":
                when(last, f_take)
            if f.__name__ == "g_merge":
                when(last, a_last)
        when(L == 1, lambda: g_copy(u).start())
        when((L == 0) & (u >= 2), lambda: ig_copy(u).start())

        def keep():
            igb[u] = gx[u]

        def first_pair():
            grads_f(0, True)
            grads_a(0, True)

        when((L == 0) & (u < 2), keep)
        when((L == 0) & (u == 1), first_pair)

    @pl.loop(0, 8)
    def _(i):
        odd = lax.rem(i, 2)
        is_f = jnp.where(L == 0, jnp.where(i < 4, 1, 0), 1 - odd)
        u = jnp.where(L == 0, lax.rem(i, 4), i // 2)
        when(is_f == 1, lambda: forward(u))
        when(is_f == 0, lambda: backward(u))

    def finish1():
        grads_f(0, True)
        f_last()
        grads_a(0, True)
        f_take()
        a_last()

    when(L == 1, finish1)
    gl_copy = remote(glp, glr, gl_s, gl_r, mate)
    gl_copy.start()
    when(e == 0, lambda: take(acca))

    def bring0():
        for u in range(2):
            fo_copy(u).wait_recv()

    def bring1():
        for u in (2, 3):
            ig_copy(u).wait_recv()

    when(L == 0, bring0)
    when(L == 1, bring1)
    fo[...] = dotf(rinv[...], fob[...].reshape(R, D)).astype(BF)
    ig[...] = dotf(rinv[...], igb[...].reshape(R, D))
    gl_copy.wait()

    if fused:
        gl1 = glp[...] + glr[...]
        glr[...] = gl1
        gy_copy = remote(glr, gy, rg_s.at[0], rg_r.at[0], across)
        gy_copy.start()

        def own_y():
            for q in range(SUB):
                if q < HALF:
                    raw_copy(q).wait()
                    r = rows(z, 1 - y, q)
                    rb[r, :] = (rb[r, :].astype(F32) + raw[q].astype(F32)).astype(BF)
                y_copy(NZ - 1, q).start()

        def hop(i, q):
            zz = dest[i]
            nz = jnp.where(zz > z, z + 1, z - 1)
            slot = jnp.where((nz == zz) & (z > zz), NZ, zz)
            return remote(yb.at[i, q], inb.at[slot, q], rz_s.at[i, q], rz_r.at[slot, q], on_line(nz))

        def arrived(slot, q):
            remote(yb.at[0, q], inb.at[slot, q], rz_s.at[0, q], rz_r.at[slot, q], across).wait_recv()

        for i in range(NZ - 1):
            zz = dest[i]
            for q in range(SUB):
                mine = rb.at[rows(zz, y, q), :]

                def combine(i=i, q=q, mine=mine):
                    y_copy(i, q).wait_recv()
                    yb[i, q] = (mine[...].astype(F32) + yb[i, q].astype(F32)).astype(BF)

                def plain(i=i, q=q, mine=mine):
                    yb[i, q] = mine[...]

                def add_in(i=i, q=q, zz=zz):
                    arrived(zz, q)
                    yb[i, q] = (yb[i, q].astype(F32) + inb[zz, q].astype(F32)).astype(BF)

                if q < HALF:
                    when(zz != buddy, combine)
                    when(zz == buddy, plain)
                else:
                    combine()
                when(jnp.where(zz > z, z > 0, z < NZ - 1), add_in)
                hop(i, q).start()
            if i == NZ - 3:
                own_y()
        gy_copy.wait()
        gl2 = glr[...] + gy[...]
        out_n[...] = gl2
        gz_copies = [
            remote(out_n, gz.at[NZ - t - 1], rg_s.at[t], rg_r.at[NZ - t], on_line(lax.rem(z + t, NZ)))
            for t in range(1, NZ)
        ]
        for c in gz_copies:
            c.start()
        for q in range(SUB):
            acc[q] = rb[rows(z, y, q), :].astype(F32)

            def from_left(q=q):
                arrived(z, q)
                acc[q] += inb[z, q].astype(F32)

            def from_right(q=q):
                arrived(NZ, q)
                acc[q] += inb[NZ, q].astype(F32)

            when(z > 0, from_left)
            when(z < NZ - 1, from_right)
            y_copy(NZ - 1, q).wait_recv()
            acc[q] += yb[NZ - 1, q].astype(F32)
        out_w[...] = acc[...].reshape(CH, D).T
        for i in range(NZ):
            for q in range(SUB):
                if q < HALF and i < NZ - 1:
                    when(dest[i] != buddy, lambda i=i, q=q: y_copy(i, q).wait_send())
                else:
                    y_copy(i, q).wait_send()
                if i < NZ - 1:
                    hop(i, q).wait_send()
        for t, c in zip(range(1, NZ), gz_copies):
            c.wait_send()
        for k in range(NZ - 1):
            remote(out_n, gz.at[k], rg_s.at[0], rg_r.at[k + 1], across).wait_recv()
        out_n[...] = gl2 + gz[0] + gz[1] + gz[2]
    else:
        out_w[...] = rb[...]
        out_n[...] = glp[...] + glr[...]

    def close_weights(k):
        for j in range(5):
            w_rem(k, j).wait_send()

    per_core(close_weights)
    def gave(src):
        for i in range(NZ):
            p_copy(i, src).wait_send()

    when(e == 0, lambda: gave(accf))
    when(e == 1, lambda: gave(acca))
    ex_copy(X.at[pl.ds(2, 2)]).wait_send()

    def close0():
        for u in range(4):
            y_copy_x(u).wait_send()
        for u in (2, 3):
            ig_copy(u).wait_send()

    def close1():
        for u in range(4):
            g_copy(u).wait_send()
        for u in range(2):
            fo_copy(u).wait_send()

    when(L == 0, close0)
    when(L == 1, close1)


def relay(fused, tok, cot, w, gain, bias, mol, key):
    R, D = tok.shape
    V = pl.BlockSpec(memory_space=pltpu.VMEM)
    dma, vm = pltpu.SemaphoreType.DMA, pltpu.VMEM
    scratch = [vm((4,) + sh, dt) for sh, dt in unit_shapes(D)] + [
        vm((D, 3 * D), BF), vm((D, 3 * D), BF), vm((3 * D, D), BF), vm((3 * D, D), BF),
        vm((1, D), F32), vm((1, D), F32), vm((1, D), F32), vm((1, D), F32),
        vm((1, R), I32), vm((1, R), I32), vm((R, R), BF), vm((16, 256), BF), vm((4, T, T), F32),
        vm((4, T, D), BF), vm((4, T, D), BF), vm((2, T, D), BF), vm((4, T, D), BF), vm((4, T, D), BF),
        vm((2, T, D), BF), vm((2, T, D), BF),
        vm((3 * D, D), BF), vm((3 * D, D), BF), vm((2, 3 * D, 2 * T), BF), vm((2, 3 * D, 2 * T), BF),
        vm((3 * D, D), BF), vm((8, D), F32), vm((8, D), F32),
        vm((T, D), F32), vm((T, D), BF), vm((T, D), BF), vm((D, T), BF),
        vm((3 * D, T), F32), vm((HEADS, T, T), BF),
        dma((3,)), dma((3,)), dma((3,)), dma((2,)), dma((2,)), dma((2,)), dma((2,)), dma, dma,
        dma((4,)), dma((4,)), dma((2,)), dma((2,)), dma((4,)), dma((4,)), dma((2,)), dma((2,)),
        dma((NZ,)), dma((NZ,)), dma, dma,
    ]
    if fused:
        CH = 3 * D // (2 * NZ)
        SR = CH // SUB
        scratch += [
            vm((NZ, SUB, SR, D), BF), vm((NZ + 1, SUB, SR, D), BF), vm((HALF, SR, D), BF),
            vm((SUB, SR, D), F32), vm((8, D), F32), vm((NZ - 1, 8, D), F32),
            dma((NZ, SUB)), dma((NZ, SUB)), dma((NZ - 1, SUB)), dma((NZ + 1, SUB)),
            dma((HALF,)), dma((HALF,)), dma((NZ,)), dma((NZ,)),
        ]
        w_out = jax.ShapeDtypeStruct((D, CH), F32)
    else:
        w_out = jax.ShapeDtypeStruct((3 * D, D), BF)
    return pl.pallas_call(
        lambda *refs: relay_kernel(fused, *refs),
        out_shape=[
            jax.ShapeDtypeStruct((R, D), BF),
            jax.ShapeDtypeStruct((R, D), F32),
            w_out,
            jax.ShapeDtypeStruct((8, D), F32),
        ],
        in_specs=[V, V, pl.BlockSpec(memory_space=pl.ANY), V, V, V, V],
        out_specs=[V] * 4,
        scratch_shapes=scratch,
        compiler_params=pltpu.CompilerParams(
            collective_id=0, has_side_effects=True, vmem_limit_bytes=64 << 20
        ),
        name="relay",
    )(tok, cot, w, gain, bias, mol, key)


def shards(tokens, cotangent, section_weight, norm_gain, norm_bias, mol_ids, key_mask):
    D = tokens.shape[1]
    ranks = lax.axis_size("dp")
    fused = ranks == 2 * NZ
    fo, ig, gw, gn = relay(
        fused, tokens, cotangent, section_weight[0], norm_gain, norm_bias, mol_ids, key_mask
    )
    e = lax.rem(lax.axis_index("section"), 2)
    if fused:
        part = D // ranks
        gn = lax.dynamic_slice(gn, (2 * e, lax.axis_index("dp") * part), (2, part))
        return fo, ig, gw[None], gn[0:1], gn[1:2]
    gn = lax.dynamic_slice_in_dim(gn, 2 * e, 2, 0)
    gw = lax.psum_scatter(gw, "dp", scatter_dimension=0, tiled=True)
    gn = lax.psum_scatter(gn, "dp", scatter_dimension=1, tiled=True)
    return fo, ig, gw.astype(F32).T[None], gn[0:1], gn[1:2]


def solution(mesh):
    return jax.shard_map(
        shards,
        mesh=mesh,
        in_specs=(
            P(("dp", "section"), None),
            P(("dp", "section"), None),
            P("section", None, None),
            P("section", None),
            P("section", None),
            P(("dp", "section"), None),
            P(("dp", "section"), None),
        ),
        out_specs=(
            P(("dp", "section"), None),
            P(("dp", "section"), None),
            P("section", None, "dp"),
            P("section", "dp"),
            P("section", "dp"),
        ),
        check_vma=False,
    )
```

time: 1420 us -> 121 us (0.09); the launches traced: 1400 us -> 121 us
  matrix products: 502 us -> 0 us
  waiting for transfers between devices: 342 us -> 0 us
  other arithmetic: 234 us -> 0 us
  local copies, waits for them, and re-layouts: 220 us -> 7.66 us
  Pallas kernels: 0 us -> 112 us
  starting transfers between devices: 43.5 us -> 0 us
  loops' own time: 32.5 us -> 0 us
  between operations: 15.4 us -> 0.66 us
    dot_general x168 -> x0, matrix products: 352 us -> none  [the longest x28 76.3 us: one_group(): jnp.einsum('gqk,gqd->gkd', soft_probs.astype(jnp.bfloat16), g_group, pref...]
    reduce_scatter x3 -> x0, waiting for transfers between devices: 191 us -> none  [the longest x1 133 us: shards(): lax.psum_scatter(grad_weight[None], 'dp', scatter_dimension=2, tiled=True)]
    sub x56 -> x0, matrix products: 150 us -> none  [softmax_probs(): weights_exp = jnp.exp(scores - top_score)]
    unnamed x9 -> x0, waiting for transfers between devices: 134 us -> none
    slice x71 -> x1, local copies, waits for them, and re-layouts: 115 us -> 0.52 us  [shards(): return (fo, ig, gw[None], gn[0:1], gn[1:2])]
    pallas_call x0 -> x1, Pallas kernels: none -> 112 us  [relay(): pl.pallas_call(lambda *refs: relay_kernel(fused, *refs), out_shape=[jax.S...]
    reduce_sum x35 -> x0, other arithmetic: 56.6 us -> none  [the longest x14 20.6 us: normalize(): center = values - jnp.mean(values, axis=-1, keepdims=True)]
    ppermute x12 -> x0, starting transfers between devices: 43.2 us -> none  [shifted(): return lax.ppermute(block, axis, route)]
  transfers between devices with their start and end apart: 19 -> 0, of which waited for: 9 -> 0; matrix products, arithmetic and copies ran while one was open for 14% -> 0% of each run, Pallas kernels for 0% -> 0%
where the time goes in v2:
time: 121 us
  Pallas kernels  112 us (93%)
  local copies, waits for them, and re-layouts  7.66 us (6%)
    pallas_call x1, Pallas kernels, relay(): pl.pallas_call(lambda *refs: relay_kernel(fused, *refs), out_shape=[jax.S...  112 us
    unnamed x3, local copies, waits for them, and re-layouts  6.35 us

profile of v2, /device:TPU:0, one launch (start us, length us, event | category | flops | bytes accessed | tf_op | source)
XLA Modules:
  0.0 120.8 jit_solution(15608136919459108739)
XLA Ops:
  0.6 112.5 %relay.1 = (bf16[256,768]{1,0:T(8,128)(2,1)}, f32[256,768]{1,0:T(8,128)}, f32[768,288]{1,0:T(8,128)}, f32[8,768]{1,0:T(8,128)}) custom-call(bf16[256,768]{1,0:T(8,128)(2,1)} %refs_0_.1, bf16[256,768]{1,0:T(8,128)(2,1)} %refs_1_.1, bf16[768,2304]{1,0:T(8,128)(2,1)} %bitcast.2, f32[1,768]{1,0:T(1,128)} %refs_3_.1, f32[1,768]{1,0:T(1,128)} %refs_4_.1, ...), custom_call_target="tpu_custom_call" | custom-call | tf_op jit(solution)/shard_map/relay/pallas_call | solution.py:705
  113.1 0.8 dynamic_slice.3
  113.9 0.5 fusion
  114.4 2.5 %copy.12 = f32[1,768,288]{1,2,0:T(8,128)} copy(f32[1,768,288]{2,1,0:T(8,128)} %bitcast.3) | data formatting | bytes 1769472
  117.0 1.8 %copy.15 = bf16[256,768]{1,0:T(8,128)(2,1)} copy(bf16[256,768]{1,0:T(8,128)(2,1)} %get-tuple-element.25) | data formatting | bytes 786432
  118.7 2.1 %copy.16 = f32[256,768]{1,0:T(8,128)} copy(f32[256,768]{1,0:T(8,128)} %get-tuple-element.26) | data formatting | bytes 1572864

commit v3 on v2

--- a/solution.py
+++ b/solution.py
@@ -42,12 +42,12 @@
 
 
 def windows(ref, rows, base):
-    return [ref[rows, pl.ds(pl.multiple_of(base + 128 * w, 128), 256)] for w in (0, 1)]
+    return [ref[rows, base + 128 * w:base + 128 * w + 256] for w in (0, 1)]
 
 
 def put_heads(ref, base, j, v):
-    ref[pl.ds(pl.multiple_of(base + 48 * j, 8), 24), :] = v[0:24, 0:T]
-    ref[pl.ds(pl.multiple_of(base + 48 * j + 24, 8), 24), :] = v[24:48, T:2 * T]
+    ref[base + 48 * j:base + 48 * j + 24, :] = v[0:24, 0:T]
+    ref[base + 48 * j + 24:base + 48 * j + 48, :] = v[24:48, T:2 * T]
 
 
 def two(ref, i, axis):
@@ -67,10 +67,9 @@
         S["qkvT"][...] = S["qkv"][...].T
 
     def scores():
-        @pl.loop(0, 2)
-        def _(g):
+        bias = mb[...]
+        for g in range(2):
             base = g * 384
-            bias = mb[...]
             qw = windows(S["qkv"], slice(None), base)
             kw = windows(S["qkv"], slice(None), D + base)
             for h in range(16):
@@ -80,11 +79,10 @@
                 S["pT"][g * 16 + h] = (ex * (1.0 / jnp.sum(ex, axis=0, keepdims=True))).astype(BF)
 
     def mix_values():
-        @pl.loop(0, 2)
-        def _(g):
+        for g in range(2):
             base = g * 384
             for j in range(8):
-                vt = S["qkvT"][pl.ds(pl.multiple_of(2 * D + base + 48 * j, 16), 48), :]
+                vt = S["qkvT"][2 * D + base + 48 * j:2 * D + base + 48 * j + 48, :]
                 put_heads(ctxT, base, j, dotf(vt, two(S["pT"], g * 16 + 2 * j, 1)))
 
     def mixed():
@@ -139,8 +137,7 @@
         gctxT[...] = t.T
 
     def g_scores():
-        @pl.loop(0, 2)
-        def _(g):
+        for g in range(2):
             base = g * 384
             vw = windows(S["qkv"], slice(None), 2 * D + base)
             gw = windows(gctx, slice(None), base)
@@ -151,29 +148,16 @@
                 d = jnp.sum(p * gp, axis=0, keepdims=True)
                 gsT[g * 16 + h] = (p * (gp - d)).astype(BF)
 
-    def g_values():
-        @pl.loop(0, 2)
-        def _(g):
+    def g_heads():
+        for g in range(2):
             base = g * 384
             for j in range(8):
-                a = gctxT[pl.ds(pl.multiple_of(base + 48 * j, 16), 48), :]
-                put_heads(gqT, 2 * D + base, j, dot_t(a, two(S["pT"], g * 16 + 2 * j, 0)))
-
-    def g_keys():
-        @pl.loop(0, 2)
-        def _(g):
-            base = g * 384
-            for j in range(8):
-                a = S["qkvT"][pl.ds(pl.multiple_of(base + 48 * j, 16), 48), :]
-                put_heads(gqT, D + base, j, dot_t(a, two(gsT, g * 16 + 2 * j, 0)) * HS ** -0.5)
-
-    def g_queries():
-        @pl.loop(0, 2)
-        def _(g):
-            base = g * 384
-            for j in range(8):
-                a = S["qkvT"][pl.ds(pl.multiple_of(D + base + 48 * j, 16), 48), :]
-                put_heads(gqT, base, j, dotf(a, two(gsT, g * 16 + 2 * j, 1)) * HS ** -0.5)
+                i = g * 16 + 2 * j
+                at48 = slice(base + 48 * j, base + 48 * j + 48)
+                put_heads(gqT, 2 * D + base, j, dot_t(gctxT[at48, :], two(S["pT"], i, 0)))
+                put_heads(gqT, D + base, j, dot_t(S["qkvT"][at48, :], two(gsT, i, 0)) * HS ** -0.5)
+                k48 = slice(D + base + 48 * j, D + base + 48 * j + 48)
+                put_heads(gqT, base, j, dotf(S["qkvT"][k48, :], two(gsT, i, 1)) * HS ** -0.5)
 
     def g_merge():
         t = gqT[...].astype(BF)
@@ -186,7 +170,7 @@
     def g_x():
         ln_back(vec, S["xha"], S["ra"], lna[0][...], 0, gb, gx)
 
-    return [g_act, g_norm, g_hidden, g_context, g_scores, g_values, g_keys, g_queries, g_merge, g_input, g_x]
+    return [g_act, g_norm, g_hidden, g_context, g_scores, g_heads, g_merge, g_input, g_x]
 
 
 def remote(src, dst, ss, rs, dev):
@@ -250,16 +234,17 @@
     )
 
 
-def relay_kernel(fused, tok, cot, w, gain, bias, mol, key, fo, ig, out_w, out_n, *scr):
+def relay_kernel(fused, tok, cot, w, gain, bias, mol, key, fo_hbm, ig_hbm, w_hbm, *scr):
     R, D = tok.shape
+    norms, scr = (scr[:2], scr[2:]) if fused else (scr[:1], scr[1:])
     n = len(UNIT)
     U = {k: r for k, r in zip(UNIT, scr[:n])}
     (
         wa, wf, waT, wfT, lga, lba, lgf, lbf, molo, keyo, rinv, hm, mb, X, G, ex, ys, gx, fob, igb,
         acca, accf, wga, wgf, rb, glp, glr, vec, gb, gctx, gctxT, gqT, gsT,
         wl_s, w_s, w_r, l_s, l_r, m_s, m_r, ex_s, ex_r, y_s, y_r, fo_s, fo_r, g_s, g_r, ig_s, ig_r,
-        p_s, p_r, gl_s, gl_r,
-    ) = scr[n:n + 54]
+        p_s, p_r, gl_s, gl_r, fo, ig, o_s,
+    ) = scr[n:n + 57]
     s = lax.axis_index("section")
     e = lax.rem(s, 2)
     L = s // 2
@@ -390,7 +375,7 @@
         grads(acca, wga, (U["an"],) * 3, p, first)
 
     if fused:
-        yb, inb, raw, acc, gy, gz, ry_s, ry_r, rz_s, rz_r, rw_s, rw_r, rg_s, rg_r = scr[n + 54:]
+        yb, inb, raw, acc, gy, gz, gn, out_w, ry_s, ry_r, rz_s, rz_r, rw_s, rw_r, rg_s, rg_r = scr[n + 57:]
         CH = 3 * D // (2 * NZ)
         SR = CH // SUB
         dest = [by_place([ORDER[k][i] for k in range(NZ)], z) for i in range(NZ)]
@@ -447,8 +432,11 @@
         when(e == 1, lambda: take(accf))
 
     def a_last():
-        grads_a(1, False)
-        when(e == 1, lambda: give(acca))
+        rhs = U["an"][2:4].reshape(2 * T, D)
+        for i in range(NZ):
+            r = piece(i)
+            acca[r, :] = (dotf(wga[1, r, :], rhs) + acca[r, :].astype(F32)).astype(BF)
+            when(e == 1, lambda i=i: p_copy(i, acca).start())
 
     def y_copy_x(u):
         return remote(ys.at[u], X.at[u], y_s.at[u], y_r.at[u], other)
@@ -502,10 +490,9 @@
             f()
             if f.__name__ == "g_context":
                 when(last, f_last)
-            if f.__name__ == "g_scores":
-                when(last, f_take)
             if f.__name__ == "g_merge":
                 when(last, a_last)
+                when(last, f_take)
         when(L == 1, lambda: g_copy(u).start())
         when((L == 0) & (u >= 2), lambda: ig_copy(u).start())
 
@@ -531,8 +518,8 @@
         grads_f(0, True)
         f_last()
         grads_a(0, True)
+        a_last()
         f_take()
-        a_last()
 
     when(L == 1, finish1)
     gl_copy = remote(glp, glr, gl_s, gl_r, mate)
@@ -551,6 +538,9 @@
     when(L == 1, bring1)
     fo[...] = dotf(rinv[...], fob[...].reshape(R, D)).astype(BF)
     ig[...] = dotf(rinv[...], igb[...].reshape(R, D))
+    emits = [pltpu.make_async_copy(fo, fo_hbm, o_s.at[0]), pltpu.make_async_copy(ig, ig_hbm, o_s.at[1])]
+    for c in emits:
+        c.start()
     gl_copy.wait()
 
     if fused:
@@ -603,9 +593,9 @@
                 own_y()
         gy_copy.wait()
         gl2 = glr[...] + gy[...]
-        out_n[...] = gl2
+        gn[...] = gl2
         gz_copies = [
-            remote(out_n, gz.at[NZ - t - 1], rg_s.at[t], rg_r.at[NZ - t], on_line(lax.rem(z + t, NZ)))
+            remote(gn, gz.at[NZ - t - 1], rg_s.at[t], rg_r.at[NZ - t], on_line(lax.rem(z + t, NZ)))
             for t in range(1, NZ)
         ]
         for c in gz_copies:
@@ -625,7 +615,9 @@
             when(z < NZ - 1, from_right)
             y_copy(NZ - 1, q).wait_recv()
             acc[q] += yb[NZ - 1, q].astype(F32)
-        out_w[...] = acc[...].reshape(CH, D).T
+        out_w[...] = acc[...].reshape(CH, D)
+        w_copy = pltpu.make_async_copy(out_w, w_hbm, o_s.at[2])
+        w_copy.start()
         for i in range(NZ):
             for q in range(SUB):
                 if q < HALF and i < NZ - 1:
@@ -637,11 +629,22 @@
         for t, c in zip(range(1, NZ), gz_copies):
             c.wait_send()
         for k in range(NZ - 1):
-            remote(out_n, gz.at[k], rg_s.at[0], rg_r.at[k + 1], across).wait_recv()
-        out_n[...] = gl2 + gz[0] + gz[1] + gz[2]
+            remote(gn, gz.at[k], rg_s.at[0], rg_r.at[k + 1], across).wait_recv()
+        gl3 = gl2 + gz[0] + gz[1] + gz[2]
+        part = D // (2 * NZ)
+        for k in range(2 * NZ):
+            def own_part(k=k):
+                for j in range(2):
+                    v = gl3[:, k * part:(k + 1) * part]
+                    norms[j][...] = jnp.where(e == 0, v[j:j + 1, :], v[2 + j:3 + j, :])
+
+            when(d == k, own_part)
     else:
-        out_w[...] = rb[...]
-        out_n[...] = glp[...] + glr[...]
+        norms[0][...] = glp[...] + glr[...]
+        w_copy = pltpu.make_async_copy(rb, w_hbm, o_s.at[2])
+        w_copy.start()
+    for c in emits + [w_copy]:
+        c.wait()
 
     def close_weights(k):
         for j in range(5):
@@ -688,30 +691,26 @@
         vm((3 * D, T), F32), vm((HEADS, T, T), BF),
         dma((3,)), dma((3,)), dma((3,)), dma((2,)), dma((2,)), dma((2,)), dma((2,)), dma, dma,
         dma((4,)), dma((4,)), dma((2,)), dma((2,)), dma((4,)), dma((4,)), dma((2,)), dma((2,)),
-        dma((NZ,)), dma((NZ,)), dma, dma,
+        dma((NZ,)), dma((NZ,)), dma, dma, vm((R, D), BF), vm((R, D), F32), dma((3,)),
     ]
     if fused:
         CH = 3 * D // (2 * NZ)
         SR = CH // SUB
         scratch += [
             vm((NZ, SUB, SR, D), BF), vm((NZ + 1, SUB, SR, D), BF), vm((HALF, SR, D), BF),
-            vm((SUB, SR, D), F32), vm((8, D), F32), vm((NZ - 1, 8, D), F32),
+            vm((SUB, SR, D), F32), vm((8, D), F32), vm((NZ - 1, 8, D), F32), vm((8, D), F32), vm((CH, D), F32),
             dma((NZ, SUB)), dma((NZ, SUB)), dma((NZ - 1, SUB)), dma((NZ + 1, SUB)),
             dma((HALF,)), dma((HALF,)), dma((NZ,)), dma((NZ,)),
         ]
-        w_out = jax.ShapeDtypeStruct((D, CH), F32)
+        outs = [jax.ShapeDtypeStruct((CH, D), F32)] + [jax.ShapeDtypeStruct((1, D // (2 * NZ)), F32)] * 2
     else:
-        w_out = jax.ShapeDtypeStruct((3 * D, D), BF)
+        outs = [jax.ShapeDtypeStruct((3 * D, D), BF), jax.ShapeDtypeStruct((8, D), F32)]
+    A = pl.BlockSpec(memory_space=pl.ANY)
     return pl.pallas_call(
         lambda *refs: relay_kernel(fused, *refs),
-        out_shape=[
-            jax.ShapeDtypeStruct((R, D), BF),
-            jax.ShapeDtypeStruct((R, D), F32),
-            w_out,
-            jax.ShapeDtypeStruct((8, D), F32),
-        ],
-        in_specs=[V, V, pl.BlockSpec(memory_space=pl.ANY), V, V, V, V],
-        out_specs=[V] * 4,
+        out_shape=[jax.ShapeDtypeStruct((R, D), BF), jax.ShapeDtypeStruct((R, D), F32)] + outs,
+        in_specs=[V, V, A, V, V, V, V],
+        out_specs=[A, A, A] + [V] * (len(outs) - 1),
         scratch_shapes=scratch,
         compiler_params=pltpu.CompilerParams(
             collective_id=0, has_side_effects=True, vmem_limit_bytes=64 << 20
@@ -720,18 +719,41 @@
     )(tok, cot, w, gain, bias, mol, key)
 
 
+def emit_kernel(*refs):
+    n = len(refs) // 3
+    sems = refs[-1]
+    ins = [pltpu.make_async_copy(refs[i], refs[2 * n + i], sems.at[0, i]) for i in range(n)]
+    outs = [pltpu.make_async_copy(refs[2 * n + i], refs[n + i], sems.at[1, i]) for i in range(n)]
+    for c in ins:
+        c.start()
+    for a, b in zip(ins, outs):
+        a.wait()
+        b.start()
+    for c in outs:
+        c.wait()
+
+
+def emit(arrays):
+    A = pl.BlockSpec(memory_space=pl.ANY)
+    n = len(arrays)
+    return pl.pallas_call(
+        emit_kernel,
+        out_shape=[jax.ShapeDtypeStruct(a.shape, a.dtype) for a in arrays],
+        in_specs=[A] * n,
+        out_specs=[A] * n,
+        scratch_shapes=[pltpu.VMEM(a.shape, a.dtype) for a in arrays] + [pltpu.SemaphoreType.DMA((2, n))],
+        name="emit",
+    )(*arrays)
+
+
 def shards(tokens, cotangent, section_weight, norm_gain, norm_bias, mol_ids, key_mask):
-    D = tokens.shape[1]
-    ranks = lax.axis_size("dp")
-    fused = ranks == 2 * NZ
-    fo, ig, gw, gn = relay(
-        fused, tokens, cotangent, section_weight[0], norm_gain, norm_bias, mol_ids, key_mask
-    )
+    fused = lax.axis_size("dp") == 2 * NZ
+    got = relay(fused, tokens, cotangent, section_weight[0], norm_gain, norm_bias, mol_ids, key_mask)
+    if fused:
+        fo, ig, gw, gg, gb = emit(got)
+        return fo, ig, gw.T[None], gg, gb
+    fo, ig, gw, gn = got
     e = lax.rem(lax.axis_index("section"), 2)
-    if fused:
-        part = D // ranks
-        gn = lax.dynamic_slice(gn, (2 * e, lax.axis_index("dp") * part), (2, part))
-        return fo, ig, gw[None], gn[0:1], gn[1:2]
     gn = lax.dynamic_slice_in_dim(gn, 2 * e, 2, 0)
     gw = lax.psum_scatter(gw, "dp", scatter_dimension=0, tiled=True)
     gn = lax.psum_scatter(gn, "dp", scatter_dimension=1, tiled=True)

time: 121 us -> 103 us (0.85)
  Pallas kernels: 112 us -> 102 us
  local copies, waits for them, and re-layouts: 7.66 us -> 0 us
    pallas_call x1, Pallas kernels: 112 us -> 99.8 us  [relay(): pl.pallas_call(lambda *refs: relay_kernel(fused, *refs), out_shape=[jax.S...]
    unnamed x3 -> x0, local copies, waits for them, and re-layouts: 6.35 us -> none
    pallas_call x0 -> x1, Pallas kernels: none -> 2.53 us  [emit(): pl.pallas_call(emit_kernel, out_shape=[jax.ShapeDtypeStruct(a.shape, a.dt...]
where the time goes in v3:
time: 103 us
  Pallas kernels  102 us (99%)
    pallas_call x1, Pallas kernels, relay(): pl.pallas_call(lambda *refs: relay_kernel(fused, *refs), out_shape=[jax.S...  99.8 us
    pallas_call x1, Pallas kernels, emit(): pl.pallas_call(emit_kernel, out_shape=[jax.ShapeDtypeStruct(a.shape, a.dt...  2.53 us

profile of v3, /device:TPU:0, one launch (start us, length us, event | category | flops | bytes accessed | tf_op | source)
XLA Modules:
  0.0 103.2 jit_solution(948869823268428261)
XLA Ops:
  0.6 99.8 %relay.1 = (bf16[256,768]{1,0:T(8,128)(2,1)}, f32[256,768]{1,0:T(8,128)}, f32[288,768]{1,0:T(8,128)}, f32[1,96]{1,0:T(1,128)}, f32[1,96]{1,0:T(1,128)}) custom-call(bf16[256,768]{1,0:T(8,128)(2,1)} %refs_0_.1, bf16[256,768]{1,0:T(8,128)(2,1)} %refs_1_.1, bf16[768,2304]{1,0:T(8,128)(2,1)} %bitcast.4, f32[1,768]{1,0:T(1,128)} %refs_3_.1, f32[1,768]{1,0:T(1,128)} %refs_4_.1, ...), custom_call_target="tpu_custom_call" | custom-call | tf_op jit(solution)/shard_map/relay/pallas_call | solution.py:709
  100.4 2.5 %emit.1 = (bf16[256,768]{1,0:T(8,128)(2,1)}, f32[256,768]{1,0:T(8,128)}, f32[288,768]{1,0:T(8,128)}, f32[1,96]{1,0:T(1,128)}, f32[1,96]{1,0:T(1,128)}) custom-call(bf16[256,768]{1,0:T(8,128)(2,1)} %get-tuple-element.15.refs_0_, f32[256,768]{1,0:T(8,128)} %get-tuple-element.16.refs_1_, f32[288,768]{1,0:T(8,128)} %get-tuple-element.17.refs_2_, ...), custom_call_target="tpu_custom_call" | custom-call | tf_op jit(solution)/shard_map/emit/pallas_call | solution.py:739

commit v4 on v3

--- a/solution.py
+++ b/solution.py
@@ -86,21 +86,21 @@
                 put_heads(ctxT, base, j, dotf(vt, two(S["pT"], g * 16 + 2 * j, 1)))
 
     def mixed():
-        S["ctx"][...] = ctxT[...].astype(BF).T
-        vec[...] = x[...].astype(F32) + dotf(S["ctx"][...], wf[:, 0:D])
+        S["cfa"][0] = ctxT[...].astype(BF).T
+        vec[...] = x[...].astype(F32) + dotf(S["cfa"][0], wf[:, 0:D])
 
     def norm_f():
-        S["xhf"][...], S["rf"][...], S["fn"][...] = ln_rows(vec[...], lnf[0][...], lnf[1][...])
+        S["xhf"][...], S["rf"][...], S["cfa"][1] = ln_rows(vec[...], lnf[0][...], lnf[1][...])
 
     def act():
-        u = dotf(S["fn"][...], wf[:, D:2 * D])
+        u = dotf(S["cfa"][1], wf[:, D:2 * D])
         u2 = u * u
         t = jnp.tanh(GELU_A * (u + GELU_B * u * u2))
-        S["act"][...] = (0.5 * u * (1.0 + t)).astype(BF)
+        S["cfa"][2] = (0.5 * u * (1.0 + t)).astype(BF)
         S["gp"][...] = 0.5 * (1.0 + t) + 0.5 * u * (1.0 - t * t) * (GELU_A + 3 * GELU_A * GELU_B * u2)
 
     def branch():
-        br = dotf(S["act"][...], wf[:, 2 * D:3 * D]).astype(BF).astype(F32)
+        br = dotf(S["cfa"][2], wf[:, 2 * D:3 * D]).astype(BF).astype(F32)
         y[...] = (vec[...].astype(BF).astype(F32) + br).astype(BF)
 
     return [norm_a, project, flip, scores, mix_values, mixed, norm_f, act, branch]
@@ -223,14 +223,13 @@
         out[base + b] = jnp.where(ok, 0.0, NEG)
 
 
-UNIT = ("xha", "ra", "an", "qkv", "qkvT", "pT", "ctx", "xhf", "rf", "fn", "act", "gp")
+UNIT = ("xha", "ra", "an", "qkv", "qkvT", "pT", "xhf", "rf", "cfa", "gp")
 
 
 def unit_shapes(D):
     return (
         ((T, D), F32), ((T, 1), F32), ((T, D), BF), ((T, 3 * D), BF), ((3 * D, T), BF),
-        ((HEADS, T, T), BF), ((T, D), BF), ((T, D), F32), ((T, 1), F32),
-        ((T, D), BF), ((T, D), BF), ((T, D), F32),
+        ((HEADS, T, T), BF), ((T, D), F32), ((T, 1), F32), ((3, T, D), BF), ((T, D), F32),
     )
 
 
@@ -241,10 +240,10 @@
     U = {k: r for k, r in zip(UNIT, scr[:n])}
     (
         wa, wf, waT, wfT, lga, lba, lgf, lbf, molo, keyo, rinv, hm, mb, X, G, ex, ys, gx, fob, igb,
-        acca, accf, wga, wgf, rb, glp, glr, vec, gb, gctx, gctxT, gqT, gsT,
+        wta, wtf, mw, mr, rb, glp, glr, vec, gb, gctx, gctxT, gqT, gsT,
         wl_s, w_s, w_r, l_s, l_r, m_s, m_r, ex_s, ex_r, y_s, y_r, fo_s, fo_r, g_s, g_r, ig_s, ig_r,
-        p_s, p_r, gl_s, gl_r, fo, ig, o_s,
-    ) = scr[n:n + 57]
+        mw_s, mw_r, mr_s, mr_r, q_s, q_r, gl_s, gl_r, fo, ig, o_s,
+    ) = scr[n:n + 61]
     s = lax.axis_index("section")
     e = lax.rem(s, 2)
     L = s // 2
@@ -290,10 +289,14 @@
             w_rem(k, j).start()
         for j in range(3):
             w_local(k, j).start()
+
+    def send_thirds(k):
         for j in range(3):
             w_rem(k, j).start()
 
     per_core(send_weights)
+    when((L == 1) & (e == 0), lambda: send_thirds(0))
+    when(e == 1, lambda: send_thirds(1))
     mol_copy = remote(mol, molo, m_s.at[0], m_r.at[0], other)
     key_copy = remote(key, keyo, m_s.at[1], m_r.at[1], other)
     mol_copy.start()
@@ -360,22 +363,39 @@
 
     when(L == 1, ready1)
 
-    def grads(acc, wg, rhs, p, first):
+    def mw_copy(k, u):
+        return remote((wta, wtf)[k].at[u], mw.at[u], mw_s.at[u], mw_r.at[u], mate)
+
+    def mr_copy(k, u, c):
+        src = (U["an"].at[u], U["cfa"].at[u, c])[k]
+        return remote(src, mr.at[u, c], mr_s.at[u, c], mr_r.at[u, c], mate)
+
+    def mine(k, u, r, c):
+        left = jnp.concatenate([(wta, wtf)[k][u, r, :], mw[u, r, :]], axis=1)
+        right = jnp.concatenate([U["an"][u] if k == 0 else U["cfa"][u, c], mr[u, c]], axis=0)
+        return left, right
+
+    def pair_dot(k, p, r, c):
+        a, b = mine(k, 2 * p, r, c), mine(k, 2 * p + 1, r, c)
+        return dotf(jnp.concatenate([a[0], b[0]], axis=1), jnp.concatenate([a[1], b[1]], axis=0))
+
+    def wait_factors(k, us):
+        for u in us:
+            mw_copy(k, u).wait_recv()
+            for c in range(1 if k == 0 else 3):
+                if k == 0 and u == 0:
+                    when(L == 1, lambda: mr_copy(0, 0, 0).wait_recv())
+                else:
+                    mr_copy(1, u, c).wait_recv()
+
+    def first_pair(k):
+        wait_factors(k, (0, 1))
         for c in range(3):
-            rs = slice(c * D, c * D + D)
-            v = dotf(wg[p, rs, :], rhs[c][2 * p:2 * p + 2].reshape(2 * T, D))
-            if not first:
-                v = v + acc[rs, :].astype(F32)
-            acc[rs, :] = v.astype(BF)
-
-    def grads_f(p, first):
-        grads(accf, wgf, (U["ctx"], U["fn"], U["act"]), p, first)
-
-    def grads_a(p, first):
-        grads(acca, wga, (U["an"],) * 3, p, first)
+            r = slice(c * D, c * D + D)
+            rb[r, :] = pair_dot(k, 0, r, 0 if k == 0 else c).astype(BF)
 
     if fused:
-        yb, inb, raw, acc, gy, gz, gn, out_w, ry_s, ry_r, rz_s, rz_r, rw_s, rw_r, rg_s, rg_r = scr[n + 57:]
+        yb, inb, raw, acc, gy, gz, gn, out_w, ry_s, ry_r, rz_s, rz_r, rw_s, rw_r, rg_s, rg_r = scr[n + 61:]
         CH = 3 * D // (2 * NZ)
         SR = CH // SUB
         dest = [by_place([ORDER[k][i] for k in range(NZ)], z) for i in range(NZ)]
@@ -398,18 +418,18 @@
         def piece(i):
             return pl.ds(i * (3 * D // NZ), 3 * D // NZ)
 
-    def p_copy(i, src):
-        return remote(src.at[piece(i), :], rb.at[piece(i), :], p_s.at[i], p_r.at[i], mate)
-
-    def give(src):
+    def finish(k):
+        wait_factors(k, (2, 3))
+        n3 = 3 * D // NZ // 3
         for i in range(NZ):
-            p_copy(i, src).start()
-
-    def take(mine):
-        for i in range(NZ):
-            p_copy(i, mine).wait_recv()
-            r = piece(i)
-            rb[r, :] = (rb[r, :].astype(F32) + mine[r, :].astype(F32)).astype(BF)
+            if k == 0:
+                r = piece(i)
+                rb[r, :] = (pair_dot(0, 1, r, 0) + rb[r, :].astype(F32)).astype(BF)
+            else:
+                for h in range(3):
+                    blk = (dest[i] if fused else i) * 3 + h
+                    r = pl.ds(pl.multiple_of(blk * n3, 16), n3)
+                    rb[r, :] = (pair_dot(1, 1, r, blk * n3 // D) + rb[r, :].astype(F32)).astype(BF)
             if fused and i < NZ - 1:
                 def to_buddy():
                     for q in range(HALF):
@@ -424,20 +444,6 @@
                 for q in range(HALF, SUB):
                     y_copy(i, q).start()
 
-    def f_last():
-        grads_f(1, False)
-        when(e == 0, lambda: give(accf))
-
-    def f_take():
-        when(e == 1, lambda: take(accf))
-
-    def a_last():
-        rhs = U["an"][2:4].reshape(2 * T, D)
-        for i in range(NZ):
-            r = piece(i)
-            acca[r, :] = (dotf(wga[1, r, :], rhs) + acca[r, :].astype(F32)).astype(BF)
-            when(e == 1, lambda i=i: p_copy(i, acca).start())
-
     def y_copy_x(u):
         return remote(ys.at[u], X.at[u], y_s.at[u], y_r.at[u], other)
 
@@ -449,23 +455,44 @@
 
     def ig_copy(u):
         return remote(gx.at[u], igb.at[u - 2], ig_s.at[u - 2], ig_r.at[u - 2], other)
+
+    q_copy = remote(U["qkv"].at[3], U["qkv"].at[0], q_s, q_r, mate)
 
     def forward(u):
         S = {k: r.at[u] for k, r in U.items()}
         when(L == 1, lambda: y_copy_x(u).wait_recv())
         when((L == 0) & (u == 2), lambda: ex_copy(X.at[pl.ds(2, 2)]).wait_recv())
         opening = (L == 0) & (u == 0)
+        lent = opening & (e == 1)
+
+        def lend():
+            mr_copy(0, 0, 0).wait_recv()
+            U["qkv"][3] = dotf(mr[0, 0], wa[...]).astype(BF)
+            q_copy.start()
+            send_thirds(0)
         st = forward_stages(
             X.at[u], ys.at[u], wa, wf, (lga, lba), (lgf, lbf), mb.at[u], hm, S, gqT.at[pl.ds(0, D)], vec
         )
         for f in st:
             if f.__name__ == "project":
-                when(opening & (e == 1), lambda: wait_all(1))
+                when(e == 1, lambda: mr_copy(0, u, 0).start())
+                when(lent, q_copy.wait_recv)
+                when((L == 0) & (u == 1) & (e == 1), lambda: wait_all(1))
+                when(jnp.logical_not(lent), f)
+                when(opening & (e == 0), lend)
+                continue
             if f.__name__ in ("mixed", "act", "branch"):
                 c = ("mixed", "act", "branch").index(f.__name__)
                 when(opening & (e == 0), lambda c=c: wait_third(1, c))
             f()
         when(L == 0, lambda: y_copy_x(u).start())
+
+        def share():
+            for c in range(3):
+                mr_copy(1, u, c).start()
+
+        when(e == 0, share)
+        when((L == 0) & (u == 0) & (e == 0), q_copy.wait_send)
         when((L == 1) & (u < 2), lambda: fo_copy(u).start())
 
         def keep():
@@ -479,32 +506,26 @@
         when((L == 1) & (u == 0), lambda: ex_copy(G.at[pl.ds(0, 2)]).wait_recv())
         when(L == 0, lambda: g_copy(u).wait_recv())
         last = (L == 0) & (u == 3)
-        p = u // 2
-        lanes = at(u - 2 * p, T)
         st = backward_stages(
             G.at[u], gx.at[u], waT, wfT, (lga, lba), (lgf, lbf), hm, S,
-            {"a": wga.at[p, :, lanes], "f": wgf.at[p, :, lanes]},
+            {"a": wta.at[u], "f": wtf.at[u]},
             glp, gb, gctx, gctxT, gqT, gsT, vec,
         )
         for f in st:
             f()
             if f.__name__ == "g_context":
-                when(last, f_last)
+                when(e == 0, lambda: mw_copy(1, u).start())
             if f.__name__ == "g_merge":
-                when(last, a_last)
-                when(last, f_take)
+                when(e == 1, lambda: mw_copy(0, u).start())
+                when(last & (e == 1), lambda: finish(1))
         when(L == 1, lambda: g_copy(u).start())
         when((L == 0) & (u >= 2), lambda: ig_copy(u).start())
 
         def keep():
             igb[u] = gx[u]
 
-        def first_pair():
-            grads_f(0, True)
-            grads_a(0, True)
-
         when((L == 0) & (u < 2), keep)
-        when((L == 0) & (u == 1), first_pair)
+        when((L == 0) & (u == 2), lambda: per_core(first_pair))
 
     @pl.loop(0, 8)
     def _(i):
@@ -514,17 +535,11 @@
         when(is_f == 1, lambda: forward(u))
         when(is_f == 0, lambda: backward(u))
 
-    def finish1():
-        grads_f(0, True)
-        f_last()
-        grads_a(0, True)
-        a_last()
-        f_take()
-
-    when(L == 1, finish1)
+    when(L == 1, lambda: per_core(first_pair))
     gl_copy = remote(glp, glr, gl_s, gl_r, mate)
     gl_copy.start()
-    when(e == 0, lambda: take(acca))
+    when(e == 0, lambda: finish(0))
+    when((e == 1) & (L == 1), lambda: finish(1))
 
     def bring0():
         for u in range(2):
@@ -651,12 +666,19 @@
             w_rem(k, j).wait_send()
 
     per_core(close_weights)
-    def gave(src):
-        for i in range(NZ):
-            p_copy(i, src).wait_send()
-
-    when(e == 0, lambda: gave(accf))
-    when(e == 1, lambda: gave(acca))
+    def gave0():
+        for u in range(4):
+            mw_copy(1, u).wait_send()
+            for c in range(3):
+                mr_copy(1, u, c).wait_send()
+
+    def gave1():
+        for u in range(4):
+            mw_copy(0, u).wait_send()
+            mr_copy(0, u, 0).wait_send()
+
+    when(e == 0, gave0)
+    when(e == 1, gave1)
     ex_copy(X.at[pl.ds(2, 2)]).wait_send()
 
     def close0():
@@ -685,13 +707,13 @@
         vm((1, R), I32), vm((1, R), I32), vm((R, R), BF), vm((16, 256), BF), vm((4, T, T), F32),
         vm((4, T, D), BF), vm((4, T, D), BF), vm((2, T, D), BF), vm((4, T, D), BF), vm((4, T, D), BF),
         vm((2, T, D), BF), vm((2, T, D), BF),
-        vm((3 * D, D), BF), vm((3 * D, D), BF), vm((2, 3 * D, 2 * T), BF), vm((2, 3 * D, 2 * T), BF),
+        vm((4, 3 * D, T), BF), vm((4, 3 * D, T), BF), vm((4, 3 * D, T), BF), vm((4, 3, T, D), BF),
         vm((3 * D, D), BF), vm((8, D), F32), vm((8, D), F32),
         vm((T, D), F32), vm((T, D), BF), vm((T, D), BF), vm((D, T), BF),
         vm((3 * D, T), F32), vm((HEADS, T, T), BF),
         dma((3,)), dma((3,)), dma((3,)), dma((2,)), dma((2,)), dma((2,)), dma((2,)), dma, dma,
         dma((4,)), dma((4,)), dma((2,)), dma((2,)), dma((4,)), dma((4,)), dma((2,)), dma((2,)),
-        dma((NZ,)), dma((NZ,)), dma, dma, vm((R, D), BF), vm((R, D), F32), dma((3,)),
+        dma((4,)), dma((4,)), dma((4, 3)), dma((4, 3)), dma, dma, dma, dma, vm((R, D), BF), vm((R, D), F32), dma((3,)),
     ]
     if fused:
         CH = 3 * D // (2 * NZ)

time: 103 us -> 103 us (level)
  no operation moved by 1% of the time
where the time goes in v4:
time: 103 us; the launch traced here: 102 us
  Pallas kernels  102 us (99%)
    pallas_call x1, Pallas kernels, relay(): pl.pallas_call(lambda *refs: relay_kernel(fused, *refs), out_shape=[jax.S...  99 us
    pallas_call x1, Pallas kernels, emit(): pl.pallas_call(emit_kernel, out_shape=[jax.ShapeDtypeStruct(a.shape, a.dt...  2.53 us

profile of v4, /device:TPU:0, one launch (start us, length us, event | category | flops | bytes accessed | tf_op | source)
XLA Modules:
  0.0 102.3 jit_solution(14595463216409119241)
XLA Ops:
  0.6 99.0 %relay.1 = (bf16[256,768]{1,0:T(8,128)(2,1)}, f32[256,768]{1,0:T(8,128)}, f32[288,768]{1,0:T(8,128)}, f32[1,96]{1,0:T(1,128)}, f32[1,96]{1,0:T(1,128)}) custom-call(bf16[256,768]{1,0:T(8,128)(2,1)} %refs_0_.1, bf16[256,768]{1,0:T(8,128)(2,1)} %refs_1_.1, bf16[768,2304]{1,0:T(8,128)(2,1)} %bitcast.4, f32[1,768]{1,0:T(1,128)} %refs_3_.1, f32[1,768]{1,0:T(1,128)} %refs_4_.1, ...), custom_call_target="tpu_custom_call" | custom-call | tf_op jit(solution)/shard_map/relay/pallas_call | solution.py:731
  99.6 2.5 %emit.1 = (bf16[256,768]{1,0:T(8,128)(2,1)}, f32[256,768]{1,0:T(8,128)}, f32[288,768]{1,0:T(8,128)}, f32[1,96]{1,0:T(1,128)}, f32[1,96]{1,0:T(1,128)}) custom-call(bf16[256,768]{1,0:T(8,128)(2,1)} %get-tuple-element.15.refs_0_, f32[256,768]{1,0:T(8,128)} %get-tuple-element.16.refs_1_, f32[288,768]{1,0:T(8,128)} %get-tuple-element.17.refs_2_, ...), custom_call_target="tpu_custom_call" | custom-call | tf_op jit(solution)/shard_map/emit/pallas_call | solution.py:761

commit v5 on v4

--- a/solution.py
+++ b/solution.py
@@ -242,8 +242,8 @@
         wa, wf, waT, wfT, lga, lba, lgf, lbf, molo, keyo, rinv, hm, mb, X, G, ex, ys, gx, fob, igb,
         wta, wtf, mw, mr, rb, glp, glr, vec, gb, gctx, gctxT, gqT, gsT,
         wl_s, w_s, w_r, l_s, l_r, m_s, m_r, ex_s, ex_r, y_s, y_r, fo_s, fo_r, g_s, g_r, ig_s, ig_r,
-        mw_s, mw_r, mr_s, mr_r, q_s, q_r, gl_s, gl_r, fo, ig, o_s,
-    ) = scr[n:n + 61]
+        mw_s, mw_r, mr_s, mr_r, x_s, x_r, q_s, q_r, gl_s, gl_r, fo, ig, o_s,
+    ) = scr[n:n + 63]
     s = lax.axis_index("section")
     e = lax.rem(s, 2)
     L = s // 2
@@ -263,7 +263,12 @@
         peers += [across] + [on_line(lax.rem(z + t, NZ)) for t in range(1, NZ)]
     for p in peers:
         pl.semaphore_signal(bar, inc=1, device_id=p, device_id_type=MESH)
-    pl.semaphore_wait(bar, len(peers))
+
+    own = ((wa, lga, lba), (wf, lgf, lbf))
+
+    def per_core(fn):
+        when(e == 0, lambda: fn(0))
+        when(e == 1, lambda: fn(1))
 
     def third(c):
         return (slice(None), pl.ds(c * D, D))
@@ -278,48 +283,26 @@
         src = (gain, bias)[j - 3]
         return remote(src, own[k][j - 2], l_s.at[j - 3], l_r.at[j - 3], mate)
 
-    own = ((wa, lga, lba), (wf, lgf, lbf))
-
-    def per_core(fn):
-        when(e == 0, lambda: fn(0))
-        when(e == 1, lambda: fn(1))
-
-    def send_weights(k):
-        for j in (3, 4):
-            w_rem(k, j).start()
+    def start_local(k):
         for j in range(3):
             w_local(k, j).start()
 
-    def send_thirds(k):
+    def wait_local(k):
         for j in range(3):
-            w_rem(k, j).start()
-
-    per_core(send_weights)
-    when((L == 1) & (e == 0), lambda: send_thirds(0))
-    when(e == 1, lambda: send_thirds(1))
-    mol_copy = remote(mol, molo, m_s.at[0], m_r.at[0], other)
-    key_copy = remote(key, keyo, m_s.at[1], m_r.at[1], other)
-    mol_copy.start()
-    key_copy.start()
-
+            w_local(k, j).wait()
+
+    per_core(start_local)
     rot, inv = rotation(mol[...], R)
     rinv[...] = inv
-    xr = dotf(rot, tok[...]).astype(BF)
-    cr = dotf(rot, cot[...]).astype(BF)
-    xu = xr.reshape(2, T, D)
-    cu = cr.reshape(2, T, D)
-
-    def ex_copy(dst):
-        return remote(ex, dst, ex_s, ex_r, other)
+    xu = dotf(rot, tok[...]).astype(BF).reshape(2, T, D)
+    cu = dotf(rot, cot[...]).astype(BF).reshape(2, T, D)
 
     def stage0():
         ex[...] = cu
-        ex_copy(G.at[pl.ds(0, 2)]).start()
         X[0:2] = xu
 
     def stage1():
         ex[...] = xu
-        ex_copy(X.at[pl.ds(2, 2)]).start()
         G[2:4] = cu
 
     when(L == 0, stage0)
@@ -329,22 +312,67 @@
     lo = HS * i0 - jnp.where(i0 < 10, 0, 128)
     hm[...] = jnp.where((i1 >= lo) & (i1 < lo + HS), 1.0, 0.0).astype(BF)
     glp[...] = jnp.zeros_like(glp)
-    mol_copy.wait()
-    key_copy.wait()
     pair_bias(mol[...], key[...], rot, mb, 2 * L, R)
-    rot_o, _ = rotation(molo[...], R)
-    pair_bias(molo[...], keyo[...], rot_o, mb, 2 - 2 * L, R)
-
-    def wait_local(k):
+
+    def unit_forward(u):
+        S = {k: r.at[u] for k, r in U.items()}
+        return forward_stages(
+            X.at[u], ys.at[u], wa, wf, (lga, lba), (lgf, lbf), mb.at[u], hm, S, gqT.at[pl.ds(0, D)], vec
+        )
+
+    first = {f.__name__: f for f in unit_forward(0)}
+
+    def own_projection():
+        wait_local(0)
+        first["norm_a"]()
+        first["project"]()
+
+    when((L == 0) & (e == 0), own_projection)
+    pl.semaphore_wait(bar, len(peers))
+
+    x_copy = remote(X.at[0], U["an"].at[3], x_s, x_r, mate)
+    q_copy = remote(U["qkv"].at[3], U["qkv"].at[0], q_s, q_r, mate)
+    mol_copy = remote(mol, molo, m_s.at[0], m_r.at[0], other)
+    key_copy = remote(key, keyo, m_s.at[1], m_r.at[1], other)
+
+    def cot_copy(u):
+        return remote(ex.at[u], G.at[u], ex_s.at[u], ex_r.at[u], other)
+
+    def tok_copy(u):
+        return remote(ex.at[u - 2], X.at[u], ex_s.at[u - 2], ex_r.at[u - 2], other)
+
+    def send_rows(k):
+        for j in (3, 4):
+            w_rem(k, j).start()
+
+    def send_thirds(k):
         for j in range(3):
-            w_local(k, j).wait()
+            w_rem(k, j).start()
+
+    def wait_rows(k):
         for j in (3, 4):
             w_rem(1 - k, j).wait_recv()
 
-    per_core(wait_local)
-
     def wait_third(k, c):
         w_rem(k, c).wait_recv()
+
+    def wait_all(k):
+        for c in range(3):
+            wait_third(1 - k, c)
+
+    when((L == 0) & (e == 1), x_copy.start)
+    per_core(send_rows)
+    when((L == 1) & (e == 0), lambda: send_thirds(0))
+    when(e == 1, lambda: send_thirds(1))
+    mol_copy.start()
+    key_copy.start()
+
+    def toks():
+        tok_copy(2).start()
+        tok_copy(3).start()
+
+    when(L == 0, lambda: cot_copy(0).start())
+    when(L == 1, toks)
 
     def turn_weights():
         @pl.loop(0, 3)
@@ -353,11 +381,16 @@
             waT[cs, :] = wa[:, cs].T
             wfT[cs, :] = wf[:, cs].T
 
-    def wait_all(k):
-        for c in range(3):
-            wait_third(1 - k, c)
+    def other_bias():
+        mol_copy.wait()
+        key_copy.wait()
+        rot_o, _ = rotation(molo[...], R)
+        pair_bias(molo[...], keyo[...], rot_o, mb, 2 - 2 * L, R)
 
     def ready1():
+        other_bias()
+        per_core(wait_local)
+        per_core(wait_rows)
         per_core(wait_all)
         turn_weights()
 
@@ -395,7 +428,7 @@
             rb[r, :] = pair_dot(k, 0, r, 0 if k == 0 else c).astype(BF)
 
     if fused:
-        yb, inb, raw, acc, gy, gz, gn, out_w, ry_s, ry_r, rz_s, rz_r, rw_s, rw_r, rg_s, rg_r = scr[n + 61:]
+        yb, inb, raw, acc, gy, gz, gn, out_w, ry_s, ry_r, rz_s, rz_r, rw_s, rw_r, rg_s, rg_r = scr[n + 63:]
         CH = 3 * D // (2 * NZ)
         SR = CH // SUB
         dest = [by_place([ORDER[k][i] for k in range(NZ)], z) for i in range(NZ)]
@@ -418,31 +451,35 @@
         def piece(i):
             return pl.ds(i * (3 * D // NZ), 3 * D // NZ)
 
-    def finish(k):
-        wait_factors(k, (2, 3))
+    def finish(k, i):
         n3 = 3 * D // NZ // 3
-        for i in range(NZ):
-            if k == 0:
-                r = piece(i)
-                rb[r, :] = (pair_dot(0, 1, r, 0) + rb[r, :].astype(F32)).astype(BF)
-            else:
-                for h in range(3):
-                    blk = (dest[i] if fused else i) * 3 + h
-                    r = pl.ds(pl.multiple_of(blk * n3, 16), n3)
-                    rb[r, :] = (pair_dot(1, 1, r, blk * n3 // D) + rb[r, :].astype(F32)).astype(BF)
-            if fused and i < NZ - 1:
-                def to_buddy():
-                    for q in range(HALF):
-                        raw_copy(q).start()
-
-                def halves(i=i):
-                    for q in range(HALF):
-                        y_copy(i, q).start()
-
-                when(dest[i] == buddy, to_buddy)
-                when(dest[i] != buddy, halves)
-                for q in range(HALF, SUB):
+        if i == 0:
+            wait_factors(k, (2, 3))
+        if k == 0:
+            r = piece(i)
+            rb[r, :] = (pair_dot(0, 1, r, 0) + rb[r, :].astype(F32)).astype(BF)
+        else:
+            for h in range(3):
+                blk = (dest[i] if fused else i) * 3 + h
+                r = pl.ds(pl.multiple_of(blk * n3, 16), n3)
+                rb[r, :] = (pair_dot(1, 1, r, blk * n3 // D) + rb[r, :].astype(F32)).astype(BF)
+        if fused and i < NZ - 1:
+            def to_buddy():
+                for q in range(HALF):
+                    raw_copy(q).start()
+
+            def halves():
+                for q in range(HALF):
                     y_copy(i, q).start()
+
+            when(dest[i] == buddy, to_buddy)
+            when(dest[i] != buddy, halves)
+            for q in range(HALF, SUB):
+                y_copy(i, q).start()
+
+    def finish_rest(k):
+        for i in range(1, NZ):
+            finish(k, i)
 
     def y_copy_x(u):
         return remote(ys.at[u], X.at[u], y_s.at[u], y_r.at[u], other)
@@ -456,114 +493,143 @@
     def ig_copy(u):
         return remote(gx.at[u], igb.at[u - 2], ig_s.at[u - 2], ig_r.at[u - 2], other)
 
-    q_copy = remote(U["qkv"].at[3], U["qkv"].at[0], q_s, q_r, mate)
+    def share(u):
+        def factors0():
+            for c in range(3):
+                mr_copy(1, u, c).start()
+
+        when(e == 0, factors0)
+        when((e == 1) & ((L == 1) | (u > 0)), lambda: mr_copy(0, u, 0).start())
+
+    def lend():
+        x_copy.wait_recv()
+        mr[0, 0] = ln_rows(U["an"][3].astype(F32), lga[...], lba[...])[2]
+        U["qkv"][3] = dotf(mr[0, 0], wa[...]).astype(BF)
+        q_copy.start()
+        send_thirds(0)
+
+    def borrow():
+        wait_local(1)
+        first["norm_a"]()
+        q_copy.wait_recv()
+
+    def opening():
+        when(e == 0, lend)
+        per_core(wait_rows)
+        when(e == 1, borrow)
+        for name in ("flip", "scores", "mix_values"):
+            first[name]()
+        for c, name in enumerate(("mixed", "act", "branch")):
+            when(e == 0, lambda c=c: wait_third(1, c))
+            first[name]()
+            if name == "mixed":
+                first["norm_f"]()
+        y_copy_x(0).start()
+        share(0)
+        other_bias()
+        when(e == 0, q_copy.wait_send)
+        when(e == 1, x_copy.wait_send)
+        when(e == 1, lambda: wait_all(1))
 
     def forward(u):
-        S = {k: r.at[u] for k, r in U.items()}
         when(L == 1, lambda: y_copy_x(u).wait_recv())
-        when((L == 0) & (u == 2), lambda: ex_copy(X.at[pl.ds(2, 2)]).wait_recv())
-        opening = (L == 0) & (u == 0)
-        lent = opening & (e == 1)
-
-        def lend():
-            mr_copy(0, 0, 0).wait_recv()
-            U["qkv"][3] = dotf(mr[0, 0], wa[...]).astype(BF)
-            q_copy.start()
-            send_thirds(0)
-        st = forward_stages(
-            X.at[u], ys.at[u], wa, wf, (lga, lba), (lgf, lbf), mb.at[u], hm, S, gqT.at[pl.ds(0, D)], vec
-        )
-        for f in st:
-            if f.__name__ == "project":
-                when(e == 1, lambda: mr_copy(0, u, 0).start())
-                when(lent, q_copy.wait_recv)
-                when((L == 0) & (u == 1) & (e == 1), lambda: wait_all(1))
-                when(jnp.logical_not(lent), f)
-                when(opening & (e == 0), lend)
-                continue
-            if f.__name__ in ("mixed", "act", "branch"):
-                c = ("mixed", "act", "branch").index(f.__name__)
-                when(opening & (e == 0), lambda c=c: wait_third(1, c))
+        when((L == 0) & (u >= 2), lambda: tok_copy(u).wait_recv())
+        for f in unit_forward(u):
             f()
         when(L == 0, lambda: y_copy_x(u).start())
-
-        def share():
-            for c in range(3):
-                mr_copy(1, u, c).start()
-
-        when(e == 0, share)
-        when((L == 0) & (u == 0) & (e == 0), q_copy.wait_send)
-        when((L == 1) & (u < 2), lambda: fo_copy(u).start())
+        when((L == 0) & (u == 1), lambda: cot_copy(u).start())
+        share(u)
 
         def keep():
             fob[u - 2] = ys[u]
 
         when((L == 1) & (u >= 2), keep)
 
-    def backward(u):
+    def unit_backward(u):
         S = {k: r.at[u] for k, r in U.items()}
-        when((L == 0) & (u == 0), turn_weights)
-        when((L == 1) & (u == 0), lambda: ex_copy(G.at[pl.ds(0, 2)]).wait_recv())
-        when(L == 0, lambda: g_copy(u).wait_recv())
-        last = (L == 0) & (u == 3)
-        st = backward_stages(
+        return backward_stages(
             G.at[u], gx.at[u], waT, wfT, (lga, lba), (lgf, lbf), hm, S,
             {"a": wta.at[u], "f": wtf.at[u]},
             glp, gb, gctx, gctxT, gqT, gsT, vec,
         )
-        for f in st:
+
+    def backward(u):
+        when((L == 0) & (u == 0), turn_weights)
+        when((L == 1) & (u < 2), lambda: cot_copy(u).wait_recv())
+        when(L == 0, lambda: g_copy(u).wait_recv())
+        for f in unit_backward(u):
+            f()
+        when(L == 1, lambda: g_copy(u).start())
+        per_core(lambda k: mw_copy(1 - k, u).start())
+        when((L == 0) & (u == 2), lambda: ig_copy(u).start())
+
+        def keep():
+            igb[u] = gx[u]
+
+        when((L == 0) & (u < 2), keep)
+        when((L == 0) & (u == 2), lambda: per_core(first_pair))
+
+    gl_copy = remote(glp, glr, gl_s, gl_r, mate)
+
+    def closing():
+        g_copy(3).wait_recv()
+        for f in unit_backward(3):
             f()
             if f.__name__ == "g_context":
-                when(e == 0, lambda: mw_copy(1, u).start())
+                when(e == 0, lambda: mw_copy(1, 3).start())
             if f.__name__ == "g_merge":
-                when(e == 1, lambda: mw_copy(0, u).start())
-                when(last & (e == 1), lambda: finish(1))
-        when(L == 1, lambda: g_copy(u).start())
-        when((L == 0) & (u >= 2), lambda: ig_copy(u).start())
-
-        def keep():
-            igb[u] = gx[u]
-
-        when((L == 0) & (u < 2), keep)
-        when((L == 0) & (u == 2), lambda: per_core(first_pair))
+                when(e == 1, lambda: mw_copy(0, 3).start())
+                when(e == 1, lambda: finish(1, 0))
+        ig_copy(3).start()
+
+    when(L == 0, opening)
 
     @pl.loop(0, 8)
     def _(i):
         odd = lax.rem(i, 2)
-        is_f = jnp.where(L == 0, jnp.where(i < 4, 1, 0), 1 - odd)
+        is_f = jnp.where(L == 0, jnp.where((i >= 1) & (i <= 3), 1, 0), 1 - odd)
+        is_b = jnp.where(L == 0, jnp.where((i >= 4) & (i <= 6), 1, 0), odd)
         u = jnp.where(L == 0, lax.rem(i, 4), i // 2)
         when(is_f == 1, lambda: forward(u))
-        when(is_f == 0, lambda: backward(u))
-
+        when(is_b == 1, lambda: backward(u))
+
+    when(L == 0, closing)
+    gl_copy.start()
     when(L == 1, lambda: per_core(first_pair))
-    gl_copy = remote(glp, glr, gl_s, gl_r, mate)
-    gl_copy.start()
-    when(e == 0, lambda: finish(0))
-    when((e == 1) & (L == 1), lambda: finish(1))
-
-    def bring0():
-        for u in range(2):
-            fo_copy(u).wait_recv()
-
-    def bring1():
-        for u in (2, 3):
-            ig_copy(u).wait_recv()
-
-    when(L == 0, bring0)
-    when(L == 1, bring1)
-    fo[...] = dotf(rinv[...], fob[...].reshape(R, D)).astype(BF)
-    ig[...] = dotf(rinv[...], igb[...].reshape(R, D))
-    emits = [pltpu.make_async_copy(fo, fo_hbm, o_s.at[0]), pltpu.make_async_copy(ig, ig_hbm, o_s.at[1])]
-    for c in emits:
-        c.start()
+    when(e == 0, lambda: finish(0, 0))
+    when((e == 1) & (L == 1), lambda: finish(1, 0))
     gl_copy.wait()
-
+    glr[...] = glp[...] + glr[...]
     if fused:
-        gl1 = glp[...] + glr[...]
-        glr[...] = gl1
         gy_copy = remote(glr, gy, rg_s.at[0], rg_r.at[0], across)
         gy_copy.start()
-
+    per_core(finish_rest)
+
+    def send_fo():
+        for u in range(2):
+            fo_copy(u).start()
+
+    when(L == 1, send_fo)
+    emits = []
+
+    def bring():
+        def bring0():
+            for u in range(2):
+                fo_copy(u).wait_recv()
+
+        def bring1():
+            for u in (2, 3):
+                ig_copy(u).wait_recv()
+
+        when(L == 0, bring0)
+        when(L == 1, bring1)
+        fo[...] = dotf(rinv[...], fob[...].reshape(R, D)).astype(BF)
+        ig[...] = dotf(rinv[...], igb[...].reshape(R, D))
+        emits.extend([pltpu.make_async_copy(fo, fo_hbm, o_s.at[0]), pltpu.make_async_copy(ig, ig_hbm, o_s.at[1])])
+        for c in emits:
+            c.start()
+
+    if fused:
         def own_y():
             for q in range(SUB):
                 if q < HALF:
@@ -604,17 +670,19 @@
                     combine()
                 when(jnp.where(zz > z, z > 0, z < NZ - 1), add_in)
                 hop(i, q).start()
+            if i == 0:
+                gy_copy.wait()
+                gl2 = glr[...] + gy[...]
+                gn[...] = gl2
+                gz_copies = [
+                    remote(gn, gz.at[NZ - t - 1], rg_s.at[t], rg_r.at[NZ - t], on_line(lax.rem(z + t, NZ)))
+                    for t in range(1, NZ)
+                ]
+                for c in gz_copies:
+                    c.start()
             if i == NZ - 3:
                 own_y()
-        gy_copy.wait()
-        gl2 = glr[...] + gy[...]
-        gn[...] = gl2
-        gz_copies = [
-            remote(gn, gz.at[NZ - t - 1], rg_s.at[t], rg_r.at[NZ - t], on_line(lax.rem(z + t, NZ)))
-            for t in range(1, NZ)
-        ]
-        for c in gz_copies:
-            c.start()
+        bring()
         for q in range(SUB):
             acc[q] = rb[rows(z, y, q), :].astype(F32)
 
@@ -655,7 +723,8 @@
 
             when(d == k, own_part)
     else:
-        norms[0][...] = glp[...] + glr[...]
+        bring()
+        norms[0][...] = glr[...]
         w_copy = pltpu.make_async_copy(rb, w_hbm, o_s.at[2])
         w_copy.start()
     for c in emits + [w_copy]:
@@ -675,11 +744,15 @@
     def gave1():
         for u in range(4):
             mw_copy(0, u).wait_send()
-            mr_copy(0, u, 0).wait_send()
+            if u == 0:
+                when(L == 1, lambda: mr_copy(0, 0, 0).wait_send())
+            else:
+                mr_copy(0, u, 0).wait_send()
 
     when(e == 0, gave0)
     when(e == 1, gave1)
-    ex_copy(X.at[pl.ds(2, 2)]).wait_send()
+    for u in range(2):
+        cot_copy(u).wait_send()
 
     def close0():
         for u in range(4):
@@ -711,9 +784,9 @@
         vm((3 * D, D), BF), vm((8, D), F32), vm((8, D), F32),
         vm((T, D), F32), vm((T, D), BF), vm((T, D), BF), vm((D, T), BF),
         vm((3 * D, T), F32), vm((HEADS, T, T), BF),
-        dma((3,)), dma((3,)), dma((3,)), dma((2,)), dma((2,)), dma((2,)), dma((2,)), dma, dma,
+        dma((3,)), dma((3,)), dma((3,)), dma((2,)), dma((2,)), dma((2,)), dma((2,)), dma((2,)), dma((2,)),
         dma((4,)), dma((4,)), dma((2,)), dma((2,)), dma((4,)), dma((4,)), dma((2,)), dma((2,)),
-        dma((4,)), dma((4,)), dma((4, 3)), dma((4, 3)), dma, dma, dma, dma, vm((R, D), BF), vm((R, D), F32), dma((3,)),
+        dma((4,)), dma((4,)), dma((4, 3)), dma((4, 3)), dma, dma, dma, dma, dma, dma, vm((R, D), BF), vm((R, D), F32), dma((3,)),
     ]
     if fused:
         CH = 3 * D // (2 * NZ)

time: 103 us -> 99.4 us (0.965)
  Pallas kernels: 102 us -> 97.9 us
    pallas_call x1, Pallas kernels: 99 us -> 95.3 us  [relay(): pl.pallas_call(lambda *refs: relay_kernel(fused, *refs), out_shape=[jax.S...]
where the time goes in v5:
time: 99.4 us; the launch traced here: 98.7 us
  Pallas kernels  97.9 us (98%)
    pallas_call x1, Pallas kernels, relay(): pl.pallas_call(lambda *refs: relay_kernel(fused, *refs), out_shape=[jax.S...  95.3 us
    pallas_call x1, Pallas kernels, emit(): pl.pallas_call(emit_kernel, out_shape=[jax.ShapeDtypeStruct(a.shape, a.dt...  2.53 us

profile of v5, /device:TPU:0, one launch (start us, length us, event | category | flops | bytes accessed | tf_op | source)
XLA Modules:
  0.0 98.7 jit_solution(11097505834898517650)
XLA Ops:
  0.6 95.3 %relay.1 = (bf16[256,768]{1,0:T(8,128)(2,1)}, f32[256,768]{1,0:T(8,128)}, f32[288,768]{1,0:T(8,128)}, f32[1,96]{1,0:T(1,128)}, f32[1,96]{1,0:T(1,128)}) custom-call(bf16[256,768]{1,0:T(8,128)(2,1)} %refs_0_.1, bf16[256,768]{1,0:T(8,128)(2,1)} %refs_1_.1, bf16[768,2304]{1,0:T(8,128)(2,1)} %bitcast.4, f32[1,768]{1,0:T(1,128)} %refs_3_.1, f32[1,768]{1,0:T(1,128)} %refs_4_.1, ...), custom_call_target="tpu_custom_call" | custom-call | tf_op jit(solution)/shard_map/relay/pallas_call | solution.py:804
  96.0 2.5 %emit.1 = (bf16[256,768]{1,0:T(8,128)(2,1)}, f32[256,768]{1,0:T(8,128)}, f32[288,768]{1,0:T(8,128)}, f32[1,96]{1,0:T(1,128)}, f32[1,96]{1,0:T(1,128)}) custom-call(bf16[256,768]{1,0:T(8,128)(2,1)} %get-tuple-element.15.refs_0_, f32[256,768]{1,0:T(8,128)} %get-tuple-element.16.refs_1_, f32[288,768]{1,0:T(8,128)} %get-tuple-element.17.refs_2_, ...), custom_call_target="tpu_custom_call" | custom-call | tf_op jit(solution)/shard_map/emit/pallas_call | solution.py:834

commit v6 on v5

--- a/solution.py
+++ b/solution.py
@@ -184,7 +184,7 @@
 
 
 NZ = 4
-SUB = 2
+SUB = 3
 HALF = 1
 ORDER = ((3, 2, 1, 0), (3, 0, 2, 1), (0, 3, 1, 2), (0, 1, 2, 3))
 
@@ -211,7 +211,7 @@
     return onehot(i0, i1), onehot(i1, i0)
 
 
-def pair_bias(mol, key, rot, out, base, R):
+def pair_bias(mol, key, rot, out, mine, R):
     mk = jnp.concatenate([mol, key, jnp.zeros((6, R), I32)], axis=0).astype(F32).astype(BF)
     row = dot_t(mk, rot)
     col = dot_t(rot, mk)
@@ -220,7 +220,7 @@
     for b in range(R // T):
         rs = slice(b * T, b * T + T)
         ok = (col[rs, 0:1] == row[0:1, rs]) & ((col[rs, 1:2] > 0.5) | (k0 == q0))
-        out[base + b] = jnp.where(ok, 0.0, NEG)
+        out[jnp.where(mine == 0, 3 * b, 1 + b)] = jnp.where(ok, 0.0, NEG)
 
 
 UNIT = ("xha", "ra", "an", "qkv", "qkvT", "pT", "xhf", "rf", "cfa", "gp")
@@ -240,10 +240,10 @@
     U = {k: r for k, r in zip(UNIT, scr[:n])}
     (
         wa, wf, waT, wfT, lga, lba, lgf, lbf, molo, keyo, rinv, hm, mb, X, G, ex, ys, gx, fob, igb,
-        wta, wtf, mw, mr, rb, glp, glr, vec, gb, gctx, gctxT, gqT, gsT,
+        wta, wtf, mw, mr, rb, glp, glr, ctxT, vec, gb, gctx, gctxT, gqT, gsT,
         wl_s, w_s, w_r, l_s, l_r, m_s, m_r, ex_s, ex_r, y_s, y_r, fo_s, fo_r, g_s, g_r, ig_s, ig_r,
         mw_s, mw_r, mr_s, mr_r, x_s, x_r, q_s, q_r, gl_s, gl_r, fo, ig, o_s,
-    ) = scr[n:n + 63]
+    ) = scr[n:n + 64]
     s = lax.axis_index("section")
     e = lax.rem(s, 2)
     L = s // 2
@@ -295,39 +295,30 @@
     rot, inv = rotation(mol[...], R)
     rinv[...] = inv
     xu = dotf(rot, tok[...]).astype(BF).reshape(2, T, D)
-    cu = dotf(rot, cot[...]).astype(BF).reshape(2, T, D)
-
-    def stage0():
-        ex[...] = cu
-        X[0:2] = xu
-
-    def stage1():
+
+    def rows0():
+        X[0] = xu[0]
+        X[3] = xu[1]
+
+    def rows1():
         ex[...] = xu
-        G[2:4] = cu
-
-    when(L == 0, stage0)
-    when(L == 1, stage1)
-    i0 = lax.broadcasted_iota(I32, (16, 256), 0)
-    i1 = lax.broadcasted_iota(I32, (16, 256), 1)
-    lo = HS * i0 - jnp.where(i0 < 10, 0, 128)
-    hm[...] = jnp.where((i1 >= lo) & (i1 < lo + HS), 1.0, 0.0).astype(BF)
-    glp[...] = jnp.zeros_like(glp)
-    pair_bias(mol[...], key[...], rot, mb, 2 * L, R)
-
-    def unit_forward(u):
+
+    when(L == 0, rows0)
+    when(L == 1, rows1)
+
+    def unit_forward(u, heads=None, rows=None):
         S = {k: r.at[u] for k, r in U.items()}
         return forward_stages(
-            X.at[u], ys.at[u], wa, wf, (lga, lba), (lgf, lbf), mb.at[u], hm, S, gqT.at[pl.ds(0, D)], vec
+            X.at[u], ys.at[u], wa, wf, (lga, lba), (lgf, lbf), mb.at[u], hm, S,
+            gqT.at[pl.ds(0, D)] if heads is None else heads, vec if rows is None else rows,
         )
 
     first = {f.__name__: f for f in unit_forward(0)}
 
     def own_projection():
-        wait_local(0)
         first["norm_a"]()
         first["project"]()
 
-    when((L == 0) & (e == 0), own_projection)
     pl.semaphore_wait(bar, len(peers))
 
     x_copy = remote(X.at[0], U["an"].at[3], x_s, x_r, mate)
@@ -336,10 +327,10 @@
     key_copy = remote(key, keyo, m_s.at[1], m_r.at[1], other)
 
     def cot_copy(u):
-        return remote(ex.at[u], G.at[u], ex_s.at[u], ex_r.at[u], other)
+        return remote(ex.at[u // 3], G.at[u], ex_s.at[u // 3], ex_r.at[u // 3], other)
 
     def tok_copy(u):
-        return remote(ex.at[u - 2], X.at[u], ex_s.at[u - 2], ex_r.at[u - 2], other)
+        return remote(ex.at[u - 1], X.at[u], ex_s.at[u - 1], ex_r.at[u - 1], other)
 
     def send_rows(k):
         for j in (3, 4):
@@ -368,11 +359,27 @@
     key_copy.start()
 
     def toks():
+        tok_copy(1).start()
         tok_copy(2).start()
-        tok_copy(3).start()
-
-    when(L == 0, lambda: cot_copy(0).start())
+
     when(L == 1, toks)
+    cu = dotf(rot, cot[...]).astype(BF).reshape(2, T, D)
+
+    def cots0():
+        ex[...] = cu
+        cot_copy(0).start()
+
+    def cots1():
+        G[1:3] = cu
+
+    when(L == 0, cots0)
+    when(L == 1, cots1)
+    i0 = lax.broadcasted_iota(I32, (16, 256), 0)
+    i1 = lax.broadcasted_iota(I32, (16, 256), 1)
+    lo = HS * i0 - jnp.where(i0 < 10, 0, 128)
+    hm[...] = jnp.where((i1 >= lo) & (i1 < lo + HS), 1.0, 0.0).astype(BF)
+    glp[...] = jnp.zeros_like(glp)
+    pair_bias(mol[...], key[...], rot, mb, L, R)
 
     def turn_weights():
         @pl.loop(0, 3)
@@ -385,7 +392,7 @@
         mol_copy.wait()
         key_copy.wait()
         rot_o, _ = rotation(molo[...], R)
-        pair_bias(molo[...], keyo[...], rot_o, mb, 2 - 2 * L, R)
+        pair_bias(molo[...], keyo[...], rot_o, mb, 1 - L, R)
 
     def ready1():
         other_bias()
@@ -408,12 +415,14 @@
         right = jnp.concatenate([U["an"][u] if k == 0 else U["cfa"][u, c], mr[u, c]], axis=0)
         return left, right
 
-    def pair_dot(k, p, r, c):
-        a, b = mine(k, 2 * p, r, c), mine(k, 2 * p + 1, r, c)
-        return dotf(jnp.concatenate([a[0], b[0]], axis=1), jnp.concatenate([a[1], b[1]], axis=0))
-
-    def wait_factors(k, us):
-        for u in us:
+    def all_units(k, r, c):
+        parts = [mine(k, u, r, c) for u in range(4)]
+        return dotf(
+            jnp.concatenate([a for a, _ in parts], axis=1), jnp.concatenate([b for _, b in parts], axis=0)
+        )
+
+    def wait_factors(k):
+        for u in range(4):
             mw_copy(k, u).wait_recv()
             for c in range(1 if k == 0 else 3):
                 if k == 0 and u == 0:
@@ -421,14 +430,8 @@
                 else:
                     mr_copy(1, u, c).wait_recv()
 
-    def first_pair(k):
-        wait_factors(k, (0, 1))
-        for c in range(3):
-            r = slice(c * D, c * D + D)
-            rb[r, :] = pair_dot(k, 0, r, 0 if k == 0 else c).astype(BF)
-
     if fused:
-        yb, inb, raw, acc, gy, gz, gn, out_w, ry_s, ry_r, rz_s, rz_r, rw_s, rw_r, rg_s, rg_r = scr[n + 63:]
+        yb, inb, raw, acc, gy, gz, gn, ry_s, ry_r, rz_s, rz_r, rw_s, rw_r, rg_s, rg_r = scr[n + 64:]
         CH = 3 * D // (2 * NZ)
         SR = CH // SUB
         dest = [by_place([ORDER[k][i] for k in range(NZ)], z) for i in range(NZ)]
@@ -444,6 +447,12 @@
             return remote(
                 rb.at[rows(buddy, 1 - y, q), :], raw.at[q], rw_s.at[q], rw_r.at[q], on_line(buddy)
             )
+
+        def hop(i, q):
+            zz = dest[i]
+            nz = jnp.where(zz > z, z + 1, z - 1)
+            slot = jnp.where((nz == zz) & (z > zz), NZ, zz)
+            return remote(yb.at[i, q], inb.at[slot, q], rz_s.at[i, q], rz_r.at[slot, q], on_line(nz))
 
         def piece(i):
             return pl.ds(pl.multiple_of(dest[i] * (2 * CH), 16), 2 * CH)
@@ -454,15 +463,15 @@
     def finish(k, i):
         n3 = 3 * D // NZ // 3
         if i == 0:
-            wait_factors(k, (2, 3))
+            wait_factors(k)
         if k == 0:
             r = piece(i)
-            rb[r, :] = (pair_dot(0, 1, r, 0) + rb[r, :].astype(F32)).astype(BF)
+            rb[r, :] = all_units(0, r, 0).astype(BF)
         else:
             for h in range(3):
                 blk = (dest[i] if fused else i) * 3 + h
                 r = pl.ds(pl.multiple_of(blk * n3, 16), n3)
-                rb[r, :] = (pair_dot(1, 1, r, blk * n3 // D) + rb[r, :].astype(F32)).astype(BF)
+                rb[r, :] = all_units(1, r, blk * n3 // D).astype(BF)
         if fused and i < NZ - 1:
             def to_buddy():
                 for q in range(HALF):
@@ -485,13 +494,13 @@
         return remote(ys.at[u], X.at[u], y_s.at[u], y_r.at[u], other)
 
     def fo_copy(u):
-        return remote(ys.at[u], fob.at[u], fo_s.at[u], fo_r.at[u], other)
+        return remote(ys.at[u], fob.at[u // 3], fo_s.at[u // 3], fo_r.at[u // 3], other)
 
     def g_copy(u):
         return remote(gx.at[u], G.at[u], g_s.at[u], g_r.at[u], other)
 
     def ig_copy(u):
-        return remote(gx.at[u], igb.at[u - 2], ig_s.at[u - 2], ig_r.at[u - 2], other)
+        return remote(gx.at[u], igb.at[u - 1], ig_s.at[u - 1], ig_r.at[u - 1], other)
 
     def share(u):
         def factors0():
@@ -502,11 +511,13 @@
         when((e == 1) & ((L == 1) | (u > 0)), lambda: mr_copy(0, u, 0).start())
 
     def lend():
+        wait_local(0)
         x_copy.wait_recv()
         mr[0, 0] = ln_rows(U["an"][3].astype(F32), lga[...], lba[...])[2]
         U["qkv"][3] = dotf(mr[0, 0], wa[...]).astype(BF)
         q_copy.start()
         send_thirds(0)
+        own_projection()
 
     def borrow():
         wait_local(1)
@@ -531,19 +542,22 @@
         when(e == 1, x_copy.wait_send)
         when(e == 1, lambda: wait_all(1))
 
+    def after_forward(u):
+        share(u)
+
+        def keep():
+            fob[u - 1] = ys[u]
+
+        when((L == 1) & ((u == 1) | (u == 2)), keep)
+
     def forward(u):
         when(L == 1, lambda: y_copy_x(u).wait_recv())
-        when((L == 0) & (u >= 2), lambda: tok_copy(u).wait_recv())
+        when((L == 0) & (u < 3), lambda: tok_copy(u).wait_recv())
         for f in unit_forward(u):
             f()
         when(L == 0, lambda: y_copy_x(u).start())
-        when((L == 0) & (u == 1), lambda: cot_copy(u).start())
-        share(u)
-
-        def keep():
-            fob[u - 2] = ys[u]
-
-        when((L == 1) & (u >= 2), keep)
+        when((L == 0) & (u == 3), lambda: cot_copy(u).start())
+        after_forward(u)
 
     def unit_backward(u):
         S = {k: r.at[u] for k, r in U.items()}
@@ -553,21 +567,34 @@
             glp, gb, gctx, gctxT, gqT, gsT, vec,
         )
 
+    def after_backward(u):
+        when(L == 1, lambda: g_copy(u).start())
+        per_core(lambda k: mw_copy(1 - k, u).start())
+
     def backward(u):
         when((L == 0) & (u == 0), turn_weights)
-        when((L == 1) & (u < 2), lambda: cot_copy(u).wait_recv())
+        when(L == 1, lambda: cot_copy(u).wait_recv())
         when(L == 0, lambda: g_copy(u).wait_recv())
         for f in unit_backward(u):
             f()
-        when(L == 1, lambda: g_copy(u).start())
-        per_core(lambda k: mw_copy(1 - k, u).start())
-        when((L == 0) & (u == 2), lambda: ig_copy(u).start())
+        after_backward(u)
+        when((L == 0) & (u > 0), lambda: ig_copy(u).start())
 
         def keep():
-            igb[u] = gx[u]
-
-        when((L == 0) & (u < 2), keep)
-        when((L == 0) & (u == 2), lambda: per_core(first_pair))
+            igb[0] = gx[0]
+
+        when((L == 0) & (u == 0), keep)
+
+    def both_ways(u):
+        y_copy_x(u + 1).wait_recv()
+        when(u == 0, lambda: cot_copy(0).wait_recv())
+        fs, bs = unit_forward(u + 1, ctxT, ig.at[pl.ds(0, T)]), unit_backward(u)
+        for i in range(max(len(fs), len(bs))):
+            for st in (bs, fs):
+                if i < len(st):
+                    st[i]()
+        after_backward(u)
+        after_forward(u + 1)
 
     gl_copy = remote(glp, glr, gl_s, gl_r, mate)
 
@@ -580,22 +607,20 @@
             if f.__name__ == "g_merge":
                 when(e == 1, lambda: mw_copy(0, 3).start())
                 when(e == 1, lambda: finish(1, 0))
-        ig_copy(3).start()
+        igb[1] = gx[3]
 
     when(L == 0, opening)
 
-    @pl.loop(0, 8)
+    @pl.loop(0, 7)
     def _(i):
-        odd = lax.rem(i, 2)
-        is_f = jnp.where(L == 0, jnp.where((i >= 1) & (i <= 3), 1, 0), 1 - odd)
-        is_b = jnp.where(L == 0, jnp.where((i >= 4) & (i <= 6), 1, 0), odd)
-        u = jnp.where(L == 0, lax.rem(i, 4), i // 2)
-        when(is_f == 1, lambda: forward(u))
-        when(is_b == 1, lambda: backward(u))
+        is_f = jnp.where(L == 0, jnp.where((i >= 1) & (i <= 3), 1, 0), jnp.where(i == 0, 1, 0))
+        is_b = jnp.where(L == 0, jnp.where(i >= 4, 1, 0), jnp.where(i == 4, 1, 0))
+        when(is_f == 1, lambda: forward(i))
+        when((L == 1) & (i >= 1) & (i <= 3), lambda: both_ways(i - 1))
+        when(is_b == 1, lambda: backward(jnp.where(L == 0, i - 4, 3)))
 
     when(L == 0, closing)
     gl_copy.start()
-    when(L == 1, lambda: per_core(first_pair))
     when(e == 0, lambda: finish(0, 0))
     when((e == 1) & (L == 1), lambda: finish(1, 0))
     gl_copy.wait()
@@ -606,7 +631,7 @@
     per_core(finish_rest)
 
     def send_fo():
-        for u in range(2):
+        for u in (0, 3):
             fo_copy(u).start()
 
     when(L == 1, send_fo)
@@ -614,11 +639,11 @@
 
     def bring():
         def bring0():
-            for u in range(2):
+            for u in (0, 3):
                 fo_copy(u).wait_recv()
 
         def bring1():
-            for u in (2, 3):
+            for u in (1, 2):
                 ig_copy(u).wait_recv()
 
         when(L == 0, bring0)
@@ -637,12 +662,6 @@
                     r = rows(z, 1 - y, q)
                     rb[r, :] = (rb[r, :].astype(F32) + raw[q].astype(F32)).astype(BF)
                 y_copy(NZ - 1, q).start()
-
-        def hop(i, q):
-            zz = dest[i]
-            nz = jnp.where(zz > z, z + 1, z - 1)
-            slot = jnp.where((nz == zz) & (z > zz), NZ, zz)
-            return remote(yb.at[i, q], inb.at[slot, q], rz_s.at[i, q], rz_r.at[slot, q], on_line(nz))
 
         def arrived(slot, q):
             remote(yb.at[0, q], inb.at[slot, q], rz_s.at[0, q], rz_r.at[slot, q], across).wait_recv()
@@ -683,6 +702,7 @@
             if i == NZ - 3:
                 own_y()
         bring()
+        w_copies = []
         for q in range(SUB):
             acc[q] = rb[rows(z, y, q), :].astype(F32)
 
@@ -698,9 +718,8 @@
             when(z < NZ - 1, from_right)
             y_copy(NZ - 1, q).wait_recv()
             acc[q] += yb[NZ - 1, q].astype(F32)
-        out_w[...] = acc[...].reshape(CH, D)
-        w_copy = pltpu.make_async_copy(out_w, w_hbm, o_s.at[2])
-        w_copy.start()
+            w_copies.append(pltpu.make_async_copy(acc.at[q], w_hbm.at[pl.ds(q * SR, SR)], o_s.at[2 + q]))
+            w_copies[-1].start()
         for i in range(NZ):
             for q in range(SUB):
                 if q < HALF and i < NZ - 1:
@@ -725,9 +744,9 @@
     else:
         bring()
         norms[0][...] = glr[...]
-        w_copy = pltpu.make_async_copy(rb, w_hbm, o_s.at[2])
-        w_copy.start()
-    for c in emits + [w_copy]:
+        w_copies = [pltpu.make_async_copy(rb, w_hbm, o_s.at[2])]
+        w_copies[0].start()
+    for c in emits + w_copies:
         c.wait()
 
     def close_weights(k):
@@ -751,19 +770,19 @@
 
     when(e == 0, gave0)
     when(e == 1, gave1)
-    for u in range(2):
-        cot_copy(u).wait_send()
+    for u in (1, 2):
+        tok_copy(u).wait_send()
 
     def close0():
         for u in range(4):
             y_copy_x(u).wait_send()
-        for u in (2, 3):
+        for u in (1, 2):
             ig_copy(u).wait_send()
 
     def close1():
         for u in range(4):
             g_copy(u).wait_send()
-        for u in range(2):
+        for u in (0, 3):
             fo_copy(u).wait_send()
 
     when(L == 0, close0)
@@ -782,18 +801,18 @@
         vm((2, T, D), BF), vm((2, T, D), BF),
         vm((4, 3 * D, T), BF), vm((4, 3 * D, T), BF), vm((4, 3 * D, T), BF), vm((4, 3, T, D), BF),
         vm((3 * D, D), BF), vm((8, D), F32), vm((8, D), F32),
-        vm((T, D), F32), vm((T, D), BF), vm((T, D), BF), vm((D, T), BF),
+        vm((D, T), F32), vm((T, D), F32), vm((T, D), BF), vm((T, D), BF), vm((D, T), BF),
         vm((3 * D, T), F32), vm((HEADS, T, T), BF),
         dma((3,)), dma((3,)), dma((3,)), dma((2,)), dma((2,)), dma((2,)), dma((2,)), dma((2,)), dma((2,)),
         dma((4,)), dma((4,)), dma((2,)), dma((2,)), dma((4,)), dma((4,)), dma((2,)), dma((2,)),
-        dma((4,)), dma((4,)), dma((4, 3)), dma((4, 3)), dma, dma, dma, dma, dma, dma, vm((R, D), BF), vm((R, D), F32), dma((3,)),
+        dma((4,)), dma((4,)), dma((4, 3)), dma((4, 3)), dma, dma, dma, dma, dma, dma, vm((R, D), BF), vm((R, D), F32), dma((2 + SUB,)),
     ]
     if fused:
         CH = 3 * D // (2 * NZ)
         SR = CH // SUB
         scratch += [
             vm((NZ, SUB, SR, D), BF), vm((NZ + 1, SUB, SR, D), BF), vm((HALF, SR, D), BF),
-            vm((SUB, SR, D), F32), vm((8, D), F32), vm((NZ - 1, 8, D), F32), vm((8, D), F32), vm((CH, D), F32),
+            vm((SUB, SR, D), F32), vm((8, D), F32), vm((NZ - 1, 8, D), F32), vm((8, D), F32),
             dma((NZ, SUB)), dma((NZ, SUB)), dma((NZ - 1, SUB)), dma((NZ + 1, SUB)),
             dma((HALF,)), dma((HALF,)), dma((NZ,)), dma((NZ,)),
         ]

time: 99.4 us -> 96.4 us (0.970)
  Pallas kernels: 97.9 us -> 95.4 us
    pallas_call x1, Pallas kernels: 95.3 us -> 92.9 us  [relay(): pl.pallas_call(lambda *refs: relay_kernel(fused, *refs), out_shape=[jax.S...]
where the time goes in v6:
time: 96.4 us; the launch traced here: 96.2 us
  Pallas kernels  95.4 us (99%)
    pallas_call x1, Pallas kernels, relay(): pl.pallas_call(lambda *refs: relay_kernel(fused, *refs), out_shape=[jax.S...  92.9 us
    pallas_call x1, Pallas kernels, emit(): pl.pallas_call(emit_kernel, out_shape=[jax.ShapeDtypeStruct(a.shape, a.dt...  2.53 us

profile of v6, /device:TPU:0, one launch (start us, length us, event | category | flops | bytes accessed | tf_op | source)
XLA Modules:
  0.0 96.2 jit_solution(1221361583193819667)
XLA Ops:
  0.6 92.9 %relay.1 = (bf16[256,768]{1,0:T(8,128)(2,1)}, f32[256,768]{1,0:T(8,128)}, f32[288,768]{1,0:T(8,128)}, f32[1,96]{1,0:T(1,128)}, f32[1,96]{1,0:T(1,128)}) custom-call(bf16[256,768]{1,0:T(8,128)(2,1)} %refs_0_.1, bf16[256,768]{1,0:T(8,128)(2,1)} %refs_1_.1, bf16[768,2304]{1,0:T(8,128)(2,1)} %bitcast.4, f32[1,768]{1,0:T(1,128)} %refs_3_.1, f32[1,768]{1,0:T(1,128)} %refs_4_.1, ...), custom_call_target="tpu_custom_call" | custom-call | tf_op jit(solution)/shard_map/relay/pallas_call | solution.py:823
  93.5 2.5 %emit.1 = (bf16[256,768]{1,0:T(8,128)(2,1)}, f32[256,768]{1,0:T(8,128)}, f32[288,768]{1,0:T(8,128)}, f32[1,96]{1,0:T(1,128)}, f32[1,96]{1,0:T(1,128)}) custom-call(bf16[256,768]{1,0:T(8,128)(2,1)} %get-tuple-element.15.refs_0_, f32[256,768]{1,0:T(8,128)} %get-tuple-element.16.refs_1_, f32[288,768]{1,0:T(8,128)} %get-tuple-element.17.refs_2_, ...), custom_call_target="tpu_custom_call" | custom-call | tf_op jit(solution)/shard_map/emit/pallas_call | solution.py:853

commit v7 on v6

--- a/solution.py
+++ b/solution.py
@@ -233,9 +233,9 @@
     )
 
 
-def relay_kernel(fused, tok, cot, w, gain, bias, mol, key, fo_hbm, ig_hbm, w_hbm, *scr):
-    R, D = tok.shape
-    norms, scr = (scr[:2], scr[2:]) if fused else (scr[:1], scr[1:])
+def relay_kernel(fused, tok_hbm, cot_hbm, w, gain, bias, mol_hbm, key_hbm, fo_hbm, ig_hbm, w_hbm, *scr):
+    R, D = tok_hbm.shape
+    norms_hbm, scr = (scr[:2], scr[2:]) if fused else (scr[:1], scr[1:])
     n = len(UNIT)
     U = {k: r for k, r in zip(UNIT, scr[:n])}
     (
@@ -243,7 +243,8 @@
         wta, wtf, mw, mr, rb, glp, glr, ctxT, vec, gb, gctx, gctxT, gqT, gsT,
         wl_s, w_s, w_r, l_s, l_r, m_s, m_r, ex_s, ex_r, y_s, y_r, fo_s, fo_r, g_s, g_r, ig_s, ig_r,
         mw_s, mw_r, mr_s, mr_r, x_s, x_r, q_s, q_r, gl_s, gl_r, fo, ig, o_s,
-    ) = scr[n:n + 64]
+        tok, cot, mol, key, i_s, n_s,
+    ) = scr[n:n + 70]
     s = lax.axis_index("section")
     e = lax.rem(s, 2)
     L = s // 2
@@ -291,8 +292,17 @@
         for j in range(3):
             w_local(k, j).wait()
 
+    inputs = [
+        pltpu.make_async_copy(a, b, i_s.at[i])
+        for i, (a, b) in enumerate(((mol_hbm, mol), (key_hbm, key), (tok_hbm, tok), (cot_hbm, cot)))
+    ]
+    for c in inputs:
+        c.start()
     per_core(start_local)
+    inputs[0].wait()
+    inputs[1].wait()
     rot, inv = rotation(mol[...], R)
+    inputs[2].wait()
     rinv[...] = inv
     xu = dotf(rot, tok[...]).astype(BF).reshape(2, T, D)
 
@@ -340,6 +350,10 @@
         for j in range(3):
             w_rem(k, j).start()
 
+    def send_from(k, c):
+        for j in range(c, 3):
+            w_rem(k, j).start()
+
     def wait_rows(k):
         for j in (3, 4):
             w_rem(1 - k, j).wait_recv()
@@ -354,6 +368,7 @@
     when((L == 0) & (e == 1), x_copy.start)
     per_core(send_rows)
     when((L == 1) & (e == 0), lambda: send_thirds(0))
+    when((L == 0) & (e == 0), lambda: w_rem(0, 0).start())
     when(e == 1, lambda: send_thirds(1))
     mol_copy.start()
     key_copy.start()
@@ -363,6 +378,7 @@
         tok_copy(2).start()
 
     when(L == 1, toks)
+    inputs[3].wait()
     cu = dotf(rot, cot[...]).astype(BF).reshape(2, T, D)
 
     def cots0():
@@ -431,7 +447,8 @@
                     mr_copy(1, u, c).wait_recv()
 
     if fused:
-        yb, inb, raw, acc, gy, gz, gn, ry_s, ry_r, rz_s, rz_r, rw_s, rw_r, rg_s, rg_r = scr[n + 64:]
+        yb, inb, raw, acc, gy, gz, gn, norm_g, norm_b, ry_s, ry_r, rz_s, rz_r, rw_s, rw_r, rg_s, rg_r = scr[n + 70:]
+        norms = (norm_g, norm_b)
         CH = 3 * D // (2 * NZ)
         SR = CH // SUB
         dest = [by_place([ORDER[k][i] for k in range(NZ)], z) for i in range(NZ)]
@@ -516,7 +533,7 @@
         mr[0, 0] = ln_rows(U["an"][3].astype(F32), lga[...], lba[...])[2]
         U["qkv"][3] = dotf(mr[0, 0], wa[...]).astype(BF)
         q_copy.start()
-        send_thirds(0)
+        send_from(0, 1)
         own_projection()
 
     def borrow():
@@ -702,6 +719,22 @@
             if i == NZ - 3:
                 own_y()
         bring()
+        for c in gz_copies:
+            c.wait_send()
+        for k in range(NZ - 1):
+            remote(gn, gz.at[k], rg_s.at[0], rg_r.at[k + 1], across).wait_recv()
+        gl3 = gl2 + gz[0] + gz[1] + gz[2]
+        part = D // (2 * NZ)
+        for k in range(2 * NZ):
+            def own_part(k=k):
+                for j in range(2):
+                    v = gl3[:, k * part:(k + 1) * part]
+                    norms[j][...] = jnp.where(e == 0, v[j:j + 1, :], v[2 + j:3 + j, :])
+
+            when(d == k, own_part)
+        emits.extend(pltpu.make_async_copy(norms[j], norms_hbm[j], n_s.at[j]) for j in range(2))
+        for c in emits[-2:]:
+            c.start()
         w_copies = []
         for q in range(SUB):
             acc[q] = rb[rows(z, y, q), :].astype(F32)
@@ -728,22 +761,10 @@
                     y_copy(i, q).wait_send()
                 if i < NZ - 1:
                     hop(i, q).wait_send()
-        for t, c in zip(range(1, NZ), gz_copies):
-            c.wait_send()
-        for k in range(NZ - 1):
-            remote(gn, gz.at[k], rg_s.at[0], rg_r.at[k + 1], across).wait_recv()
-        gl3 = gl2 + gz[0] + gz[1] + gz[2]
-        part = D // (2 * NZ)
-        for k in range(2 * NZ):
-            def own_part(k=k):
-                for j in range(2):
-                    v = gl3[:, k * part:(k + 1) * part]
-                    norms[j][...] = jnp.where(e == 0, v[j:j + 1, :], v[2 + j:3 + j, :])
-
-            when(d == k, own_part)
     else:
         bring()
-        norms[0][...] = glr[...]
+        emits.append(pltpu.make_async_copy(glr, norms_hbm[0], n_s.at[0]))
+        emits[-1].start()
         w_copies = [pltpu.make_async_copy(rb, w_hbm, o_s.at[2])]
         w_copies[0].start()
     for c in emits + w_copies:
@@ -806,6 +827,7 @@
         dma((3,)), dma((3,)), dma((3,)), dma((2,)), dma((2,)), dma((2,)), dma((2,)), dma((2,)), dma((2,)),
         dma((4,)), dma((4,)), dma((2,)), dma((2,)), dma((4,)), dma((4,)), dma((2,)), dma((2,)),
         dma((4,)), dma((4,)), dma((4, 3)), dma((4, 3)), dma, dma, dma, dma, dma, dma, vm((R, D), BF), vm((R, D), F32), dma((2 + SUB,)),
+        vm((R, D), BF), vm((R, D), BF), vm((1, R), I32), vm((1, R), I32), dma((4,)), dma((2,)),
     ]
     if fused:
         CH = 3 * D // (2 * NZ)
@@ -813,6 +835,7 @@
         scratch += [
             vm((NZ, SUB, SR, D), BF), vm((NZ + 1, SUB, SR, D), BF), vm((HALF, SR, D), BF),
             vm((SUB, SR, D), F32), vm((8, D), F32), vm((NZ - 1, 8, D), F32), vm((8, D), F32),
+            vm((1, D // (2 * NZ)), F32), vm((1, D // (2 * NZ)), F32),
             dma((NZ, SUB)), dma((NZ, SUB)), dma((NZ - 1, SUB)), dma((NZ + 1, SUB)),
             dma((HALF,)), dma((HALF,)), dma((NZ,)), dma((NZ,)),
         ]
@@ -823,8 +846,8 @@
     return pl.pallas_call(
         lambda *refs: relay_kernel(fused, *refs),
         out_shape=[jax.ShapeDtypeStruct((R, D), BF), jax.ShapeDtypeStruct((R, D), F32)] + outs,
-        in_specs=[V, V, A, V, V, V, V],
-        out_specs=[A, A, A] + [V] * (len(outs) - 1),
+        in_specs=[A] * 7,
+        out_specs=[A] * (2 + len(outs)),
         scratch_shapes=scratch,
         compiler_params=pltpu.CompilerParams(
             collective_id=0, has_side_effects=True, vmem_limit_bytes=64 << 20

time: 96.4 us -> 95.5 us (level)
  Pallas kernels: 95.4 us -> 94.4 us
where the time goes in v7:
time: 95.5 us; the launch traced here: 95.3 us
  Pallas kernels  94.4 us (99%)
    pallas_call x1, Pallas kernels, relay(): pl.pallas_call(lambda *refs: relay_kernel(fused, *refs), out_shape=[jax.S...  91.9 us
    pallas_call x1, Pallas kernels, emit(): pl.pallas_call(emit_kernel, out_shape=[jax.ShapeDtypeStruct(a.shape, a.dt...  2.53 us

profile of v7, /device:TPU:0, one launch (start us, length us, event | category | flops | bytes accessed | tf_op | source)
XLA Modules:
  0.0 95.3 jit_solution(13765696740816125385)
XLA Ops:
  0.6 91.9 %relay.1 = (bf16[256,768]{1,0:T(8,128)(2,1)}, f32[256,768]{1,0:T(8,128)}, f32[288,768]{1,0:T(8,128)}, f32[1,96]{1,0:T(1,128)}, f32[1,96]{1,0:T(1,128)}) custom-call(bf16[256,768]{1,0:T(8,128)(2,1)} %refs_0_.1, bf16[256,768]{1,0:T(8,128)(2,1)} %refs_1_.1, bf16[768,2304]{1,0:T(8,128)(2,1)} %bitcast.4, f32[1,768]{1,0:T(1,128)} %refs_3_.1, f32[1,768]{1,0:T(1,128)} %refs_4_.1, ...), custom_call_target="tpu_custom_call" | custom-call | tf_op jit(solution)/shard_map/relay/pallas_call | solution.py:846
  92.5 2.5 %emit.1 = (bf16[256,768]{1,0:T(8,128)(2,1)}, f32[256,768]{1,0:T(8,128)}, f32[288,768]{1,0:T(8,128)}, f32[1,96]{1,0:T(1,128)}, f32[1,96]{1,0:T(1,128)}) custom-call(bf16[256,768]{1,0:T(8,128)(2,1)} %get-tuple-element.15.refs_0_, f32[256,768]{1,0:T(8,128)} %get-tuple-element.16.refs_1_, f32[288,768]{1,0:T(8,128)} %get-tuple-element.17.refs_2_, ...), custom_call_target="tpu_custom_call" | custom-call | tf_op jit(solution)/shard_map/emit/pallas_call | solution.py:876

commit v8 on v7

--- a/solution.py
+++ b/solution.py
@@ -95,9 +95,10 @@
     def act():
         u = dotf(S["cfa"][1], wf[:, D:2 * D])
         u2 = u * u
-        t = jnp.tanh(GELU_A * (u + GELU_B * u * u2))
-        S["cfa"][2] = (0.5 * u * (1.0 + t)).astype(BF)
-        S["gp"][...] = 0.5 * (1.0 + t) + 0.5 * u * (1.0 - t * t) * (GELU_A + 3 * GELU_A * GELU_B * u2)
+        h = 0.5 + 0.5 * jnp.tanh(GELU_A * u * (1.0 + GELU_B * u2))
+        a = u * h
+        S["cfa"][2] = a.astype(BF)
+        S["gp"][...] = h + a * (1.0 - h) * (2 * GELU_A + 6 * GELU_A * GELU_B * u2)
 
     def branch():
         br = dotf(S["cfa"][2], wf[:, 2 * D:3 * D]).astype(BF).astype(F32)
@@ -233,18 +234,17 @@
     )
 
 
-def relay_kernel(fused, tok_hbm, cot_hbm, w, gain, bias, mol_hbm, key_hbm, fo_hbm, ig_hbm, w_hbm, *scr):
+def relay_kernel(fused, tok_hbm, cot_hbm, w, gain, bias, mol_hbm, key_hbm, fo, ig, w_out, *scr):
     R, D = tok_hbm.shape
-    norms_hbm, scr = (scr[:2], scr[2:]) if fused else (scr[:1], scr[1:])
+    norms, scr = scr[:1], scr[1:]
     n = len(UNIT)
     U = {k: r for k, r in zip(UNIT, scr[:n])}
     (
         wa, wf, waT, wfT, lga, lba, lgf, lbf, molo, keyo, rinv, hm, mb, X, G, ex, ys, gx, fob, igb,
         wta, wtf, mw, mr, rb, glp, glr, ctxT, vec, gb, gctx, gctxT, gqT, gsT,
         wl_s, w_s, w_r, l_s, l_r, m_s, m_r, ex_s, ex_r, y_s, y_r, fo_s, fo_r, g_s, g_r, ig_s, ig_r,
-        mw_s, mw_r, mr_s, mr_r, x_s, x_r, q_s, q_r, gl_s, gl_r, fo, ig, o_s,
-        tok, cot, mol, key, i_s, n_s,
-    ) = scr[n:n + 70]
+        mw_s, mw_r, mr_s, mr_r, x_s, x_r, q_s, q_r, gl_s, gl_r, tok, cot, mol, key, i_s,
+    ) = scr[n:n + 66]
     s = lax.axis_index("section")
     e = lax.rem(s, 2)
     L = s // 2
@@ -303,7 +303,6 @@
     inputs[1].wait()
     rot, inv = rotation(mol[...], R)
     inputs[2].wait()
-    rinv[...] = inv
     xu = dotf(rot, tok[...]).astype(BF).reshape(2, T, D)
 
     def rows0():
@@ -378,6 +377,7 @@
         tok_copy(2).start()
 
     when(L == 1, toks)
+    rinv[...] = inv
     inputs[3].wait()
     cu = dotf(rot, cot[...]).astype(BF).reshape(2, T, D)
 
@@ -447,8 +447,8 @@
                     mr_copy(1, u, c).wait_recv()
 
     if fused:
-        yb, inb, raw, acc, gy, gz, gn, norm_g, norm_b, ry_s, ry_r, rz_s, rz_r, rw_s, rw_r, rg_s, rg_r = scr[n + 70:]
-        norms = (norm_g, norm_b)
+        yb, inb, raw, gy, gz, gn, ry_s, ry_r, rz_s, rz_r, rw_s, rw_r, rg_s, rg_r = scr[n + 66:]
+        acc = w_out
         CH = 3 * D // (2 * NZ)
         SR = CH // SUB
         dest = [by_place([ORDER[k][i] for k in range(NZ)], z) for i in range(NZ)]
@@ -652,7 +652,6 @@
             fo_copy(u).start()
 
     when(L == 1, send_fo)
-    emits = []
 
     def bring():
         def bring0():
@@ -667,9 +666,6 @@
         when(L == 1, bring1)
         fo[...] = dotf(rinv[...], fob[...].reshape(R, D)).astype(BF)
         ig[...] = dotf(rinv[...], igb[...].reshape(R, D))
-        emits.extend([pltpu.make_async_copy(fo, fo_hbm, o_s.at[0]), pltpu.make_async_copy(ig, ig_hbm, o_s.at[1])])
-        for c in emits:
-            c.start()
 
     if fused:
         def own_y():
@@ -729,13 +725,9 @@
             def own_part(k=k):
                 for j in range(2):
                     v = gl3[:, k * part:(k + 1) * part]
-                    norms[j][...] = jnp.where(e == 0, v[j:j + 1, :], v[2 + j:3 + j, :])
+                    norms[0][j:j + 1, :] = jnp.where(e == 0, v[j:j + 1, :], v[2 + j:3 + j, :])
 
             when(d == k, own_part)
-        emits.extend(pltpu.make_async_copy(norms[j], norms_hbm[j], n_s.at[j]) for j in range(2))
-        for c in emits[-2:]:
-            c.start()
-        w_copies = []
         for q in range(SUB):
             acc[q] = rb[rows(z, y, q), :].astype(F32)
 
@@ -751,8 +743,6 @@
             when(z < NZ - 1, from_right)
             y_copy(NZ - 1, q).wait_recv()
             acc[q] += yb[NZ - 1, q].astype(F32)
-            w_copies.append(pltpu.make_async_copy(acc.at[q], w_hbm.at[pl.ds(q * SR, SR)], o_s.at[2 + q]))
-            w_copies[-1].start()
         for i in range(NZ):
             for q in range(SUB):
                 if q < HALF and i < NZ - 1:
@@ -763,12 +753,8 @@
                     hop(i, q).wait_send()
     else:
         bring()
-        emits.append(pltpu.make_async_copy(glr, norms_hbm[0], n_s.at[0]))
-        emits[-1].start()
-        w_copies = [pltpu.make_async_copy(rb, w_hbm, o_s.at[2])]
-        w_copies[0].start()
-    for c in emits + w_copies:
-        c.wait()
+        norms[0][...] = glr[...]
+        w_out[...] = rb[...]
 
     def close_weights(k):
         for j in range(5):
@@ -826,69 +812,43 @@
         vm((3 * D, T), F32), vm((HEADS, T, T), BF),
         dma((3,)), dma((3,)), dma((3,)), dma((2,)), dma((2,)), dma((2,)), dma((2,)), dma((2,)), dma((2,)),
         dma((4,)), dma((4,)), dma((2,)), dma((2,)), dma((4,)), dma((4,)), dma((2,)), dma((2,)),
-        dma((4,)), dma((4,)), dma((4, 3)), dma((4, 3)), dma, dma, dma, dma, dma, dma, vm((R, D), BF), vm((R, D), F32), dma((2 + SUB,)),
-        vm((R, D), BF), vm((R, D), BF), vm((1, R), I32), vm((1, R), I32), dma((4,)), dma((2,)),
+        dma((4,)), dma((4,)), dma((4, 3)), dma((4, 3)), dma, dma, dma, dma, dma, dma,
+        vm((R, D), BF), vm((R, D), BF), vm((1, R), I32), vm((1, R), I32), dma((4,)),
     ]
     if fused:
         CH = 3 * D // (2 * NZ)
         SR = CH // SUB
         scratch += [
             vm((NZ, SUB, SR, D), BF), vm((NZ + 1, SUB, SR, D), BF), vm((HALF, SR, D), BF),
-            vm((SUB, SR, D), F32), vm((8, D), F32), vm((NZ - 1, 8, D), F32), vm((8, D), F32),
-            vm((1, D // (2 * NZ)), F32), vm((1, D // (2 * NZ)), F32),
+            vm((8, D), F32), vm((NZ - 1, 8, D), F32), vm((8, D), F32),
             dma((NZ, SUB)), dma((NZ, SUB)), dma((NZ - 1, SUB)), dma((NZ + 1, SUB)),
             dma((HALF,)), dma((HALF,)), dma((NZ,)), dma((NZ,)),
         ]
-        outs = [jax.ShapeDtypeStruct((CH, D), F32)] + [jax.ShapeDtypeStruct((1, D // (2 * NZ)), F32)] * 2
+        outs = [vm((R, D), BF), vm((R, D), F32), vm((SUB, SR, D), F32)] + [vm((2, D // (2 * NZ)), F32)]
     else:
-        outs = [jax.ShapeDtypeStruct((3 * D, D), BF), jax.ShapeDtypeStruct((8, D), F32)]
-    A = pl.BlockSpec(memory_space=pl.ANY)
+        outs = [
+            jax.ShapeDtypeStruct(sh, dt)
+            for sh, dt in (((R, D), BF), ((R, D), F32), ((3 * D, D), BF), ((8, D), F32))
+        ]
     return pl.pallas_call(
         lambda *refs: relay_kernel(fused, *refs),
-        out_shape=[jax.ShapeDtypeStruct((R, D), BF), jax.ShapeDtypeStruct((R, D), F32)] + outs,
-        in_specs=[A] * 7,
-        out_specs=[A] * (2 + len(outs)),
+        out_shape=outs,
+        in_specs=[pl.BlockSpec(memory_space=pl.ANY)] * 7,
+        out_specs=[V] * len(outs),
         scratch_shapes=scratch,
         compiler_params=pltpu.CompilerParams(
-            collective_id=0, has_side_effects=True, vmem_limit_bytes=64 << 20
+            collective_id=0, has_side_effects=True, vmem_limit_bytes=(61 if fused else 64) << 20
         ),
         name="relay",
     )(tok, cot, w, gain, bias, mol, key)
-
-
-def emit_kernel(*refs):
-    n = len(refs) // 3
-    sems = refs[-1]
-    ins = [pltpu.make_async_copy(refs[i], refs[2 * n + i], sems.at[0, i]) for i in range(n)]
-    outs = [pltpu.make_async_copy(refs[2 * n + i], refs[n + i], sems.at[1, i]) for i in range(n)]
-    for c in ins:
-        c.start()
-    for a, b in zip(ins, outs):
-        a.wait()
-        b.start()
-    for c in outs:
-        c.wait()
-
-
-def emit(arrays):
-    A = pl.BlockSpec(memory_space=pl.ANY)
-    n = len(arrays)
-    return pl.pallas_call(
-        emit_kernel,
-        out_shape=[jax.ShapeDtypeStruct(a.shape, a.dtype) for a in arrays],
-        in_specs=[A] * n,
-        out_specs=[A] * n,
-        scratch_shapes=[pltpu.VMEM(a.shape, a.dtype) for a in arrays] + [pltpu.SemaphoreType.DMA((2, n))],
-        name="emit",
-    )(*arrays)
 
 
 def shards(tokens, cotangent, section_weight, norm_gain, norm_bias, mol_ids, key_mask):
     fused = lax.axis_size("dp") == 2 * NZ
     got = relay(fused, tokens, cotangent, section_weight[0], norm_gain, norm_bias, mol_ids, key_mask)
     if fused:
-        fo, ig, gw, gg, gb = emit(got)
-        return fo, ig, gw.T[None], gg, gb
+        fo, ig, gw, gn = got
+        return fo, ig, gw.reshape(-1, gw.shape[-1]).T[None], gn[0:1], gn[1:2]
     fo, ig, gw, gn = got
     e = lax.rem(lax.axis_index("section"), 2)
     gn = lax.dynamic_slice_in_dim(gn, 2 * e, 2, 0)

time: 95.5 us -> 95.2 us (level)
  local copies, waits for them, and re-layouts: 0 us -> 3.06 us
  Pallas kernels: 94.4 us -> 91.4 us
    pallas_call x2 -> x1, Pallas kernels: 94.4 us -> 91.4 us  [relay(): pl.pallas_call(lambda *refs: relay_kernel(fused, *refs), out_shape=outs,...]
    unnamed x0 -> x3, local copies, waits for them, and re-layouts: none -> 2.54 us
where the time goes in v8:
time: 95.2 us; the launch traced here: 95.1 us
  Pallas kernels  91.4 us (96%)
  local copies, waits for them, and re-layouts  3.06 us (3%)
    pallas_call x1, Pallas kernels, relay(): pl.pallas_call(lambda *refs: relay_kernel(fused, *refs), out_shape=outs,...  91.4 us
    unnamed x3, local copies, waits for them, and re-layouts  2.54 us

profile of v8, /device:TPU:0, one launch (start us, length us, event | category | flops | bytes accessed | tf_op | source)
XLA Modules:
  0.0 95.1 jit_solution(6084814860702403252)
XLA Ops:
  0.6 91.4 %relay.1 = (bf16[256,768]{1,0:T(8,128)(2,1)S(1)}, f32[256,768]{1,0:T(8,128)S(1)}, f32[3,96,768]{2,1,0:T(8,128)S(1)}, f32[2,96]{1,0:T(2,128)S(1)}) custom-call(bf16[256,768]{1,0:T(8,128)(2,1)} %refs_0_.1, bf16[256,768]{1,0:T(8,128)(2,1)} %refs_1_.1, bf16[768,2304]{1,0:T(8,128)(2,1)} %bitcast.7, f32[1,768]{1,0:T(1,128)} %refs_3_.1, f32[1,768]{1,0:T(1,128)} %refs_4_.1, ...), custom_call_target="tpu_custom_call" | custom-call | tf_op jit(solution)/shard_map/relay/pallas_call | solution.py:833
  92.0 0.7 copy.15
  92.8 0.5 fusion
  93.3 0.9 copy.16
  94.2 0.9 copy.17
